TPU v7x, 32 devices: a whole 2x2x4 slice. The times are simulated.
32 devices in a mesh: groups: 2 (over x), ctx: 16 (over z, y, core).
Axes of the slice: x: 2, y: 2, z: 4, core: 2. Of those that a mesh axis runs over, the one named last changes fastest.
Arguments:
- queries: bfloat16 [8, 128, 576], P('groups', 'ctx'), parts along dimension 0, may hold values from -300 to 300
- cache: bfloat16 [16384, 576], P(('groups', 'ctx')), parts along dimension 0, may hold values from -5 to 5
- page_row: int32 [128], P(('groups', 'ctx')), parts along dimension 0, may hold values from 0 to 3, as said below
- page_index: int32 [128], P(('groups', 'ctx')), parts along dimension 0, may hold values from 0 to 31, as said below
- lengths: int32 [8], P('groups'), parts along dimension 0, may hold values from 2 to 4096, as said below
- hidden_in: bfloat16 [8, 7168], P('groups', 'ctx'), parts along dimension 0, may hold values from -4 to 4
- norm_gain: float32 [7168], replicated, may hold values from 0.1 to 1.9
- absorb_value: bfloat16 [128, 512, 128], P('ctx'), may hold values from -0.5 to 0.5
- out_proj: bfloat16 [16384, 7168], P('ctx'), may hold values from -0.09375 to 0.09375
- gate_proj: bfloat16 [7168, 9216], P(None, 'ctx'), may hold values from -0.0625 to 0.0625
- up_proj: bfloat16 [7168, 9216], P(None, 'ctx'), may hold values from -0.0625 to 0.0625
- down_proj: bfloat16 [9216, 7168], P('ctx'), may hold values from -0.125 to 0.125
Outputs:
- mixed: bfloat16 [8, 7168], P('groups', 'ctx'), parts along dimension 0
There are 2 independent parts, one for each index of `groups`. A program takes and returns all parts, laid end to end along the dimension named above; an argument that names none is the same for every part. Nothing has to cross between parts.
Inputs may be any that keep to these rules, and one draw needn't show every extreme that they name: `page_row`: every page belongs to a row; a row's pages are consecutive in page order and every row owns one or more. A row's pages have page_index 0, 1, 2 and so on in page order; slot j of a page holds the row's token page_index * 128 + j. `lengths`: every row's tokens fill its pages but for part of its last page, which holds two or more.
All inputs are finite; a program needn't handle non-finite values.
Results may differ from a plain program's by a relative error of at most 0.02.
Values may be sent and summed in bfloat16 or wider, within the bound.
No kernel may reach another device: no remote copies, remote signals or barrier semaphores. Data moves between devices by JAX's collectives and lax.ppermute only.
A program may use at most 128 MiB of HBM per device.

v0:
```python
import jax
import jax.numpy as jnp
from jax import lax
from jax.sharding import PartitionSpec as P

LAT = 512
ROPE = 64
VHEAD = 128
PAGE = 128


NEG_BIG = -1e30
EPS = 1e-06


def shard_partials(query_all, cache, page_row, page_index, lengths):
    slot_ids = jnp.arange(cache.shape[0], dtype=jnp.int32)
    row_of = jnp.repeat(page_row, PAGE)
    position = jnp.repeat(page_index, PAGE) * PAGE + slot_ids % PAGE
    row_ids = jnp.arange(lengths.shape[0], dtype=jnp.int32)
    visible = (row_of[None, :] == row_ids[:, None]) & (position[None, :] < lengths[:, None])
    softmax_scale = float(VHEAD + ROPE) ** (-0.5)
    scores = (
        jnp.einsum("bhe,te->bht", query_all, cache, preferred_element_type=jnp.float32)
        * softmax_scale
    )
    masked = jnp.where(visible[:, None, :], scores, NEG_BIG)
    shard_max = jnp.max(masked, axis=2)
    weights = jnp.where(visible[:, None, :], jnp.exp(scores - shard_max[..., None]), 0.0)
    shard_total = jnp.sum(weights, axis=2)
    shard_latent = jnp.einsum(
        "bht,tc->bhc",
        weights.astype(jnp.bfloat16),
        cache[:, :LAT],
        preferred_element_type=jnp.float32,
    )
    return (shard_max, shard_total, shard_latent)


def shards(
    queries,
    cache,
    page_row,
    page_index,
    lengths,
    hidden_in,
    norm_gain,
    absorb_value,
    out_proj,
    gate_proj,
    up_proj,
    down_proj,
):
    row_count = queries.shape[0]
    head_count = queries.shape[1]
    shard_index = lax.axis_index("ctx")
    query_all = lax.all_gather(queries, "ctx", axis=1, tiled=True)
    shard_max, shard_total, shard_latent = shard_partials(
        query_all, cache, page_row, page_index, lengths
    )
    pieces = (
        lax.all_to_all(
            shard_max[None].astype(jnp.bfloat16), "ctx", split_axis=2, concat_axis=0, tiled=True
        ).astype(jnp.float32),
        lax.all_to_all(
            shard_total[None].astype(jnp.bfloat16), "ctx", split_axis=2, concat_axis=0, tiled=True
        ).astype(jnp.float32),
        lax.all_to_all(
            shard_latent[None].astype(jnp.bfloat16), "ctx", split_axis=2, concat_axis=0, tiled=True
        ).astype(jnp.float32),
    )
    joint = jnp.max(pieces[0], axis=0)
    factor = jnp.exp(pieces[0] - joint[None])
    own_total = jnp.sum(pieces[1] * factor, axis=0)
    own_latent = jnp.sum(pieces[2] * factor[..., None], axis=0)
    latent_out = (own_latent / own_total[..., None]).astype(jnp.bfloat16)
    value_heads = jnp.einsum(
        "bhc,hcv->bhv", latent_out, absorb_value, preferred_element_type=jnp.float32
    ).astype(jnp.bfloat16)
    flat = value_heads.reshape(row_count, head_count * value_heads.shape[2])
    attn_terms = jnp.dot(flat, out_proj, preferred_element_type=jnp.float32)
    width_dev = hidden_in.shape[1]
    col_start = shard_index * width_dev
    residual_in = hidden_in.astype(jnp.float32)
    own_cols = lax.dynamic_slice_in_dim(attn_terms, col_start, width_dev, 1) + residual_in
    attn_terms = lax.dynamic_update_slice_in_dim(attn_terms, own_cols, col_start, 1)
    stream = lax.psum(attn_terms, "ctx")
    norm_scale = lax.rsqrt(jnp.mean(stream * stream, axis=1, keepdims=True) + EPS)
    normed = (stream * norm_scale * norm_gain).astype(jnp.bfloat16)
    stream_own = lax.dynamic_slice_in_dim(stream, col_start, width_dev, 1)
    gate_act = jnp.dot(normed, gate_proj, preferred_element_type=jnp.float32)
    up_act = jnp.dot(normed, up_proj, preferred_element_type=jnp.float32)
    activated = (jax.nn.silu(gate_act) * up_act).astype(jnp.bfloat16)
    down_terms = jnp.dot(activated, down_proj, preferred_element_type=jnp.float32)
    ffn_own = lax.psum_scatter(down_terms, "ctx", scatter_dimension=1, tiled=True)
    return (stream_own + ffn_own).astype(jnp.bfloat16)


def solution(mesh):
    in_specs = (
        P("groups", "ctx", None),
        P(("groups", "ctx"), None),
        P(("groups", "ctx")),
        P(("groups", "ctx")),
        P("groups"),
        P("groups", "ctx"),
        P(),
        P("ctx", None, None),
        P("ctx", None),
        P(None, "ctx"),
        P(None, "ctx"),
        P("ctx", None),
    )
    out_specs = P("groups", "ctx")
    return jax.shard_map(shards, mesh=mesh, in_specs=in_specs, out_specs=out_specs, check_vma=False)
```

profile of v0, /device:TPU:0, one launch (start us, length us, event | category | flops | bytes accessed | tf_op | source)
XLA Modules:
  0.0 268.7 jit_solution(9457608546645874062)
XLA Ops:
  6.5 0.0 copy-start
  6.5 0.7 broadcast_multiply_fusion
  7.3 0.1 fusion.23
  7.4 0.7 broadcast_bitcast_fusion
  8.1 25.3 %all_gather.3 = bf16[4,128,576]{2,1,0:T(8,128)(2,1)S(1)} all-gather(bf16[4,8,576]{2,1,0:T(8,128)(2,1)} %param.12), channel_id=1, replica_groups=mesh['groups'=2,'ctx'=16] {'ctx'}, dimensions={1}, use_global_device_ids=true | all-gather | bytes 626688 | tf_op jit(solution)/shard_map/all_gather | solution.py:57
  33.4 0.7 fusion.21
  34.1 1.7 select_reduce_fusion
  35.9 0.3 fusion.4
  36.2 0.8 copy.35
  37.0 3.5 %all-to-all-start.2 = ((bf16[1,4,128]{1,0,2:T(2,128)(2,1)}), bf16[1,4,128]{1,0,2:T(2,128)(2,1)S(1)}, u32[]{:S(2)}, u32[]{:S(2)}) async-start(bf16[1,4,128]{1,0,2:T(2,128)(2,1)} %copy.35), calls=%async_computation.2 | async-start | bytes 131072 | tf_op jit(solution)/shard_map/all_to_all | solution.py:65
  40.5 0.8 copy.33
  41.2 6.1 %all-to-all-done.2 = bf16[1,4,128]{1,0,2:T(2,128)(2,1)S(1)} async-done(((bf16[1,4,128]{1,0,2:T(2,128)(2,1)}), bf16[1,4,128]{1,0,2:T(2,128)(2,1)S(1)}, u32[]{:S(2)}, u32[]{:S(2)}) %all-to-all-start.2) | async-done | bytes 1056 | tf_op jit(solution)/shard_map/all_to_all | solution.py:65
  47.3 3.5 %all-to-all-start.1 = ((bf16[1,4,128]{1,0,2:T(2,128)(2,1)}), bf16[1,4,128]{1,0,2:T(2,128)(2,1)S(1)}, u32[]{:S(2)}, u32[]{:S(2)}) async-start(bf16[1,4,128]{1,0,2:T(2,128)(2,1)} %copy.33), calls=%async_computation.1 | async-start | bytes 131072 | tf_op jit(solution)/shard_map/all_to_all | solution.py:62
  50.8 1.5 fusion
  52.4 1.2 copy.31
  53.6 4.1 %all-to-all-done.1 = bf16[1,4,128]{1,0,2:T(2,128)(2,1)S(1)} async-done(((bf16[1,4,128]{1,0,2:T(2,128)(2,1)}), bf16[1,4,128]{1,0,2:T(2,128)(2,1)S(1)}, u32[]{:S(2)}, u32[]{:S(2)}) %all-to-all-start.1) | async-done | bytes 1056 | tf_op jit(solution)/shard_map/all_to_all | solution.py:62
  57.7 3.6 %all-to-all-start = ((bf16[1,4,128,512]{3,1,0,2:T(4,128)(2,1)}), bf16[1,4,128,512]{3,1,0,2:T(4,128)(2,1)S(1)}, u32[]{:S(2)}, u32[]{:S(2)}) async-start(bf16[1,4,128,512]{3,1,0,2:T(4,128)(2,1)} %copy.31), calls=%async_computation | async-start | bytes 1048576 | tf_op jit(solution)/shard_map/all_to_all | solution.py:68
  61.3 0.0 all-reduce.2.cloned.1.call-start
  61.3 0.1 copy.36
  61.4 0.1 reshape.120
  61.5 0.1 copy.34
  61.6 0.1 all_to_all.12
  61.8 13.7 %all-to-all-done = bf16[1,4,128,512]{3,1,0,2:T(4,128)(2,1)S(1)} async-done(((bf16[1,4,128,512]{3,1,0,2:T(4,128)(2,1)}), bf16[1,4,128,512]{3,1,0,2:T(4,128)(2,1)S(1)}, u32[]{:S(2)}, u32[]{:S(2)}) %all-to-all-start) | async-done | bytes 524320 | tf_op jit(solution)/shard_map/all_to_all | solution.py:68
  75.5 0.2 convert.13
  75.7 0.3 fusion.3
  76.0 0.0 copy-start.4
  76.0 0.0 copy-start.3
  76.0 0.1 divide_convert_fusion
  76.1 0.0 copy-done
  76.1 6.4 %fusion.7 = f32[4,7168]{1,0:T(4,128)S(1)} fusion(bf16[1024,7168]{1,0:T(8,128)(2,1)} %param.20, bf16[8,512,128]{2,1,0:T(8,128)(2,1)S(1)} %copy-done, bf16[4,8,512]{2,1,0:T(8,128)(2,1)S(1)} %divide_convert_fusion), kind=kOutput, calls=%fused_computation.15 | convolution fusion | flops 62918656 | bytes 15876096 | tf_op jit(solution)/shard_map/dot_general | solution.py:81
  82.5 0.0 copy-done.4
  82.5 0.1 convert_add_fusion
  82.6 0.2 dynamic_update_slice.3
  82.8 0.0 copy-start.2
  82.8 0.6 copy-done.2
  83.4 0.0 all-reduce.2.cloned.1.call-update
  83.4 0.0 reduce-scatter.4.cloned.1.call-start
  83.5 86.5 %all-reduce.2.cloned.1.call-done = f32[4,7168]{1,0:T(4,128)} async-done(((f32[4,7168]{1,0:T(4,128)}), f32[4,7168]{1,0:T(4,128)}) %all-reduce.2.cloned.1.call-update) | async-done | bytes 114704 | tf_op jit(solution)/shard_map/psum | solution.py:87
  170.0 0.0 copy-start.1
  170.0 1.1 multiply_reduce_fusion
  171.2 0.0 copy-done.3
  171.2 5.6 %fusion.29 = f32[4,576]{1,0:T(4,128)S(1)} fusion(bf16[7168,576]{0,1:T(8,128)(2,1)} %param.21, f32[4,7168]{1,0:T(4,128)} %all-reduce.2.cloned.1.call-done, f32[7168]{0:T(1024)S(1)} %copy-done.3, f32[4]{0:T(128)S(1)} %add_rsqrt_fusion), kind=kOutput, calls=%fused_computation.52 | convolution fusion | flops 33116160 | bytes 8410128 | tf_op jit(solution)/shard_map/dot_general | solution.py:91
  176.8 0.0 copy-done.1
  176.8 12.2 %convolution_bitcast_fusion = f32[7168,4]{1,0:T(8,128)} fusion(bf16[576,7168]{1,0:T(8,128)(2,1)} %param.23, bf16[7168,576]{0,1:T(8,128)(2,1)} %param.22, f32[4,576]{1,0:T(4,128)S(1)} %fusion.29, f32[4,7168]{1,0:T(4,128)S(1)} %copy-done.1, f32[7168]{0:T(1024)S(1)} %copy-done.3, f32[4]{0:T(128)S(1)} %add_rsqrt_fusion), kind=kOutput, calls=%fused_computation | convolution fusion | flops 66160128 | bytes 16782352
  189.1 0.0 reduce-scatter.4.cloned.1.call-update
  189.1 71.0 %reduce-scatter.4.cloned.1.call-done = f32[448,4]{1,0:T(8,128)} async-done(((f32[7168,4]{1,0:T(8,128)}), f32[448,4]{1,0:T(8,128)}) %reduce-scatter.4.cloned.1.call-update) | async-done | bytes 7184
  260.1 1.0 copy.39
  261.2 0.7 add_convert_fusion
  (5 shorter events, 0.1 us)
Async XLA Ops:
  6.5 69.6 %copy-start = (bf16[8,512,128]{2,1,0:T(8,128)(2,1)S(1)}, bf16[8,512,128]{2,1,0:T(8,128)(2,1)}, u32[]{:S(2)}) copy-start(bf16[8,512,128]{2,1,0:T(8,128)(2,1)} %param.19) | copy-start | bytes 3145732
  37.0 10.4 %all-to-all-start.2 = ((bf16[1,4,128]{1,0,2:T(2,128)(2,1)}), bf16[1,4,128]{1,0,2:T(2,128)(2,1)S(1)}, u32[]{:S(2)}, u32[]{:S(2)}) async-start(bf16[1,4,128]{1,0,2:T(2,128)(2,1)} %copy.35), calls=%async_computation.2 | async-start | bytes 131072 | tf_op jit(solution)/shard_map/all_to_all | solution.py:65
  47.3 10.4 %all-to-all-start.1 = ((bf16[1,4,128]{1,0,2:T(2,128)(2,1)}), bf16[1,4,128]{1,0,2:T(2,128)(2,1)S(1)}, u32[]{:S(2)}, u32[]{:S(2)}) async-start(bf16[1,4,128]{1,0,2:T(2,128)(2,1)} %copy.33), calls=%async_computation.1 | async-start | bytes 131072 | tf_op jit(solution)/shard_map/all_to_all | solution.py:62
  57.7 17.8 %all-to-all-start = ((bf16[1,4,128,512]{3,1,0,2:T(4,128)(2,1)}), bf16[1,4,128,512]{3,1,0,2:T(4,128)(2,1)S(1)}, u32[]{:S(2)}, u32[]{:S(2)}) async-start(bf16[1,4,128,512]{3,1,0,2:T(4,128)(2,1)} %copy.31), calls=%async_computation | async-start | bytes 1048576 | tf_op jit(solution)/shard_map/all_to_all | solution.py:68
  61.3 108.8 %all-reduce.2.cloned.1.call-start = ((), (), s32[]{:S(2)}) async-start(), calls=%async_computation.4 | async-start | bytes 229376 | tf_op jit(solution)/shard_map/psum | solution.py:87
  76.0 6.5 %copy-start.4 = (bf16[4,448]{1,0:T(4,128)(2,1)S(1)}, bf16[4,448]{1,0:T(4,128)(2,1)}, u32[]{:S(2)}) copy-start(bf16[4,448]{1,0:T(4,128)(2,1)} %param.17) | copy-start | bytes 10756
  76.0 95.2 %copy-start.3 = (f32[7168]{0:T(1024)S(1)}, f32[7168]{0:T(1024)}, u32[]{:S(2)}) copy-start(f32[7168]{0:T(1024)} %param.18) | copy-start | bytes 86020
  82.8 0.6 copy-start.2
  83.4 176.7 %reduce-scatter.4.cloned.1.call-start = ((), (), s32[]{:S(2)}) async-start(), calls=%async_computation.5 | async-start | bytes 3899392
  170.0 6.8 %copy-start.1 = (f32[4,7168]{1,0:T(4,128)S(1)}, f32[4,7168]{1,0:T(4,128)}, u32[]{:S(2)}) copy-start(f32[4,7168]{1,0:T(4,128)} %all-reduce.2.cloned.1.call-done) | copy-start | bytes 344068
Sparse Core Ops, SparseCore 0:
  83.6 86.4 all-reduce.1
  189.2 70.8 reduce-scatter.3
where the time goes:
time: 269 us
  waiting for transfers between devices  182 us (68%)
  matrix products  27.5 us (10%)
  blocking collectives  25.3 us (9%)
  between operations  13.5 us (5%)
  starting transfers between devices  10.6 us (4%)
  local copies, waits for them, and re-layouts  5.74 us (2%)
  other arithmetic  4.41 us (2%)
    psum x1, waiting for transfers between devices, shards(): stream = lax.psum(attn_terms, 'ctx')  86.5 us
    unnamed x3, waiting for transfers between devices  71.1 us
    all_gather x1, blocking collectives, shards(): query_all = lax.all_gather(queries, 'ctx', axis=1, tiled=True)  25.3 us
    all_to_all x1, waiting for transfers between devices, shards(): lax.all_to_all(shard_latent[None].astype(jnp.bfloat16), 'ctx', split_axis...  13.7 us
    unnamed x1, matrix products  12.2 us
    dot_general x1, matrix products, shards(): attn_terms = jnp.dot(flat, out_proj, preferred_element_type=jnp.float32)  6.36 us
    all_to_all x1, waiting for transfers between devices, shards(): lax.all_to_all(shard_total[None].astype(jnp.bfloat16), 'ctx', split_axis=...  6.09 us
    dot_general x1, matrix products, shards(): gate_act = jnp.dot(normed, gate_proj, preferred_element_type=jnp.float32)  5.64 us
  transfers between devices with their start and end apart: 5, of which 5 were waited for; matrix products, arithmetic and copies ran while one was open for 1% of the time, Pallas kernels for 0%

commit v1 on v0

v1 whole, which is shorter than its diff:
```python
import jax
import jax.numpy as jnp
from jax import lax
from jax.sharding import PartitionSpec as P

LAT = 512
ROPE = 64
VHEAD = 128
PAGE = 128
LANES = 128


NEG_BIG = -1e30
EPS = 1e-06


def swap(value):
    count = lax.axis_size("ctx")
    return lax.ppermute(value, "ctx", [(i, i ^ 1) for i in range(count)])


def core_groups():
    count = lax.axis_size("ctx")
    return [list(range(core, count, 2)) for core in range(2)]


def exchange(value):
    return lax.all_to_all(value, "ctx", 0, 0, tiled=True, axis_index_groups=core_groups())


def spread(value):
    chips = lax.axis_size("ctx") // 2
    return exchange(jnp.broadcast_to(value[None], (chips,) + value.shape))


def shard_partials(query_rows, cache, visible):
    softmax_scale = float(VHEAD + ROPE) ** (-0.5)
    scores = (
        jnp.einsum("pbhe,te->pbht", query_rows, cache, preferred_element_type=jnp.float32)
        * softmax_scale
    )
    mask = visible[None, :, None, :]
    shard_max = jnp.max(jnp.where(mask, scores, NEG_BIG), axis=3)
    weights = jnp.where(mask, jnp.exp(scores - shard_max[..., None]), 0.0)
    shard_total = jnp.sum(weights, axis=3)
    shard_latent = jnp.einsum(
        "pbht,tc->pbhc",
        weights.astype(jnp.bfloat16),
        cache[:, :LAT],
        preferred_element_type=jnp.float32,
    )
    return (shard_max, shard_total, shard_latent)


def pieces_of(value):
    high = lax.reduce_precision(value, 8, 7)
    middle = lax.reduce_precision(value - high, 8, 7)
    return (high, middle, value - high - middle)


def shards(
    queries,
    cache,
    page_row,
    page_index,
    lengths,
    hidden_in,
    norm_gain,
    absorb_value,
    out_proj,
    gate_proj,
    up_proj,
    down_proj,
):
    row_count, head_count, entry = queries.shape
    count = lax.axis_size("ctx")
    chips = count // 2
    shard_index = lax.axis_index("ctx")
    core = shard_index % 2
    slot_ids = jnp.arange(cache.shape[0], dtype=jnp.int32)
    row_of = jnp.repeat(page_row, PAGE)
    position = jnp.repeat(page_index, PAGE) * PAGE + slot_ids % PAGE
    row_ids = jnp.arange(row_count, dtype=jnp.int32)
    visible = (row_of[None, :] == row_ids[:, None]) & (position[None, :] < lengths[:, None])

    query_own = spread(queries.reshape(row_count * head_count, entry))
    query_other = swap(query_own)
    shape = (chips, row_count, head_count, entry)
    max_other, total_other, latent_other = shard_partials(query_other.reshape(shape), cache, visible)
    max_own, total_own, latent_own = shard_partials(query_own.reshape(shape), cache, visible)
    max_in, total_in = swap(jnp.stack([max_other, total_other]))
    latent_in = swap(latent_other.astype(jnp.bfloat16))
    chip_max = jnp.maximum(max_own, max_in)
    factor_own = jnp.exp(max_own - chip_max)
    factor_in = jnp.exp(max_in - chip_max)
    chip_total = total_own * factor_own + total_in * factor_in
    chip_latent = latent_own * factor_own[..., None] + latent_in * factor_in[..., None]
    stats = jnp.stack(pieces_of(chip_max) + pieces_of(chip_total), axis=-1)
    stats = jnp.pad(stats, ((0, 0), (0, 0), (0, 0), (0, LANES - stats.shape[-1])))
    message = jnp.concatenate([chip_latent, stats], axis=-1).astype(jnp.bfloat16)
    message = message.reshape(chips, row_count * head_count, LAT + LANES)
    pieces = exchange(message).astype(jnp.float32)
    part_max = pieces[..., LAT] + pieces[..., LAT + 1] + pieces[..., LAT + 2]
    part_total = pieces[..., LAT + 3] + pieces[..., LAT + 4] + pieces[..., LAT + 5]
    joint = jnp.max(part_max, axis=0)
    factor = jnp.exp(part_max - joint[None])
    total = jnp.sum(part_total * factor, axis=0)
    latent = jnp.sum(pieces[..., :LAT] * factor[..., None], axis=0)
    latent_out = (latent / total[..., None]).astype(jnp.bfloat16)
    latent_out = latent_out.reshape(row_count, head_count, LAT)
    value_heads = jnp.einsum(
        "bhc,hcv->bhv", latent_out, absorb_value, preferred_element_type=jnp.float32
    ).astype(jnp.bfloat16)
    flat = value_heads.reshape(row_count, head_count * value_heads.shape[2])
    attn_terms = jnp.dot(flat, out_proj, preferred_element_type=jnp.float32)

    width_dev = hidden_in.shape[1]
    width = attn_terms.shape[1]
    col_start = shard_index * width_dev
    own_cols = lax.dynamic_slice_in_dim(attn_terms, col_start, width_dev, 1)
    own_cols = own_cols + hidden_in.astype(jnp.float32)
    attn_terms = lax.dynamic_update_slice_in_dim(attn_terms, own_cols, col_start, 1)
    halves = attn_terms.reshape(row_count, 2, width // 2)
    keep = lax.dynamic_index_in_dim(halves, core, 1, keepdims=False)
    send = lax.dynamic_index_in_dim(halves, 1 - core, 1, keepdims=False)
    chip_terms = (keep + swap(send)).astype(jnp.bfloat16)
    mine = jnp.sum(spread(chip_terms).astype(jnp.float32), axis=0)
    other = swap(mine)
    first = jnp.where(core == 0, mine, other)
    second = jnp.where(core == 0, other, mine)
    stream = jnp.concatenate([first, second], axis=1)

    norm_scale = lax.rsqrt(jnp.mean(stream * stream, axis=1, keepdims=True) + EPS)
    normed = (stream * norm_scale * norm_gain).astype(jnp.bfloat16)
    stream_own = lax.dynamic_slice_in_dim(stream, col_start, width_dev, 1)
    gate_act = jnp.dot(normed, gate_proj, preferred_element_type=jnp.float32)
    up_act = jnp.dot(normed, up_proj, preferred_element_type=jnp.float32)
    activated = (jax.nn.silu(gate_act) * up_act).astype(jnp.bfloat16)
    down_terms = jnp.dot(activated, down_proj, preferred_element_type=jnp.float32)
    blocks = down_terms.reshape(row_count, count, width_dev).swapaxes(0, 1)
    parts = lax.all_to_all(blocks.astype(jnp.bfloat16), "ctx", 0, 0, tiled=True)
    ffn_own = jnp.sum(parts.astype(jnp.float32), axis=0)
    return (stream_own + ffn_own).astype(jnp.bfloat16)


def solution(mesh):
    in_specs = (
        P("groups", "ctx", None),
        P(("groups", "ctx"), None),
        P(("groups", "ctx")),
        P(("groups", "ctx")),
        P("groups"),
        P("groups", "ctx"),
        P(),
        P("ctx", None, None),
        P("ctx", None),
        P(None, "ctx"),
        P(None, "ctx"),
        P("ctx", None),
    )
    out_specs = P("groups", "ctx")
    return jax.shard_map(shards, mesh=mesh, in_specs=in_specs, out_specs=out_specs, check_vma=False)
```

time: 269 us -> 97.9 us (0.36)
  waiting for transfers between devices: 182 us -> 22.9 us
  between operations: 13.5 us -> 0.26 us
  blocking collectives: 25.3 us -> 22.3 us
    psum x1 -> x0, waiting for transfers between devices: 86.5 us -> none  [shards(): stream = lax.psum(attn_terms, 'ctx')]
    unnamed x3 -> x0, waiting for transfers between devices: 71.1 us -> none
    all_gather x1 -> x0, blocking collectives: 25.3 us -> none  [shards(): query_all = lax.all_gather(queries, 'ctx', axis=1, tiled=True)]
    all_to_all x0 -> x2, blocking collectives: none -> 22.3 us  [the longest x1 12.2 us: exchange(): lax.all_to_all(value, 'ctx', 0, 0, tiled=True, axis_index_groups=core_gro...]
    unnamed x1 -> x0, matrix products: 12.2 us -> none
    dot_general x2 -> x5, matrix products: 3.26 us -> 15.4 us  [the longest x1 9.52 us: shards(): jnp.dot(activated, down_proj, preferred_element_type=jnp.float32)]
    all_to_all x3 -> x2, waiting for transfers between devices: 23.9 us -> 19.4 us  [exchange(): lax.all_to_all(value, 'ctx', 0, 0, tiled=True, axis_index_groups=core_gro...]
    ppermute x0 -> x5, waiting for transfers between devices: none -> 3.5 us  [swap(): return lax.ppermute(value, 'ctx', [(i, i ^ 1) for i in range(count)])]
  transfers between devices with their start and end apart: 5 -> 7, of which waited for: 5 -> 5; matrix products, arithmetic and copies ran while one was open for 1% -> 6% of each run, Pallas kernels for 0% -> 0%
where the time goes in v1:
time: 97.9 us; the launch traced here: 97.2 us
  matrix products  27.3 us (28%)
  waiting for transfers between devices  22.9 us (23%)
  blocking collectives  22.3 us (23%)
  starting transfers between devices  11.7 us (12%)
  local copies, waits for them, and re-layouts  6.33 us (6%)
  other arithmetic  6.32 us (6%)
    all_to_all x2, waiting for transfers between devices, exchange(): lax.all_to_all(value, 'ctx', 0, 0, tiled=True, axis_index_groups=core_gro...  19.4 us
    all_to_all x1, blocking collectives, exchange(): lax.all_to_all(value, 'ctx', 0, 0, tiled=True, axis_index_groups=core_gro...  12.2 us
    all_to_all x2, starting transfers between devices, exchange(): lax.all_to_all(value, 'ctx', 0, 0, tiled=True, axis_index_groups=core_gro...  10.9 us
    all_to_all x1, blocking collectives, shards(): parts = lax.all_to_all(blocks.astype(jnp.bfloat16), 'ctx', 0, 0, tiled=True)  10.2 us
    dot_general x1, matrix products, shards(): jnp.dot(activated, down_proj, preferred_element_type=jnp.float32)  9.52 us
    dot_general x1, matrix products, shards(): attn_terms = jnp.dot(flat, out_proj, preferred_element_type=jnp.float32)  6.36 us
    dot_general x1, matrix products, shards(): gate_act = jnp.dot(normed, gate_proj, preferred_element_type=jnp.float32)  5.57 us
    ppermute x5, waiting for transfers between devices, swap(): return lax.ppermute(value, 'ctx', [(i, i ^ 1) for i in range(count)])  3.5 us
  transfers between devices with their start and end apart: 7, of which 5 were waited for; matrix products, arithmetic and copies ran while one was open for 6% of the time, Pallas kernels for 0%

profile of v1, /device:TPU:0, one launch (start us, length us, event | category | flops | bytes accessed | tf_op | source)
XLA Modules:
  0.0 97.2 jit_solution(2364887615928731393)
XLA Ops:
  0.0 1.6 %broadcast_in_dim.63 = bf16[8,32,576]{2,1,0:T(8,128)(2,1)} broadcast(bf16[32,576]{1,0:T(8,128)(2,1)} %bitcast.146), dimensions={1,2} | broadcast | bytes 331776 | tf_op jit(solution)/shard_map/broadcast_in_dim | solution.py:33
  1.6 7.3 %all-to-all-start = ((bf16[8,32,576]{2,1,0:T(8,128)(2,1)}), bf16[8,32,576]{2,1,0:T(8,128)(2,1)S(1)}, u32[]{:S(2)}, u32[]{:S(2)}) async-start(bf16[8,32,576]{2,1,0:T(8,128)(2,1)} %broadcast_in_dim.63), calls=%async_computation | async-start | bytes 655360 | tf_op jit(solution)/shard_map/all_to_all | solution.py:28
  8.9 0.7 broadcast_multiply_fusion
  9.6 0.1 fusion.51
  9.6 0.7 broadcast_bitcast_fusion
  10.4 8.8 %all-to-all-done = bf16[8,32,576]{2,1,0:T(8,128)(2,1)S(1)} async-done(((bf16[8,32,576]{2,1,0:T(8,128)(2,1)}), bf16[8,32,576]{2,1,0:T(8,128)(2,1)S(1)}, u32[]{:S(2)}, u32[]{:S(2)}) %all-to-all-start) | async-done | bytes 294944 | tf_op jit(solution)/shard_map/all_to_all | solution.py:28
  19.2 0.7 fusion.45
  19.9 1.5 %select_reduce_fusion.1 = (f32[8,4,8]{2,1,0:T(4,128)S(1)}, f32[8,4,8,512]{3,2,1,0:T(8,128)S(1)}) fusion(pred[4,512]{1,0:T(4,128)(4,1)S(1)} %fusion.45, bf16[512,576]{0,1:T(8,128)(2,1)} %param.13, bf16[8,32,576]{2,1,0:T(8,128)(2,1)S(1)} %all-to-all-done), kind=kOutput, calls=%fused_computation.20 | convolution fusion | flops 151387904 | bytes 1412096 | tf_op jit(solution)/shard_map/pbhe,te->pbht/dot_general | solution.py:39
  21.5 1.5 %fusion.15 = (f32[8,4,8]{2,1,0:T(4,128)S(1)}, f32[8,4,8]{2,1,0:T(4,128)S(1)}, f32[8,4,8,512]{3,2,1,0:T(8,128)S(1)}) fusion(f32[8,4,8,512]{3,2,1,0:T(8,128)S(1)} %get-tuple-element.18, f32[8,4,8]{2,1,0:T(4,128)S(1)} %get-tuple-element.17, pred[4,512]{1,0:T(4,128)(4,1)S(1)} %fusion.45, bf16[512,576]{0,1:T(8,128)(2,1)} %param.13, ...), kind=kOutput, calls=%fused_computation.25 | convolution fusion | flops 151780864 | bytes 1938432 | tf_op jit(solution)/shard_map/pbhe,te->pbht/dot_general | solution.py:39
  23.0 0.2 fusion.18
  23.3 0.6 collective-permute-start.1
  23.9 1.4 %convolution_convert_fusion.1 = bf16[8,4,8,512]{3,2,1,0:T(8,128)(2,1)S(1)} fusion(bf16[512,576]{0,1:T(8,128)(2,1)} %param.13, f32[8,4,8,512]{3,2,1,0:T(8,128)S(1)} %get-tuple-element.19, f32[8,4,8]{2,1,0:T(4,128)S(1)} %get-tuple-element.6, pred[4,512]{1,0:T(4,128)(4,1)S(1)} %fusion.45), kind=kOutput, calls=%fused_computation.6 | convolution fusion | flops 134742016 | bytes 1313792 | tf_op jit(solution)/shard_map/pbht,tc->pbhc/dot_general | solution.py:46
  25.3 0.1 collective-permute-start.2
  25.5 0.3 copy.93
  25.8 1.0 %collective-permute-done.2 = bf16[8,4,8,512]{3,2,1,0:T(8,128)(2,1)S(1)} collective-permute-done((bf16[8,4,8,512]{3,2,1,0:T(8,128)(2,1)S(1)}, bf16[8,4,8,512]{3,2,1,0:T(8,128)(2,1)S(1)}, u32[]{:S(2)}, u32[]{:S(2)}) %collective-permute-start.2) | collective-permute-done | bytes 262176 | tf_op jit(solution)/shard_map/ppermute | solution.py:19
  26.9 1.4 %fusion.12 = bf16[8,32,512]{2,1,0:T(8,128)(2,1)S(1)} fusion(bf16[8,4,8,512]{3,2,1,0:T(8,128)(2,1)S(1)} %collective-permute-done.2, bf16[512,576]{0,1:T(8,128)(2,1)} %param.13, f32[8,4,8,512]{3,2,1,0:T(8,128)S(1)} %get-tuple-element.18, f32[8,4,8]{2,1,0:T(4,128)S(1)} %copy.77, f32[8,4,8]{2,1,0:T(4,128)S(1)} %copy.76, f32[8,4,8]{2,1,0:T(4,128)S(1)} %get-tuple-element.17, ...), kind=kOutput, calls=%fused_computation.23 | convolution fusion | flops 135266304 | bytes 1577984 | tf_op jit(solution)/shard_map/pbht,tc->pbhc/dot_general | solution.py:46
  28.3 0.7 pad_maximum_fusion
  29.0 3.6 %all-to-all-start.1 = ((bf16[8,32,640]{2,1,0:T(8,128)(2,1)}), bf16[8,32,640]{2,1,0:T(8,128)(2,1)S(1)}, u32[]{:S(2)}, u32[]{:S(2)}) async-start(bf16[8,32,640]{2,1,0:T(8,128)(2,1)} %pad_maximum_fusion), calls=%async_computation.1 | async-start | bytes 655360 | tf_op jit(solution)/shard_map/all_to_all | solution.py:28
  32.6 10.6 %all-to-all-done.1 = bf16[8,32,640]{2,1,0:T(8,128)(2,1)S(1)} async-done(((bf16[8,32,640]{2,1,0:T(8,128)(2,1)}), bf16[8,32,640]{2,1,0:T(8,128)(2,1)S(1)}, u32[]{:S(2)}, u32[]{:S(2)}) %all-to-all-start.1) | async-done | bytes 327712 | tf_op jit(solution)/shard_map/all_to_all | solution.py:28
  43.2 1.3 %copy.83 = bf16[8,32,640]{1,0,2:T(8,128)(2,1)S(1)} copy(bf16[8,32,640]{2,1,0:T(8,128)(2,1)S(1)} %all-to-all-done.1) | data formatting | bytes 655360 | tf_op jit(solution)/shard_map/all_to_all | solution.py:28
  44.5 0.2 convert_element_type.63
  44.7 1.5 %copy-done.1 = f32[8,32,640]{1,0,2:T(8,128)} copy-done((f32[8,32,640]{1,0,2:T(8,128)}, f32[8,32,640]{1,0,2:T(8,128)S(1)}, u32[]{:S(2)}) %copy-start.1) | copy-done | bytes 655384
  46.2 0.1 div.18
  46.3 2.2 %fusion = f32[32,512]{0,1:T(8,128)S(1)} fusion(f32[8,32,640]{1,0,2:T(8,128)} %copy-done.1, f32[8,32]{1,0:T(8,128)S(1)} %exponential_bitcast_fusion), kind=kLoop, calls=%fused_computation.2 | loop fusion | flops 245760 | bytes 590848 | tf_op jit(solution)/shard_map/reduce_sum | solution.py:108
  48.6 0.0 copy-start.3
  48.6 0.1 copy.84
  48.7 0.1 fusion.29
  48.8 0.0 copy-done
  48.8 0.0 copy-start.2
  48.8 6.4 %fusion.5 = f32[4,7168]{1,0:T(4,128)S(1)} fusion(bf16[1024,7168]{1,0:T(8,128)(2,1)} %param.20, bf16[8,512,128]{2,1,0:T(8,128)(2,1)S(1)} %copy-done, bf16[4,8,512]{2,1,0:T(8,128)(2,1)S(1)} %fusion.29), kind=kOutput, calls=%fused_computation.13 | convolution fusion | flops 62918656 | bytes 15876096 | tf_op jit(solution)/shard_map/dot_general | solution.py:115
  55.1 0.1 convert_add_fusion
  55.2 0.2 dynamic_update_slice.3
  55.5 0.1 reshape.271
  55.6 0.1 constant_dynamic-slice_fusion.1
  55.7 0.1 collective-permute-start.3
  55.8 1.2 %collective-permute-done.3 = f32[4,3584]{1,0:T(4,128)S(1)} collective-permute-done((f32[4,3584]{1,0:T(4,128)S(1)}, f32[4,3584]{1,0:T(4,128)S(1)}, u32[]{:S(2)}, u32[]{:S(2)}) %collective-permute-start.3) | collective-permute-done | bytes 57376 | tf_op jit(solution)/shard_map/ppermute | solution.py:19
  57.1 0.1 broadcast_in_dim.66
  57.1 12.2 %all_to_all.20 = bf16[8,4,3584]{2,1,0:T(4,128)(2,1)S(1)} all-to-all(bf16[8,4,3584]{2,1,0:T(4,128)(2,1)S(1)} %broadcast_in_dim.66), channel_id=1, replica_groups={{0,2,4,6,8,10,12,14},{1,3,5,7,9,11,13,15},{16,18,20,22,24,26,28,30},{17..., dimensions={0} | all-to-all | bytes 458752 | tf_op jit(solution)/shard_map/all_to_all | solution.py:28
  69.3 0.2 convert_reduce_fusion
  69.5 0.1 collective-permute-start.4
  69.6 1.2 %collective-permute-done.4 = f32[4,3584]{1,0:T(4,128)S(1)} collective-permute-done((f32[4,3584]{1,0:T(4,128)S(1)}, f32[4,3584]{1,0:T(4,128)S(1)}, u32[]{:S(2)}, u32[]{:S(2)}) %collective-permute-start.4) | collective-permute-done | bytes 57376 | tf_op jit(solution)/shard_map/ppermute | solution.py:19
  70.8 0.2 multiply_reduce_fusion
  71.0 5.6 %fusion.58 = f32[4,576]{1,0:T(4,128)S(1)} fusion(bf16[7168,576]{0,1:T(8,128)(2,1)} %param.21, f32[4,3584]{1,0:T(4,128)S(1)} %get-tuple-element.12, f32[4,3584]{1,0:T(4,128)S(1)} %get-tuple-element.11, f32[7168]{0:T(1024)S(1)} %copy-done.2, f32[4]{0:T(128)S(1)} %add_rsqrt_fusion), kind=kOutput, calls=%fused_computation.120 | convolution fusion | flops 33144832 | bytes 8410128 | tf_op jit(solution)/shard_map/dot_general | solution.py:136
  76.6 9.5 %convolution_convert_fusion = bf16[4,7168]{1,0:T(4,128)(2,1)S(1)} fusion(bf16[576,7168]{1,0:T(8,128)(2,1)} %param.23, bf16[7168,576]{0,1:T(8,128)(2,1)} %param.22, f32[4,576]{1,0:T(4,128)S(1)} %fusion.58, f32[4,3584]{1,0:T(4,128)S(1)} %get-tuple-element.12, f32[4,3584]{1,0:T(4,128)S(1)} %get-tuple-element.11, f32[7168]{0:T(1024)S(1)} %copy-done.2, ...), kind=kOutput, calls=%fused_computation | convolution fusion | flops 66217472 | bytes 16725008 | tf_op jit(solution)/shard_map/dot_general | solution.py:139
  86.1 0.1 convert_element_type.73
  86.2 0.1 copy.117
  86.3 10.2 %all_to_all.21 = bf16[16,4,448]{2,1,0:T(4,128)(2,1)S(1)} all-to-all(bf16[16,4,448]{2,1,0:T(4,128)(2,1)S(1)} %bitcast.144), channel_id=1, replica_groups=mesh['groups'=2,'ctx'=16] {'ctx'}, dimensions={0} | all-to-all | bytes 114688 | tf_op jit(solution)/shard_map/all_to_all | solution.py:141
  96.5 0.7 add_convert_fusion.1
  (27 shorter events, 0.3 us)
Async XLA Ops:
  0.0 48.8 %copy-start = (bf16[8,512,128]{2,1,0:T(8,128)(2,1)S(1)}, bf16[8,512,128]{2,1,0:T(8,128)(2,1)}, u32[]{:S(2)}) copy-start(bf16[8,512,128]{2,1,0:T(8,128)(2,1)} %param.19) | copy-start | bytes 3145732
  1.6 17.6 %all-to-all-start = ((bf16[8,32,576]{2,1,0:T(8,128)(2,1)}), bf16[8,32,576]{2,1,0:T(8,128)(2,1)S(1)}, u32[]{:S(2)}, u32[]{:S(2)}) async-start(bf16[8,32,576]{2,1,0:T(8,128)(2,1)} %broadcast_in_dim.63), calls=%async_computation | async-start | bytes 655360 | tf_op jit(solution)/shard_map/all_to_all | solution.py:28
  19.2 2.3 %collective-permute-start = (bf16[8,32,576]{2,1,0:T(8,128)(2,1)S(1)}, bf16[8,32,576]{2,1,0:T(8,128)(2,1)S(1)}, u32[]{:S(2)}, u32[]{:S(2)}) collective-permute-start(bf16[8,32,576]{2,1,0:T(8,128)(2,1)S(1)} %all-to-all-done), channel_id=1, source_target_pairs={{0,1},{1,0},{2,3},{3,2},{4,5},{5,4},{6,7},{7,6},{8,9},{9,8},{10,11... | collective-permute-start | bytes 884744 | tf_op jit(solution)/shard_map/ppermute | solution.py:19
  23.3 2.1 %collective-permute-start.1 = (f32[2,8,4,8]{3,1,2,0:T(8,128)S(1)}, f32[2,8,4,8]{3,1,2,0:T(8,128)S(1)}, u32[]{:S(2)}, u32[]{:S(2)}) collective-permute-start(f32[2,8,4,8]{3,1,2,0:T(8,128)S(1)} %pad_maximum_fusion.2), channel_id=1, source_target_pairs={{0,1},{1,0},{2,3},{3,2},{4,5},{5,4},{6,7},{7,6},{8,9},{9,8},{10,11... | collective-permute-start | bytes 6152 | tf_op jit(solution)/shard_map/ppermute | solution.py:19
  25.3 1.6 %collective-permute-start.2 = (bf16[8,4,8,512]{3,2,1,0:T(8,128)(2,1)S(1)}, bf16[8,4,8,512]{3,2,1,0:T(8,128)(2,1)S(1)}, u32[]{:S(2)}, u32[]{:S(2)}) collective-permute-start(bf16[8,4,8,512]{3,2,1,0:T(8,128)(2,1)S(1)} %convolution_convert_fusion.1), channel_id=1, source_target_pairs={{0,1},{1,0},{2,3},{3,2},{4,5},{5,4},{6,7},{7,6},{8,9},{9,8},{10,11... | collective-permute-start | bytes 786440 | tf_op jit(solution)/shard_map/ppermute | solution.py:19
  29.0 14.2 %all-to-all-start.1 = ((bf16[8,32,640]{2,1,0:T(8,128)(2,1)}), bf16[8,32,640]{2,1,0:T(8,128)(2,1)S(1)}, u32[]{:S(2)}, u32[]{:S(2)}) async-start(bf16[8,32,640]{2,1,0:T(8,128)(2,1)} %pad_maximum_fusion), calls=%async_computation.1 | async-start | bytes 655360 | tf_op jit(solution)/shard_map/all_to_all | solution.py:28
  44.7 1.5 %copy-start.1 = (f32[8,32,640]{1,0,2:T(8,128)}, f32[8,32,640]{1,0,2:T(8,128)S(1)}, u32[]{:S(2)}) copy-start(f32[8,32,640]{1,0,2:T(8,128)S(1)} %convert_element_type.63) | copy-start | bytes 1966084
  48.6 6.6 %copy-start.3 = (bf16[4,448]{1,0:T(4,128)(2,1)S(1)}, bf16[4,448]{1,0:T(4,128)(2,1)}, u32[]{:S(2)}) copy-start(bf16[4,448]{1,0:T(4,128)(2,1)} %param.17) | copy-start | bytes 10756
  48.8 22.2 %copy-start.2 = (f32[7168]{0:T(1024)S(1)}, f32[7168]{0:T(1024)}, u32[]{:S(2)}) copy-start(f32[7168]{0:T(1024)} %param.18) | copy-start | bytes 86020
  55.7 1.3 %collective-permute-start.3 = (f32[4,3584]{1,0:T(4,128)S(1)}, f32[4,3584]{1,0:T(4,128)S(1)}, u32[]{:S(2)}, u32[]{:S(2)}) collective-permute-start(f32[4,3584]{1,0:T(4,128)S(1)} %bitcast.145), channel_id=1, source_target_pairs={{0,1},{1,0},{2,3},{3,2},{4,5},{5,4},{6,7},{7,6},{8,9},{9,8},{10,11... | collective-permute-start | bytes 172040 | tf_op jit(solution)/shard_map/ppermute | solution.py:19
  69.5 1.3 %collective-permute-start.4 = (f32[4,3584]{1,0:T(4,128)S(1)}, f32[4,3584]{1,0:T(4,128)S(1)}, u32[]{:S(2)}, u32[]{:S(2)}) collective-permute-start(f32[4,3584]{1,0:T(4,128)S(1)} %convert_reduce_fusion), channel_id=1, source_target_pairs={{0,1},{1,0},{2,3},{3,2},{4,5},{5,4},{6,7},{7,6},{8,9},{9,8},{10,11... | collective-permute-start | bytes 172040 | tf_op jit(solution)/shard_map/ppermute | solution.py:19

commit v2 on v0

v2 whole, which is shorter than its diff:
```python
import functools
import math

import jax
import jax.numpy as jnp
from jax import lax
from jax.experimental import pallas as pl
from jax.experimental.pallas import tpu as pltpu
from jax.sharding import PartitionSpec as P

LAT = 512
ROPE = 64
VHEAD = 128
PAGE = 128
LANES = 128
COLUMN_BLOCK = 1792
KERNEL_VMEM = 6 << 20
HINT_FLOPS = 100_000
HINT_TRANSCENDENTALS = 100_000_000


NEG_BIG = -1e30
EPS = 1e-06

VMEM = pl.BlockSpec(memory_space=pltpu.VMEM)
SMEM = pl.BlockSpec(memory_space=pltpu.SMEM)


def swap(value):
    count = lax.axis_size("ctx")
    return lax.ppermute(value, "ctx", [(i, i ^ 1) for i in range(count)])


def core_groups():
    count = lax.axis_size("ctx")
    return [list(range(core, count, 2)) for core in range(2)]


def exchange(value):
    return lax.all_to_all(value, "ctx", 0, 0, tiled=True, axis_index_groups=core_groups())


def spread(value):
    chips = lax.axis_size("ctx") // 2
    return exchange(jnp.broadcast_to(value[None], (chips,) + value.shape))


def call(kernel, out_shape, specs, operands, scratch=(), ahead=()):
    bytes_of = [x.size * x.dtype.itemsize for x in operands]
    flops = HINT_FLOPS * sum(x.size * x.dtype.itemsize for x in ahead)
    return pl.pallas_call(
        kernel,
        out_shape=out_shape,
        in_specs=list(specs),
        out_specs=jax.tree.map(lambda _: VMEM, out_shape),
        scratch_shapes=list(scratch),
        cost_estimate=pl.CostEstimate(
            flops=flops, bytes_accessed=sum(bytes_of), transcendentals=HINT_TRANSCENDENTALS
        ),
        compiler_params=pltpu.CompilerParams(vmem_limit_bytes=KERNEL_VMEM),
    )(*operands)


def as_pieces(value):
    high = value.astype(jnp.bfloat16).astype(jnp.float32)
    rest = value - high
    middle = rest.astype(jnp.bfloat16).astype(jnp.float32)
    return (high, middle, rest - middle)


def copies_kernel(query, copies):
    for chip in range(copies.shape[0]):
        copies[chip] = query[...]


def stats_tile(shard_max, total):
    lane = lax.broadcasted_iota(jnp.int32, (shard_max.shape[0], LANES), 1)
    tile = jnp.zeros(lane.shape, jnp.float32)
    for at, piece in enumerate(as_pieces(shard_max) + as_pieces(total)):
        tile = jnp.where(lane == at, piece, tile)
    return tile.astype(jnp.bfloat16)


def from_stats(tile):
    tile = tile.astype(jnp.float32)
    shard_max = tile[:, 0:1] + tile[:, 1:2] + tile[:, 2:3]
    total = tile[:, 3:4] + tile[:, 4:5] + tile[:, 5:6]
    return (shard_max, total)


def attend(rows, heads, page_row, page_index, lengths, query, cache):
    scale = float(VHEAD + ROPE) ** (-0.5)
    scores = jnp.dot(query[...], cache[...], preferred_element_type=jnp.float32) * scale
    line = lax.broadcasted_iota(jnp.int32, (query.shape[0], PAGE), 0)
    lane = lax.broadcasted_iota(jnp.int32, (query.shape[0], PAGE), 1)
    row_of = lax.rem(lax.div(line, jnp.int32(heads)), jnp.int32(rows))
    visible, blocks = [], []
    for page in range(cache.shape[1] // PAGE):
        owner = page_row[page]
        filled = lengths[owner] - page_index[page] * PAGE
        visible.append((row_of == owner) & (lane < filled))
        blocks.append(scores[:, page * PAGE : (page + 1) * PAGE])
    top = jnp.full((query.shape[0], PAGE), NEG_BIG, jnp.float32)
    for seen, block in zip(visible, blocks):
        top = jnp.maximum(top, jnp.where(seen, block, NEG_BIG))
    shard_max = jnp.max(top, axis=1, keepdims=True)
    weights = [
        jnp.where(seen, jnp.exp(block - shard_max), 0.0) for seen, block in zip(visible, blocks)
    ]
    total = jnp.sum(functools.reduce(jnp.add, weights), axis=1, keepdims=True)
    latent = lax.dot_general(
        jnp.concatenate(weights, axis=1).astype(jnp.bfloat16),
        cache[:LAT, :],
        (((1,), (1,)), ((), ())),
        preferred_element_type=jnp.float32,
    )
    return (shard_max, total, latent)


def send_kernel(rows, heads, page_row, page_index, lengths, query, cache, message):
    shard_max, total, latent = attend(rows, heads, page_row, page_index, lengths, query, cache)
    message[:, :LAT] = latent.astype(jnp.bfloat16)
    message[:, LAT:] = stats_tile(shard_max, total)


def keep_kernel(rows, heads, page_row, page_index, lengths, query, cache, latent_out, stats):
    shard_max, total, latent = attend(rows, heads, page_row, page_index, lengths, query, cache)
    latent_out[...] = latent
    stats[:, :LANES] = jnp.broadcast_to(shard_max, (shard_max.shape[0], LANES))
    stats[:, LANES:] = jnp.broadcast_to(total, (total.shape[0], LANES))


def merge_kernel(latent_own, stats, received, message):
    max_own, total_own = stats[:, 0:1], stats[:, LANES : LANES + 1]
    max_in, total_in = from_stats(received[:, LAT:])
    chip_max = jnp.maximum(max_own, max_in)
    factor_own = jnp.exp(max_own - chip_max)
    factor_in = jnp.exp(max_in - chip_max)
    latent = latent_own[...] * factor_own + received[:, :LAT].astype(jnp.float32) * factor_in
    message[:, :LAT] = latent.astype(jnp.bfloat16)
    message[:, LAT:] = stats_tile(chip_max, total_own * factor_own + total_in * factor_in)


def own_span(width_dev):
    index = lax.axis_index("ctx")
    span = math.lcm(width_dev, LANES)
    start = pl.multiple_of(lax.div(index, span // width_dev) * span, LANES)
    return (start, span, lax.rem(index, span // width_dev))


def heads_kernel(rows, heads, parts, absorb, out_proj, hidden, keep, send, latent_buf):
    chips = parts.shape[0]
    stats = [from_stats(parts[chip, :, LAT:]) for chip in range(chips)]
    joint = functools.reduce(jnp.maximum, [shard_max for shard_max, _ in stats])
    total = jnp.zeros_like(joint)
    latent = jnp.zeros((rows * heads, LAT), jnp.float32)
    for chip, (shard_max, part_total) in enumerate(stats):
        factor = jnp.exp(shard_max - joint)
        total += part_total * factor
        latent += parts[chip, :, :LAT].astype(jnp.float32) * factor
    latent = latent / total
    tiles = range(LAT // LANES)
    for tile in tiles:
        latent_buf[tile] = latent[:, tile * LANES : (tile + 1) * LANES]
    value_heads = []
    for head in range(heads):
        lines = pl.ds(head, rows, stride=heads)
        own = jnp.concatenate([latent_buf[tile, lines, :] for tile in tiles], axis=1)
        own = own.astype(jnp.bfloat16)
        value_heads.append(jnp.dot(own, absorb[head], preferred_element_type=jnp.float32))
    flat = jnp.concatenate(value_heads, axis=1).astype(jnp.bfloat16)
    core = lax.rem(lax.axis_index("ctx"), 2)
    half = keep.shape[1]
    step = math.gcd(half, COLUMN_BLOCK)
    for target, start in ((send, (1 - core) * half), (keep, core * half)):
        for at in range(0, half, step):
            columns = pl.ds(pl.multiple_of(start + at, LANES), step)
            terms = jnp.dot(flat, out_proj[:, columns], preferred_element_type=jnp.float32)
            target[:, at : at + step] = terms
    width_dev = hidden.shape[1]
    start, span, place = own_span(width_dev)
    own = hidden[...].astype(jnp.float32)
    residual = jnp.zeros((rows, span), jnp.float32)
    for at in range(span // width_dev):
        before, after = at * width_dev, span - (at + 1) * width_dev
        pads = [jnp.zeros((rows, size), jnp.float32) for size in (before, after)]
        parts_of = [pads[0]] * (before > 0) + [own] + [pads[1]] * (after > 0)
        residual = jnp.where(place == at, jnp.concatenate(parts_of, axis=1), residual)
    in_half = pl.ds(pl.multiple_of(lax.rem(start, half), LANES), span)
    kept = lax.div(start, half) == core

    @pl.when(kept)
    def _():
        keep[:, in_half] += residual

    @pl.when(jnp.logical_not(kept))
    def _():
        send[:, in_half] += residual


def ffn_kernel(mine, other, gain, gate, up, down, blocks, stream_own):
    rows, half = mine.shape
    width = 2 * half
    core = lax.rem(lax.axis_index("ctx"), 2)
    square = jnp.sum(mine[...] * mine[...], axis=1, keepdims=True)
    square += jnp.sum(other[...] * other[...], axis=1, keepdims=True)
    norm_scale = lax.rsqrt(square / width + EPS)
    step = math.gcd(half, COLUMN_BLOCK)
    gate_act = jnp.zeros((rows, gate.shape[0]), jnp.float32)
    up_act = jnp.zeros((rows, gate.shape[0]), jnp.float32)
    minor = (((1,), (1,)), ((), ()))
    for source, start in ((mine, core * half), (other, (1 - core) * half)):
        for at in range(0, half, step):
            columns = pl.ds(pl.multiple_of(start + at, LANES), step)
            normed = source[:, at : at + step] * norm_scale * gain[:, columns]
            normed = normed.astype(jnp.bfloat16)
            gate_act += lax.dot_general(
                normed, gate[:, columns], minor, preferred_element_type=jnp.float32
            )
            up_act += lax.dot_general(
                normed, up[:, columns], minor, preferred_element_type=jnp.float32
            )
    activated = (gate_act / (1.0 + jnp.exp(-gate_act)) * up_act).astype(jnp.bfloat16)
    count, _, width_dev = blocks.shape
    step = math.lcm(width_dev, LANES)
    for at in range(0, width, step):
        terms = jnp.dot(activated, down[:, at : at + step], preferred_element_type=jnp.float32)
        terms = terms.astype(jnp.bfloat16)
        for inner in range(0, step, width_dev):
            blocks[(at + inner) // width_dev] = terms[:, inner : inner + width_dev]
    start, span, place = own_span(width_dev)
    in_half = pl.ds(pl.multiple_of(lax.rem(start, half), LANES), span)
    near = jnp.where(lax.div(start, half) == core, mine[:, in_half], other[:, in_half])
    own = near[:, :width_dev]
    for at in range(1, span // width_dev):
        own = jnp.where(place == at, near[:, at * width_dev : (at + 1) * width_dev], own)
    stream_own[...] = own


def shards(
    queries,
    cache,
    page_row,
    page_index,
    lengths,
    hidden_in,
    norm_gain,
    absorb_value,
    out_proj,
    gate_proj,
    up_proj,
    down_proj,
):
    rows, heads, entry = queries.shape
    count = lax.axis_size("ctx")
    chips = count // 2
    width_dev = hidden_in.shape[1]
    width = out_proj.shape[1]
    half = width // 2
    lines = rows * heads
    group = chips * lines
    bf16, f32 = jnp.bfloat16, jnp.float32
    shaped = jax.ShapeDtypeStruct

    copies = call(
        copies_kernel,
        shaped((chips, lines, entry), bf16),
        [VMEM],
        (queries.reshape(lines, entry),),
        ahead=(cache, cache),
    )
    query_own = exchange(copies).reshape(group, entry)
    query_other = swap(query_own)
    cache_t = cache.T
    tables = (page_row, page_index, lengths)
    specs = [SMEM, SMEM, SMEM, VMEM, VMEM]
    message = call(
        functools.partial(send_kernel, rows, heads),
        shaped((group, LAT + LANES), bf16),
        specs,
        tables + (query_other, cache_t),
    )
    received = swap(message)
    latent_own, stats = call(
        functools.partial(keep_kernel, rows, heads),
        (shaped((group, LAT), f32), shaped((group, 2 * LANES), f32)),
        specs,
        tables + (query_own, cache_t),
    )
    message = call(
        merge_kernel,
        shaped((group, LAT + LANES), bf16),
        [VMEM] * 3,
        (latent_own, stats, received),
        ahead=(absorb_value, out_proj),
    )
    parts = exchange(message.reshape(chips, lines, LAT + LANES))

    keep, send = call(
        functools.partial(heads_kernel, rows, heads),
        (shaped((rows, half), f32), shaped((rows, half), f32)),
        [VMEM] * 4,
        (parts, absorb_value, out_proj, hidden_in),
        scratch=[pltpu.VMEM((LAT // LANES, lines, LANES), f32)],
        ahead=(gate_proj, up_proj, down_proj),
    )
    chip_terms = (keep + swap(send)).astype(bf16)
    mine = jnp.sum(spread(chip_terms).astype(f32), axis=0)
    other = swap(mine)
    blocks, stream_own = call(
        ffn_kernel,
        (shaped((count, rows, width_dev), bf16), shaped((rows, width_dev), f32)),
        [VMEM] * 6,
        (mine, other, norm_gain[None], gate_proj.T, up_proj.T, down_proj),
    )
    received = lax.all_to_all(blocks, "ctx", 0, 0, tiled=True)
    return (stream_own + jnp.sum(received.astype(f32), axis=0)).astype(bf16)


def solution(mesh):
    in_specs = (
        P("groups", "ctx", None),
        P(("groups", "ctx"), None),
        P(("groups", "ctx")),
        P(("groups", "ctx")),
        P("groups"),
        P("groups", "ctx"),
        P(),
        P("ctx", None, None),
        P("ctx", None),
        P(None, "ctx"),
        P(None, "ctx"),
        P("ctx", None),
    )
    out_specs = P("groups", "ctx")
    return jax.shard_map(shards, mesh=mesh, in_specs=in_specs, out_specs=out_specs, check_vma=False)
```

time: 269 us -> 72.5 us (0.27)
  waiting for transfers between devices: 182 us -> 4.31 us
  blocking collectives: 25.3 us -> 54.6 us
  matrix products: 27.5 us -> 0 us
  between operations: 13.5 us -> 0.13 us
  Pallas kernels: 0 us -> 11.2 us
  starting transfers between devices: 10.6 us -> 0.27 us
  local copies, waits for them, and re-layouts: 5.74 us -> 0.89 us
  other arithmetic: 4.41 us -> 0.84 us
    psum x1 -> x0, waiting for transfers between devices: 86.5 us -> none  [shards(): stream = lax.psum(attn_terms, 'ctx')]
    unnamed x3 -> x0, waiting for transfers between devices: 71.1 us -> none
    all_to_all x0 -> x4, blocking collectives: none -> 54.6 us  [the longest x3 44.4 us: exchange(): lax.all_to_all(value, 'ctx', 0, 0, tiled=True, axis_index_groups=core_gro...]
    all_gather x1 -> x0, blocking collectives: 25.3 us -> none  [shards(): query_all = lax.all_gather(queries, 'ctx', axis=1, tiled=True)]
    all_to_all x3 -> x0, waiting for transfers between devices: 23.9 us -> none  [the longest x1 13.7 us: shards(): lax.all_to_all(shard_latent[None].astype(jnp.bfloat16), 'ctx', split_axis...]
    dot_general x4 -> x0, matrix products: 15.3 us -> none  [the longest x1 6.36 us: shards(): attn_terms = jnp.dot(flat, out_proj, preferred_element_type=jnp.float32)]
    unnamed x1 -> x0, matrix products: 12.2 us -> none
    pallas_call x0 -> x6, Pallas kernels: none -> 11.2 us  [call(): pl.pallas_call(kernel, out_shape=out_shape, in_specs=list(specs), out_spe...]
  transfers between devices with their start and end apart: 5 -> 4, of which waited for: 5 -> 4; matrix products, arithmetic and copies ran while one was open for 1% -> 0% of each run, Pallas kernels for 0% -> 2%
where the time goes in v2:
time: 72.5 us; the launch traced here: 72.2 us
  blocking collectives  54.6 us (75%)
  Pallas kernels  11.2 us (15%)
  waiting for transfers between devices  4.31 us (6%)
  local copies, waits for them, and re-layouts  0.89 us (1%)
  other arithmetic  0.84 us (1%)
    all_to_all x3, blocking collectives, exchange(): lax.all_to_all(value, 'ctx', 0, 0, tiled=True, axis_index_groups=core_gro...  44.4 us
    pallas_call x6, Pallas kernels, call(): pl.pallas_call(kernel, out_shape=out_shape, in_specs=list(specs), out_spe...  11.2 us
    all_to_all x1, blocking collectives, shards(): received = lax.all_to_all(blocks, 'ctx', 0, 0, tiled=True)  10.2 us
    ppermute x4, waiting for transfers between devices, swap(): return lax.ppermute(value, 'ctx', [(i, i ^ 1) for i in range(count)])  4.31 us
  transfers between devices with their start and end apart: 4, of which 4 were waited for; matrix products, arithmetic and copies ran while one was open for 0% of the time, Pallas kernels for 2%

profile of v2, /device:TPU:0, one launch (start us, length us, event | category | flops | bytes accessed | tf_op | source)
XLA Modules:
  0.0 72.2 jit_solution(8544069510978920070)
XLA Ops:
  0.0 0.0 copy-start.6
  0.0 0.8 %copy-done.6 = bf16[4,8,576]{2,1,0:T(8,128)(2,1)S(1)} copy-done((bf16[4,8,576]{2,1,0:T(8,128)(2,1)S(1)}, bf16[4,8,576]{2,1,0:T(8,128)(2,1)}, u32[]{:S(2)}) %copy-start.6) | copy-done | bytes 36888
  0.8 0.0 copy-start.5
  0.8 0.0 copy-start.9
  0.8 0.0 copy-start.10
  0.8 0.0 copy-start.11
  0.8 18.1 %all_to_all.20 = bf16[8,32,576]{2,1,0:T(8,128)(2,1)S(1)} all-to-all(bf16[8,32,576]{2,1,0:T(8,128)(2,1)S(1)} %shard_map.118), channel_id=1, replica_groups={{0,2,4,6,8,10,12,14},{1,3,5,7,9,11,13,15},{16,18,20,22,24,26,28,30},{17..., dimensions={0} | all-to-all | bytes 589824 | tf_op jit(solution)/shard_map/all_to_all | solution.py:40
  19.0 0.0 collective-permute-start
  19.0 1.6 %collective-permute-done.query = bf16[256,576]{1,0:T(8,128)(2,1)S(1)} collective-permute-done((bf16[256,576]{1,0:T(8,128)(2,1)S(1)}, bf16[256,576]{1,0:T(8,128)(2,1)S(1)}, u32[]{:S(2)}, u32[]{:S(2)}) %collective-permute-start) | collective-permute-done | bytes 294944 | tf_op jit(solution)/shard_map/ppermute | solution.py:31
  20.6 0.0 copy-done.5
  20.6 0.0 copy-done.9
  20.6 0.0 copy-done.10
  20.6 0.0 copy-done.11
  20.6 1.3 %shard_map.120 = bf16[256,640]{1,0:T(8,128)(2,1)S(1)} custom-call(s32[4]{0:T(128)S(1)} %copy-done.9, s32[4]{0:T(128)S(1)} %copy-done.10, s32[4]{0:T(128)S(1)} %copy-done.11, bf16[256,576]{1,0:T(8,128)(2,1)S(1)} %collective-permute-done.query, bf16[576,512]{1,0:T(8,128)(2,1)S(1)} %bitcast.12), custom_call_target="tpu_custom_call" | custom-call | bytes 884784 | tf_op jit(solution)/shard_map/pallas_call | solution.py:51
  22.0 0.2 collective-permute-start.1
  22.1 1.3 %shard_map.119 = (f32[256,512]{1,0:T(8,128)S(1)}, f32[256,256]{1,0:T(8,128)S(1)}) custom-call(s32[4]{0:T(128)S(1)} %copy-done.9, s32[4]{0:T(128)S(1)} %copy-done.10, s32[4]{0:T(128)S(1)} %copy-done.11, bf16[256,576]{1,0:T(8,128)(2,1)S(1)} %bitcast.8, bf16[576,512]{1,0:T(8,128)(2,1)S(1)} %bitcast.13), custom_call_target="tpu_custom_call" | custom-call | bytes 884784 | tf_op jit(solution)/shard_map/pallas_call | solution.py:51
  23.4 0.2 collective-permute-done.1.received
  23.6 0.0 copy-start
  23.6 0.0 copy-start.4
  23.7 0.0 copy-start.8
  23.7 0.5 shard_map.121
  24.1 14.5 %all_to_all.21.parts = bf16[8,32,640]{2,1,0:T(8,128)(2,1)S(1)} all-to-all(bf16[8,32,640]{2,1,0:T(8,128)(2,1)S(1)} %bitcast.9), channel_id=1, replica_groups={{0,2,4,6,8,10,12,14},{1,3,5,7,9,11,13,15},{16,18,20,22,24,26,28,30},{17..., dimensions={0} | all-to-all | bytes 655360 | tf_op jit(solution)/shard_map/all_to_all | solution.py:40
  38.6 0.0 copy-done
  38.6 0.0 copy-done.4
  38.6 0.0 copy-done.8
  38.6 0.0 copy-start.1
  38.6 0.0 copy-start.2
  38.6 0.0 copy-start.3
  38.7 0.0 copy-start.7
  38.7 2.4 %shard_map.122 = (f32[4,3584]{1,0:T(4,128)S(1)}, f32[4,3584]{1,0:T(4,128)S(1)}) custom-call(bf16[8,32,640]{2,1,0:T(8,128)(2,1)S(1)} %all_to_all.21.parts, bf16[8,512,128]{2,1,0:T(8,128)(2,1)S(1)} %copy-done.4, bf16[1024,7168]{1,0:T(8,128)(2,1)S(1)} %copy-done, bf16[4,448]{1,0:T(4,128)(2,1)S(1)} %copy-done.8), custom_call_target="tpu_custom_call" | custom-call | flops 2477260800000 | bytes 16059904 | tf_op jit(solution)/shard_map/pallas_call | solution.py:51
  41.1 0.0 collective-permute-start.2
  41.1 1.2 %collective-permute-done.2 = f32[4,3584]{1,0:T(4,128)S(1)} collective-permute-done((f32[4,3584]{1,0:T(4,128)S(1)}, f32[4,3584]{1,0:T(4,128)S(1)}, u32[]{:S(2)}, u32[]{:S(2)}) %collective-permute-start.2) | collective-permute-done | bytes 57376 | tf_op jit(solution)/shard_map/ppermute | solution.py:31
  42.4 0.1 broadcast_in_dim.4
  42.5 11.8 %all_to_all.22 = bf16[8,4,3584]{2,1,0:T(4,128)(2,1)S(1)} all-to-all(bf16[8,4,3584]{2,1,0:T(4,128)(2,1)S(1)} %broadcast_in_dim.4), channel_id=1, replica_groups={{0,2,4,6,8,10,12,14},{1,3,5,7,9,11,13,15},{16,18,20,22,24,26,28,30},{17..., dimensions={0} | all-to-all | bytes 458752 | tf_op jit(solution)/shard_map/all_to_all | solution.py:40
  54.3 0.2 convert_reduce_fusion.mine
  54.4 0.1 collective-permute-start.3
  54.5 1.2 %collective-permute-done.3.other = f32[4,3584]{1,0:T(4,128)S(1)} collective-permute-done((f32[4,3584]{1,0:T(4,128)S(1)}, f32[4,3584]{1,0:T(4,128)S(1)}, u32[]{:S(2)}, u32[]{:S(2)}) %collective-permute-start.3) | collective-permute-done | bytes 57376 | tf_op jit(solution)/shard_map/ppermute | solution.py:31
  55.8 0.0 copy-done.1
  55.8 0.0 copy-done.2
  55.8 0.0 copy-done.3
  55.8 0.0 copy-done.7
  55.8 5.7 %shard_map.123 = (bf16[16,4,448]{2,1,0:T(4,128)(2,1)S(1)}, f32[4,448]{1,0:T(4,128)S(1)}) custom-call(f32[4,3584]{1,0:T(4,128)S(1)} %convert_reduce_fusion.mine, f32[4,3584]{1,0:T(4,128)S(1)} %collective-permute-done.3.other, f32[1,7168]{1,0:T(1,128)S(1)} %bitcast.15, bf16[576,7168]{1,0:T(8,128)(2,1)S(1)} %bitcast.10, bf16[576,7168]{1,0:T(8,128)(2,1)S(1)} %bitcast.11, ...), custom_call_target="tpu_custom_call" | custom-call | bytes 24915968 | tf_op jit(solution)/shard_map/pallas_call | solution.py:51
  61.4 10.2 %all_to_all.23 = bf16[16,4,448]{2,1,0:T(4,128)(2,1)S(1)} all-to-all(bf16[16,4,448]{2,1,0:T(4,128)(2,1)S(1)} %get-tuple-element.16), channel_id=1, replica_groups=mesh['groups'=2,'ctx'=16] {'ctx'}, dimensions={0} | all-to-all | bytes 114688 | tf_op jit(solution)/shard_map/all_to_all | solution.py:316
  71.6 0.6 add_convert_fusion.1
  (3 shorter events, 0.1 us)
Async XLA Ops:
  0.0 0.8 %copy-start.6 = (bf16[4,8,576]{2,1,0:T(8,128)(2,1)S(1)}, bf16[4,8,576]{2,1,0:T(8,128)(2,1)}, u32[]{:S(2)}) copy-start(bf16[4,8,576]{2,1,0:T(8,128)(2,1)} %param.12) | copy-start | bytes 110596
  0.8 19.8 %copy-start.5 = (bf16[512,576]{0,1:T(8,128)(2,1)S(1)}, bf16[512,576]{0,1:T(8,128)(2,1)}, u32[]{:S(2)}) copy-start(bf16[512,576]{0,1:T(8,128)(2,1)} %param.13) | copy-start | bytes 1769476
  0.8 19.8 %copy-start.9 = (s32[4]{0:T(128)S(1)}, s32[4]{0:T(128)}, u32[]{:S(2)}) copy-start(s32[4]{0:T(128)} %page_row.3) | copy-start | bytes 52
  0.8 19.8 %copy-start.10 = (s32[4]{0:T(128)S(1)}, s32[4]{0:T(128)}, u32[]{:S(2)}) copy-start(s32[4]{0:T(128)} %page_index.3) | copy-start | bytes 52
  0.8 19.8 %copy-start.11 = (s32[4]{0:T(128)S(1)}, s32[4]{0:T(128)}, u32[]{:S(2)}) copy-start(s32[4]{0:T(128)} %lengths.3) | copy-start | bytes 52
  19.0 1.6 %collective-permute-start = (bf16[256,576]{1,0:T(8,128)(2,1)S(1)}, bf16[256,576]{1,0:T(8,128)(2,1)S(1)}, u32[]{:S(2)}, u32[]{:S(2)}) collective-permute-start(bf16[256,576]{1,0:T(8,128)(2,1)S(1)} %bitcast.7), channel_id=1, source_target_pairs={{0,1},{1,0},{2,3},{3,2},{4,5},{5,4},{6,7},{7,6},{8,9},{9,8},{10,11... | collective-permute-start | bytes 884744 | tf_op jit(solution)/shard_map/ppermute | solution.py:31
  22.0 1.7 %collective-permute-start.1 = (bf16[256,640]{1,0:T(8,128)(2,1)S(1)}, bf16[256,640]{1,0:T(8,128)(2,1)S(1)}, u32[]{:S(2)}, u32[]{:S(2)}) collective-permute-start(bf16[256,640]{1,0:T(8,128)(2,1)S(1)} %shard_map.120), channel_id=1, source_target_pairs={{0,1},{1,0},{2,3},{3,2},{4,5},{5,4},{6,7},{7,6},{8,9},{9,8},{10,11... | collective-permute-start | bytes 983048 | tf_op jit(solution)/shard_map/ppermute | solution.py:31
  23.6 15.0 %copy-start = (bf16[1024,7168]{1,0:T(8,128)(2,1)S(1)}, bf16[1024,7168]{1,0:T(8,128)(2,1)}, u32[]{:S(2)}) copy-start(bf16[1024,7168]{1,0:T(8,128)(2,1)} %out_proj.1) | copy-start | bytes 44040196
  23.6 15.0 %copy-start.4 = (bf16[8,512,128]{2,1,0:T(8,128)(2,1)S(1)}, bf16[8,512,128]{2,1,0:T(8,128)(2,1)}, u32[]{:S(2)}) copy-start(bf16[8,512,128]{2,1,0:T(8,128)(2,1)} %absorb.1) | copy-start | bytes 3145732
  23.7 15.0 %copy-start.8 = (bf16[4,448]{1,0:T(4,128)(2,1)S(1)}, bf16[4,448]{1,0:T(4,128)(2,1)}, u32[]{:S(2)}) copy-start(bf16[4,448]{1,0:T(4,128)(2,1)} %hidden.1) | copy-start | bytes 10756
  38.6 17.1 %copy-start.1 = (bf16[7168,576]{0,1:T(8,128)(2,1)S(1)}, bf16[7168,576]{0,1:T(8,128)(2,1)}, u32[]{:S(2)}) copy-start(bf16[7168,576]{0,1:T(8,128)(2,1)} %param.21) | copy-start | bytes 24772612
  38.6 17.1 %copy-start.2 = (bf16[7168,576]{0,1:T(8,128)(2,1)S(1)}, bf16[7168,576]{0,1:T(8,128)(2,1)}, u32[]{:S(2)}) copy-start(bf16[7168,576]{0,1:T(8,128)(2,1)} %param.22) | copy-start | bytes 24772612
  38.6 17.1 %copy-start.3 = (bf16[576,7168]{1,0:T(8,128)(2,1)S(1)}, bf16[576,7168]{1,0:T(8,128)(2,1)}, u32[]{:S(2)}) copy-start(bf16[576,7168]{1,0:T(8,128)(2,1)} %down.1) | copy-start | bytes 24772612
  38.7 17.1 %copy-start.7 = (f32[7168]{0:T(1024)S(1)}, f32[7168]{0:T(1024)}, u32[]{:S(2)}) copy-start(f32[7168]{0:T(1024)} %param.18) | copy-start | bytes 86020
  41.1 1.2 %collective-permute-start.2 = (f32[4,3584]{1,0:T(4,128)S(1)}, f32[4,3584]{1,0:T(4,128)S(1)}, u32[]{:S(2)}, u32[]{:S(2)}) collective-permute-start(f32[4,3584]{1,0:T(4,128)S(1)} %get-tuple-element.14), channel_id=1, source_target_pairs={{0,1},{1,0},{2,3},{3,2},{4,5},{5,4},{6,7},{7,6},{8,9},{9,8},{10,11... | collective-permute-start | bytes 172040 | tf_op jit(solution)/shard_map/ppermute | solution.py:31
  54.4 1.3 %collective-permute-start.3 = (f32[4,3584]{1,0:T(4,128)S(1)}, f32[4,3584]{1,0:T(4,128)S(1)}, u32[]{:S(2)}, u32[]{:S(2)}) collective-permute-start(f32[4,3584]{1,0:T(4,128)S(1)} %convert_reduce_fusion.mine), channel_id=1, source_target_pairs={{0,1},{1,0},{2,3},{3,2},{4,5},{5,4},{6,7},{7,6},{8,9},{9,8},{10,11... | collective-permute-start | bytes 172040 | tf_op jit(solution)/shard_map/ppermute | solution.py:31

commit v3 on v2

v3 whole, which is shorter than its diff:
```python
import functools
import math

import jax
import jax.numpy as jnp
from jax import lax
from jax.experimental import pallas as pl
from jax.experimental.pallas import tpu as pltpu
from jax.sharding import PartitionSpec as P

LAT = 512
ROPE = 64
VHEAD = 128
PAGE = 128
LANES = 128
COLUMN_BLOCK = 1792
KERNEL_VMEM = 12 << 20
HINT_FLOPS = 100_000
HINT_TRANSCENDENTALS = 100_000_000


NEG_BIG = -1e30
EPS = 1e-06

VMEM = pl.BlockSpec(memory_space=pltpu.VMEM)
HBM = pl.BlockSpec(memory_space=pltpu.HBM)


def swap(value):
    count = lax.axis_size("ctx")
    return lax.ppermute(value, "ctx", [(i, i ^ 1) for i in range(count)])


def core_groups():
    count = lax.axis_size("ctx")
    return [list(range(core, count, 2)) for core in range(2)]


def gather_blocks(block):
    count = lax.axis_size("ctx")
    blocks, mask = {0: block}, count // 4
    while mask:
        pairs = [(i, i ^ (2 * mask)) for i in range(count)]
        blocks |= {mask | at: lax.ppermute(held, "ctx", pairs) for at, held in blocks.items()}
        mask //= 2
    return blocks


def exchange(value):
    return lax.all_to_all(value, "ctx", 0, 0, tiled=True, axis_index_groups=core_groups())


def spread(value):
    chips = lax.axis_size("ctx") // 2
    return exchange(jnp.broadcast_to(value[None], (chips,) + value.shape))


def call(kernel, out_shape, specs, operands, scratch=(), ahead=()):
    bytes_of = [x.size * x.dtype.itemsize for x in operands]
    flops = HINT_FLOPS * sum(x.size * x.dtype.itemsize for x in ahead)
    return pl.pallas_call(
        kernel,
        out_shape=out_shape,
        in_specs=list(specs),
        out_specs=jax.tree.map(lambda _: VMEM, out_shape),
        scratch_shapes=list(scratch),
        cost_estimate=pl.CostEstimate(
            flops=flops, bytes_accessed=sum(bytes_of), transcendentals=HINT_TRANSCENDENTALS
        ),
        compiler_params=pltpu.CompilerParams(vmem_limit_bytes=KERNEL_VMEM),
    )(*operands)


def as_pieces(value):
    high = value.astype(jnp.bfloat16).astype(jnp.float32)
    rest = value - high
    middle = rest.astype(jnp.bfloat16).astype(jnp.float32)
    return (high, middle, rest - middle)


def stats_tile(shard_max, total):
    lane = lax.broadcasted_iota(jnp.int32, (shard_max.shape[0], LANES), 1)
    tile = jnp.zeros(lane.shape, jnp.float32)
    for at, piece in enumerate(as_pieces(shard_max) + as_pieces(total)):
        tile = jnp.where(lane == at, piece, tile)
    return tile.astype(jnp.bfloat16)


def from_stats(tile):
    tile = tile.astype(jnp.float32)
    shard_max = tile[:, 0:1] + tile[:, 1:2] + tile[:, 2:3]
    total = tile[:, 3:4] + tile[:, 4:5] + tile[:, 5:6]
    return (shard_max, total)


def first_kernel(mark):
    mark[...] = jnp.zeros_like(mark)


def table_kernel(page_row, page_index, lengths, mark, table, *scratch):
    held, arrived = scratch[:3], scratch[3]
    copies = [
        pltpu.make_async_copy(source, target, arrived.at[at])
        for at, (source, target) in enumerate(zip((page_row, page_index, lengths), held))
    ]
    for copy in copies:
        copy.start()
    for copy in copies:
        copy.wait()
    rows_held, index_held, lengths_held = held
    for page in range(page_row.shape[0]):
        owner = rows_held[page]
        filled = lengths_held[owner] - index_held[page] * PAGE
        table[2 * page : 2 * page + 1] = jnp.full((1, LANES), owner, jnp.int32)
        table[2 * page + 1 : 2 * page + 2] = jnp.full((1, LANES), filled, jnp.int32)


def attend_kernel(rows, heads, masks, tables, queries, own, other, before, message):
    query = jnp.concatenate([block[...] for block in queries], axis=0)
    scale = float(VHEAD + ROPE) ** (-0.5)
    shape = (query.shape[0], PAGE)
    line = lax.broadcasted_iota(jnp.int32, shape, 0)
    lane = lax.broadcasted_iota(jnp.int32, shape, 1)
    row_of = lax.rem(lax.div(line, jnp.int32(heads)), jnp.int32(rows))
    visible, blocks = [], []
    for table, cache in zip(tables, (own, other)):
        scores = jnp.dot(query, cache[...], preferred_element_type=jnp.float32) * scale
        for page in range(cache.shape[1] // PAGE):
            owner, filled = table[2 * page : 2 * page + 1], table[2 * page + 1 : 2 * page + 2]
            visible.append((row_of == owner) & (lane < filled))
            blocks.append(scores[:, page * PAGE : (page + 1) * PAGE])
    top = jnp.full(shape, NEG_BIG, jnp.float32)
    for seen, block in zip(visible, blocks):
        top = jnp.maximum(top, jnp.where(seen, block, NEG_BIG))
    chip_max = jnp.max(top, axis=1, keepdims=True)
    weights = [
        jnp.where(seen, jnp.exp(block - chip_max), 0.0) for seen, block in zip(visible, blocks)
    ]
    total = jnp.sum(functools.reduce(jnp.add, weights), axis=1, keepdims=True)
    latent = jnp.zeros((query.shape[0], LAT), jnp.float32)
    pages = own.shape[1] // PAGE
    for side, cache in enumerate((own, other)):
        low = jnp.concatenate(weights[side * pages : (side + 1) * pages], axis=1)
        latent += lax.dot_general(
            low.astype(jnp.bfloat16),
            cache[:LAT, :],
            (((1,), (1,)), ((), ())),
            preferred_element_type=jnp.float32,
        )
    lines = rows * heads
    stats = stats_tile(chip_max, total)
    latent = latent.astype(jnp.bfloat16)
    chip = lax.div(lax.axis_index("ctx"), 2)
    for at, mask in enumerate(masks):
        target = at if before is None else chip ^ mask
        message[target, :, :LAT] = latent[at * lines : (at + 1) * lines]
        message[target, :, LAT:] = stats[at * lines : (at + 1) * lines]
    if before is not None:
        finished, finished_masks = before
        for at, mask in enumerate(finished_masks):
            message[chip ^ mask] = finished[at]


def near_kernel(rows, heads, masks, *refs):
    tables, queries, (own, other, message) = refs[:2], refs[2:-3], refs[-3:]
    attend_kernel(rows, heads, masks, tables, queries, own, other, None, message)


def far_kernel(rows, heads, masks, near_masks, *refs):
    tables, queries, (own, other, near, message) = refs[:2], refs[2:-4], refs[-4:]
    before = (near, near_masks)
    attend_kernel(rows, heads, masks, tables, queries, own, other, before, message)


def own_span(width_dev):
    index = lax.axis_index("ctx")
    span = math.lcm(width_dev, LANES)
    start = pl.multiple_of(lax.div(index, span // width_dev) * span, LANES)
    return (start, span, lax.rem(index, span // width_dev))


def project(flat, out_proj, start, target):
    step = math.gcd(target.shape[1], COLUMN_BLOCK)
    for at in range(0, target.shape[1], step):
        columns = pl.ds(pl.multiple_of(start + at, LANES), step)
        terms = jnp.dot(flat, out_proj[:, columns], preferred_element_type=jnp.float32)
        target[:, at : at + step] = terms


def add_residual(hidden, wanted, target):
    rows, width_dev = hidden.shape
    half = target.shape[1]
    start, span, place = own_span(width_dev)

    @pl.when(lax.div(start, half) == wanted)
    def _():
        own = hidden[...].astype(jnp.float32)
        residual = jnp.zeros((rows, span), jnp.float32)
        for at in range(span // width_dev):
            before, after = at * width_dev, span - (at + 1) * width_dev
            pieces = [jnp.zeros((rows, before), jnp.float32)] * (before > 0) + [own]
            pieces += [jnp.zeros((rows, after), jnp.float32)] * (after > 0)
            residual = jnp.where(place == at, jnp.concatenate(pieces, axis=1), residual)
        target[:, pl.ds(pl.multiple_of(lax.rem(start, half), LANES), span)] += residual


def heads_kernel(rows, heads, parts, absorb, out_proj, hidden, send, flat_out, latent_buf):
    chips = parts.shape[0]
    stats = [from_stats(parts[chip, :, LAT:]) for chip in range(chips)]
    joint = functools.reduce(jnp.maximum, [shard_max for shard_max, _ in stats])
    total = jnp.zeros_like(joint)
    latent = jnp.zeros((rows * heads, LAT), jnp.float32)
    for chip, (shard_max, part_total) in enumerate(stats):
        factor = jnp.exp(shard_max - joint)
        total += part_total * factor
        latent += parts[chip, :, :LAT].astype(jnp.float32) * factor
    latent = latent / total
    tiles = range(LAT // LANES)
    for tile in tiles:
        latent_buf[tile] = latent[:, tile * LANES : (tile + 1) * LANES]
    value_heads = []
    for head in range(heads):
        lines = pl.ds(head, rows, stride=heads)
        own = jnp.concatenate([latent_buf[tile, lines, :] for tile in tiles], axis=1)
        own = own.astype(jnp.bfloat16)
        value_heads.append(jnp.dot(own, absorb[head], preferred_element_type=jnp.float32))
    flat = jnp.concatenate(value_heads, axis=1).astype(jnp.bfloat16)
    flat_out[...] = flat
    other_core = 1 - lax.rem(lax.axis_index("ctx"), 2)
    project(flat, out_proj, other_core * send.shape[1], send)
    add_residual(hidden, other_core, send)


def keep_kernel(flat, out_proj, hidden, keep):
    core = lax.rem(lax.axis_index("ctx"), 2)
    project(flat[...], out_proj, core * keep.shape[1], keep)
    add_residual(hidden, core, keep)


def expand(side, start, gain, gate, up):
    rows, half = side.shape
    units = gate.shape[0]
    step = math.gcd(half, COLUMN_BLOCK)
    both = jnp.zeros((rows, 2 * units), jnp.float32)
    for at in range(0, half, step):
        columns = pl.ds(pl.multiple_of(start + at, LANES), step)
        scaled = (side[:, at : at + step] * gain[:, columns]).astype(jnp.bfloat16)
        both += lax.dot_general(
            scaled,
            jnp.concatenate([gate[:, columns], up[:, columns]], axis=0),
            (((1,), (1,)), ((), ())),
            preferred_element_type=jnp.float32,
        )
    return both


def own_half_kernel(mine, gain, gate, up, both):
    core = lax.rem(lax.axis_index("ctx"), 2)
    both[...] = expand(mine, core * mine.shape[1], gain, gate, up)


def ffn_kernel(mine, other, both, gain, gate, up, down, blocks, stream_own):
    rows, half = mine.shape
    width, units = 2 * half, gate.shape[0]
    core = lax.rem(lax.axis_index("ctx"), 2)
    square = jnp.sum(mine[...] * mine[...], axis=1, keepdims=True)
    square += jnp.sum(other[...] * other[...], axis=1, keepdims=True)
    norm_scale = lax.rsqrt(square / width + EPS)
    acts = (both[...] + expand(other, (1 - core) * half, gain, gate, up)) * norm_scale
    gate_act, up_act = acts[:, :units], acts[:, units:]
    activated = (gate_act / (1.0 + jnp.exp(-gate_act)) * up_act).astype(jnp.bfloat16)
    count, _, width_dev = blocks.shape
    step = math.lcm(width_dev, LANES)
    for at in range(0, width, step):
        terms = jnp.dot(activated, down[:, at : at + step], preferred_element_type=jnp.float32)
        terms = terms.astype(jnp.bfloat16)
        for inner in range(0, step, width_dev):
            blocks[(at + inner) // width_dev] = terms[:, inner : inner + width_dev]
    start, span, place = own_span(width_dev)
    in_half = pl.ds(pl.multiple_of(lax.rem(start, half), LANES), span)
    near = jnp.where(lax.div(start, half) == core, mine[:, in_half], other[:, in_half])
    own = near[:, :width_dev]
    for at in range(1, span // width_dev):
        own = jnp.where(place == at, near[:, at * width_dev : (at + 1) * width_dev], own)
    stream_own[...] = own


def shards(
    queries,
    cache,
    page_row,
    page_index,
    lengths,
    hidden_in,
    norm_gain,
    absorb_value,
    out_proj,
    gate_proj,
    up_proj,
    down_proj,
):
    rows, heads, entry = queries.shape
    count = lax.axis_size("ctx")
    chips = count // 2
    width_dev = hidden_in.shape[1]
    width = out_proj.shape[1]
    half = width // 2
    lines = rows * heads
    group = chips * lines
    bf16, f32 = jnp.bfloat16, jnp.float32
    shaped = jax.ShapeDtypeStruct

    mark = call(first_kernel, shaped((8, LANES), f32), [], (), ahead=(cache, cache))
    queries, cache_sent, mark = lax.optimization_barrier((queries, cache, mark))
    cache_t = cache.T
    cache_other = swap(cache_sent.T)
    pages = page_row.shape[0]
    table = call(
        table_kernel,
        shaped((2 * pages, LANES), jnp.int32),
        [HBM] * 3 + [VMEM],
        (page_row, page_index, lengths, mark),
        scratch=[
            pltpu.SMEM((pages,), jnp.int32),
            pltpu.SMEM((pages,), jnp.int32),
            pltpu.SMEM((rows,), jnp.int32),
            pltpu.SemaphoreType.DMA((3,)),
        ],
    )
    tables = (table, swap(table))
    blocks = gather_blocks(queries.reshape(lines, entry))
    near_masks = [mask for mask in blocks if mask % 2 == 0]
    far_masks = [mask for mask in blocks if mask % 2 == 1]
    near = call(
        functools.partial(near_kernel, rows, heads, near_masks),
        shaped((len(near_masks), lines, LAT + LANES), bf16),
        [VMEM] * (len(near_masks) + 4),
        tables + tuple(blocks[mask] for mask in near_masks) + (cache_t, cache_other),
    )
    message = call(
        functools.partial(far_kernel, rows, heads, far_masks, near_masks),
        shaped((chips, lines, LAT + LANES), bf16),
        [VMEM] * (len(far_masks) + 5),
        tables + tuple(blocks[mask] for mask in far_masks) + (cache_t, cache_other, near),
        ahead=(absorb_value, out_proj),
    )
    parts = exchange(message)
    send, flat = call(
        functools.partial(heads_kernel, rows, heads),
        (shaped((rows, half), f32), shaped((rows, absorb_value.shape[0] * VHEAD), bf16)),
        [VMEM] * 4,
        (parts, absorb_value, out_proj, hidden_in),
        scratch=[pltpu.VMEM((LAT // LANES, lines, LANES), f32)],
        ahead=(gate_proj, up_proj, down_proj),
    )
    keep = call(
        keep_kernel, shaped((rows, half), f32), [VMEM] * 3, (flat, out_proj, hidden_in)
    )
    chip_terms = (keep + swap(send)).astype(bf16)
    mine = jnp.sum(spread(chip_terms).astype(f32), axis=0)
    other = swap(mine)
    weights = (norm_gain[None], gate_proj.T, up_proj.T)
    both = call(
        own_half_kernel,
        shaped((rows, 2 * gate_proj.shape[1]), f32),
        [VMEM] * 4,
        (mine,) + weights,
    )
    blocks, stream_own = call(
        ffn_kernel,
        (shaped((count, rows, width_dev), bf16), shaped((rows, width_dev), f32)),
        [VMEM] * 7,
        (mine, other, both) + weights + (down_proj,),
    )
    received = lax.all_to_all(blocks, "ctx", 0, 0, tiled=True)
    return (stream_own + jnp.sum(received.astype(f32), axis=0)).astype(bf16)


def solution(mesh):
    in_specs = (
        P("groups", "ctx", None),
        P(("groups", "ctx"), None),
        P(("groups", "ctx")),
        P(("groups", "ctx")),
        P("groups"),
        P("groups", "ctx"),
        P(),
        P("ctx", None, None),
        P("ctx", None),
        P(None, "ctx"),
        P(None, "ctx"),
        P("ctx", None),
    )
    out_specs = P("groups", "ctx")
    return jax.shard_map(shards, mesh=mesh, in_specs=in_specs, out_specs=out_specs, check_vma=False)
```

time: 72.5 us -> 65.8 us (0.908)
  blocking collectives: 54.6 us -> 37.3 us
  starting transfers between devices: 0.27 us -> 12.6 us
  waiting for transfers between devices: 4.31 us -> 2.84 us
    all_to_all x3 -> x2, blocking collectives: 44.4 us -> 27.1 us  [exchange(): lax.all_to_all(value, 'ctx', 0, 0, tiled=True, axis_index_groups=core_gro...]
    ppermute x0 -> x7, starting transfers between devices: none -> 11.9 us  [gather_blocks(): lax.ppermute(held, 'ctx', pairs)]
    ppermute x4, waiting for transfers between devices: 4.31 us -> 0.14 us  [swap(): return lax.ppermute(value, 'ctx', [(i, i ^ 1) for i in range(count)])]
    ppermute x0 -> x7, waiting for transfers between devices: none -> 2.69 us  [gather_blocks(): lax.ppermute(held, 'ctx', pairs)]
    pallas_call x6 -> x8, Pallas kernels: 11.2 us -> 10.7 us  [call(): pl.pallas_call(kernel, out_shape=out_shape, in_specs=list(specs), out_spe...]
  transfers between devices with their start and end apart: 4 -> 11, of which waited for: 4 -> 4; matrix products, arithmetic and copies ran while one was open for 0% -> 0% of each run, Pallas kernels for 2% -> 7%
where the time goes in v3:
time: 65.8 us; the launch traced here: 65.6 us
  blocking collectives  37.3 us (57%)
  starting transfers between devices  12.6 us (19%)
  Pallas kernels  10.7 us (16%)
  waiting for transfers between devices  2.84 us (4%)
  local copies, waits for them, and re-layouts  1.18 us (2%)
  other arithmetic  0.85 us (1%)
    all_to_all x2, blocking collectives, exchange(): lax.all_to_all(value, 'ctx', 0, 0, tiled=True, axis_index_groups=core_gro...  27.1 us
    ppermute x7, starting transfers between devices, gather_blocks(): lax.ppermute(held, 'ctx', pairs)  11.9 us
    pallas_call x8, Pallas kernels, call(): pl.pallas_call(kernel, out_shape=out_shape, in_specs=list(specs), out_spe...  10.7 us
    all_to_all x1, blocking collectives, shards(): received = lax.all_to_all(blocks, 'ctx', 0, 0, tiled=True)  10.2 us
    ppermute x7, waiting for transfers between devices, gather_blocks(): lax.ppermute(held, 'ctx', pairs)  2.69 us
  transfers between devices with their start and end apart: 11, of which 4 were waited for; matrix products, arithmetic and copies ran while one was open for 0% of the time, Pallas kernels for 7%

profile of v3, /device:TPU:0, one launch (start us, length us, event | category | flops | bytes accessed | tf_op | source)
XLA Modules:
  0.0 65.6 jit_solution(13537408738592633629)
XLA Ops:
  0.0 1.0 %copy-done.4 = bf16[512,576]{0,1:T(8,128)(2,1)S(1)} copy-done((bf16[512,576]{0,1:T(8,128)(2,1)S(1)}, bf16[512,576]{0,1:T(8,128)(2,1)}, u32[]{:S(2)}) %copy-start.4) | copy-done | bytes 589848
  1.1 0.5 collective-permute-start.8
  1.6 0.0 copy-done.5
  1.6 3.6 %collective-permute-start.2 = (bf16[32,576]{1,0:T(8,128)(2,1)S(1)}, bf16[32,576]{1,0:T(8,128)(2,1)S(1)}, u32[]{:S(2)}, u32[]{:S(2)}) collective-permute-start(bf16[32,576]{1,0:T(8,128)(2,1)S(1)} %bitcast.15), channel_id=1, source_target_pairs={{0,8},{1,9},{2,10},{3,11},{4,12},{5,13},{6,14},{7,15},{8,0},{9,1},... | collective-permute-start | bytes 110600 | tf_op jit(solution)/shard_map/ppermute | solution.py:44
  5.1 1.6 %collective-permute-start.4 = (bf16[32,576]{1,0:T(8,128)(2,1)S(1)}, bf16[32,576]{1,0:T(8,128)(2,1)S(1)}, u32[]{:S(2)}, u32[]{:S(2)}) collective-permute-start(bf16[32,576]{1,0:T(8,128)(2,1)S(1)} %bitcast.16), channel_id=1, source_target_pairs={{0,4},{1,5},{2,6},{3,7},{4,0},{5,1},{6,2},{7,3},{8,12},{9,13},{10,... | collective-permute-start | bytes 110600 | tf_op jit(solution)/shard_map/ppermute | solution.py:44
  6.7 0.7 %collective-permute-done.2.refs_3_ = bf16[32,576]{1,0:T(8,128)(2,1)S(1)} collective-permute-done((bf16[32,576]{1,0:T(8,128)(2,1)S(1)}, bf16[32,576]{1,0:T(8,128)(2,1)S(1)}, u32[]{:S(2)}, u32[]{:S(2)}) %collective-permute-start.2) | collective-permute-done | bytes 36896 | tf_op jit(solution)/shard_map/ppermute | solution.py:44
  7.4 2.1 %collective-permute-start.6 = (bf16[32,576]{1,0:T(8,128)(2,1)S(1)}, bf16[32,576]{1,0:T(8,128)(2,1)S(1)}, u32[]{:S(2)}, u32[]{:S(2)}) collective-permute-start(bf16[32,576]{1,0:T(8,128)(2,1)S(1)} %collective-permute-done.2.refs_3_), channel_id=1, source_target_pairs={{0,4},{1,5},{2,6},{3,7},{4,0},{5,1},{6,2},{7,3},{8,12},{9,13},{10,... | collective-permute-start | bytes 110600 | tf_op jit(solution)/shard_map/ppermute | solution.py:44
  9.4 0.0 copy-done.10
  9.4 0.0 copy-done.9
  9.4 0.0 copy-done.8
  9.4 0.6 shard_map.119.refs_0_
  10.0 0.1 collective-permute-start
  10.1 1.6 %collective-permute-start.1 = (bf16[32,576]{1,0:T(8,128)(2,1)S(1)}, bf16[32,576]{1,0:T(8,128)(2,1)S(1)}, u32[]{:S(2)}, u32[]{:S(2)}) collective-permute-start(bf16[32,576]{1,0:T(8,128)(2,1)S(1)} %bitcast.17), channel_id=1, source_target_pairs={{0,2},{1,3},{2,0},{3,1},{4,6},{5,7},{6,4},{7,5},{8,10},{9,11},{10,... | collective-permute-start | bytes 110600 | tf_op jit(solution)/shard_map/ppermute | solution.py:44
  11.7 0.0 collective-permute-done.refs_1_
  11.7 1.1 %collective-permute-start.3 = (bf16[32,576]{1,0:T(8,128)(2,1)S(1)}, bf16[32,576]{1,0:T(8,128)(2,1)S(1)}, u32[]{:S(2)}, u32[]{:S(2)}) collective-permute-start(bf16[32,576]{1,0:T(8,128)(2,1)S(1)} %collective-permute-done.2.refs_3_), channel_id=1, source_target_pairs={{0,2},{1,3},{2,0},{3,1},{4,6},{5,7},{6,4},{7,5},{8,10},{9,11},{10,... | collective-permute-start | bytes 110600 | tf_op jit(solution)/shard_map/ppermute | solution.py:44
  12.8 0.0 collective-permute-done.4.refs_4_
  12.8 0.9 %collective-permute-start.5 = (bf16[32,576]{1,0:T(8,128)(2,1)S(1)}, bf16[32,576]{1,0:T(8,128)(2,1)S(1)}, u32[]{:S(2)}, u32[]{:S(2)}) collective-permute-start(bf16[32,576]{1,0:T(8,128)(2,1)S(1)} %collective-permute-done.4.refs_4_), channel_id=1, source_target_pairs={{0,2},{1,3},{2,0},{3,1},{4,6},{5,7},{6,4},{7,5},{8,10},{9,11},{10,... | collective-permute-start | bytes 110600 | tf_op jit(solution)/shard_map/ppermute | solution.py:44
  13.7 0.0 collective-permute-done.6.refs_5_
  13.8 1.1 %collective-permute-start.7 = (bf16[32,576]{1,0:T(8,128)(2,1)S(1)}, bf16[32,576]{1,0:T(8,128)(2,1)S(1)}, u32[]{:S(2)}, u32[]{:S(2)}) collective-permute-start(bf16[32,576]{1,0:T(8,128)(2,1)S(1)} %collective-permute-done.6.refs_5_), channel_id=1, source_target_pairs={{0,2},{1,3},{2,0},{3,1},{4,6},{5,7},{6,4},{7,5},{8,10},{9,11},{10,... | collective-permute-start | bytes 110600 | tf_op jit(solution)/shard_map/ppermute | solution.py:44
  14.8 0.0 collective-permute-done.8.refs_7_
  14.8 0.9 %shard_map.120.refs_8_ = bf16[4,32,640]{2,1,0:T(8,128)(2,1)S(1)} custom-call(s32[8,128]{1,0:T(8,128)S(1)} %shard_map.119.refs_0_, s32[8,128]{1,0:T(8,128)S(1)} %collective-permute-done.refs_1_, bf16[32,576]{1,0:T(8,128)(2,1)S(1)} %bitcast.18, bf16[32,576]{1,0:T(8,128)(2,1)S(1)} %collective-permute-done.2.refs_3_, ...), custom_call_target="tpu_custom_call" | custom-call | bytes 1335296 | tf_op jit(solution)/shard_map/pallas_call | solution.py:61
  15.7 0.0 collective-permute-done.1.refs_2_
  15.7 1.3 %collective-permute-done.5.refs_4_ = bf16[32,576]{1,0:T(8,128)(2,1)S(1)} collective-permute-done((bf16[32,576]{1,0:T(8,128)(2,1)S(1)}, bf16[32,576]{1,0:T(8,128)(2,1)S(1)}, u32[]{:S(2)}, u32[]{:S(2)}) %collective-permute-start.5) | collective-permute-done | bytes 36896 | tf_op jit(solution)/shard_map/ppermute | solution.py:44
  17.0 0.0 collective-permute-done.3.refs_3_
  17.0 0.7 %collective-permute-done.7.refs_5_ = bf16[32,576]{1,0:T(8,128)(2,1)S(1)} collective-permute-done((bf16[32,576]{1,0:T(8,128)(2,1)S(1)}, bf16[32,576]{1,0:T(8,128)(2,1)S(1)}, u32[]{:S(2)}, u32[]{:S(2)}) %collective-permute-start.7) | collective-permute-done | bytes 36896 | tf_op jit(solution)/shard_map/ppermute | solution.py:44
  17.8 0.9 %shard_map.121 = bf16[8,32,640]{2,1,0:T(8,128)(2,1)S(1)} custom-call(s32[8,128]{1,0:T(8,128)S(1)} %shard_map.119.refs_0_, s32[8,128]{1,0:T(8,128)S(1)} %collective-permute-done.refs_1_, bf16[32,576]{1,0:T(8,128)(2,1)S(1)} %collective-permute-done.1.refs_2_, bf16[32,576]{1,0:T(8,128)(2,1)S(1)} %collective-permute-done.3.refs_3_, ...), custom_call_target="tpu_custom_call" | custom-call | flops 1572864000000 | bytes 1499136 | tf_op jit(solution)/shard_map/pallas_call | solution.py:61
  18.7 14.9 %all_to_all.15.parts = bf16[8,32,640]{2,1,0:T(8,128)(2,1)S(1)} all-to-all(bf16[8,32,640]{2,1,0:T(8,128)(2,1)S(1)} %shard_map.121), channel_id=1, replica_groups={{0,2,4,6,8,10,12,14},{1,3,5,7,9,11,13,15},{16,18,20,22,24,26,28,30},{17..., dimensions={0} | all-to-all | bytes 655360 | tf_op jit(solution)/shard_map/all_to_all | solution.py:50
  33.5 0.0 copy-done
  33.5 0.0 copy-done.3
  33.5 0.0 copy-done.7
  33.5 1.5 %shard_map.122 = (f32[4,3584]{1,0:T(4,128)S(1)}, bf16[4,1024]{1,0:T(4,128)(2,1)S(1)}) custom-call(bf16[8,32,640]{2,1,0:T(8,128)(2,1)S(1)} %all_to_all.15.parts, bf16[8,512,128]{2,1,0:T(8,128)(2,1)S(1)} %copy-done.3, bf16[1024,7168]{1,0:T(8,128)(2,1)S(1)} %copy-done, bf16[4,448]{1,0:T(4,128)(2,1)S(1)} %copy-done.7), custom_call_target="tpu_custom_call" | custom-call | flops 2477260800000 | bytes 16059904 | tf_op jit(solution)/shard_map/pallas_call | solution.py:61
  35.0 0.0 collective-permute-start.9
  35.0 0.0 copy-start.6
  35.1 0.0 slice-start
  35.1 1.1 %shard_map.123 = f32[4,3584]{1,0:T(4,128)S(1)} custom-call(bf16[4,1024]{1,0:T(4,128)(2,1)S(1)} %get-tuple-element.15.flat, bf16[1024,7168]{1,0:T(8,128)(2,1)S(1)} %copy-done, bf16[4,448]{1,0:T(4,128)(2,1)S(1)} %copy-done.7), custom_call_target="tpu_custom_call" | custom-call | bytes 14691840 | tf_op jit(solution)/shard_map/pallas_call | solution.py:61
  36.1 0.1 collective-permute-done.9
  36.3 0.1 broadcast_in_dim.4
  36.4 0.0 slice-start.1
  36.4 12.2 %all_to_all.16 = bf16[8,4,3584]{2,1,0:T(4,128)(2,1)S(1)} all-to-all(bf16[8,4,3584]{2,1,0:T(4,128)(2,1)S(1)} %broadcast_in_dim.4), channel_id=1, replica_groups={{0,2,4,6,8,10,12,14},{1,3,5,7,9,11,13,15},{16,18,20,22,24,26,28,30},{17..., dimensions={0} | all-to-all | bytes 458752 | tf_op jit(solution)/shard_map/all_to_all | solution.py:50
  48.6 0.2 convert_reduce_fusion.mine
  48.7 0.1 collective-permute-start.10
  48.8 0.0 copy-done.1
  48.9 2.2 %shard_map.124.both = f32[4,1152]{1,0:T(4,128)S(1)} custom-call(f32[4,3584]{1,0:T(4,128)S(1)} %convert_reduce_fusion.mine, f32[1,7168]{1,0:T(1,128)S(1)} %bitcast.19, bf16[576,7168]{1,0:T(8,128)(2,1)S(1)} %bitcast.6, bf16[576,7168]{1,0:T(8,128)(2,1)S(1)} %bitcast.8), custom_call_target="tpu_custom_call" | custom-call | bytes 16601088 | tf_op jit(solution)/shard_map/pallas_call | solution.py:61
  51.1 0.0 collective-permute-done.10.other
  51.1 0.0 slice-done.1
  51.1 3.6 %shard_map.125 = (bf16[16,4,448]{2,1,0:T(4,128)(2,1)S(1)}, f32[4,448]{1,0:T(4,128)S(1)}) custom-call(f32[4,3584]{1,0:T(4,128)S(1)} %convert_reduce_fusion.mine, f32[4,3584]{1,0:T(4,128)S(1)} %collective-permute-done.10.other, f32[4,1152]{1,0:T(4,128)S(1)} %shard_map.124.both, f32[1,7168]{1,0:T(1,128)S(1)} %bitcast.20, bf16[576,7168]{1,0:T(8,128)(2,1)S(1)} %bitcast.7, ...), custom_call_target="tpu_custom_call" | custom-call | bytes 24934400 | tf_op jit(solution)/shard_map/pallas_call | solution.py:61
  54.7 10.2 %all_to_all.17 = bf16[16,4,448]{2,1,0:T(4,128)(2,1)S(1)} all-to-all(bf16[16,4,448]{2,1,0:T(4,128)(2,1)S(1)} %get-tuple-element.18), channel_id=1, replica_groups=mesh['groups'=2,'ctx'=16] {'ctx'}, dimensions={0} | all-to-all | bytes 114688 | tf_op jit(solution)/shard_map/all_to_all | solution.py:375
  65.0 0.6 add_convert_fusion.1
  (17 shorter events, 0.1 us)
Async XLA Ops:
  0.0 1.1 %copy-start.4 = (bf16[512,576]{0,1:T(8,128)(2,1)S(1)}, bf16[512,576]{0,1:T(8,128)(2,1)}, u32[]{:S(2)}) copy-start(bf16[512,576]{0,1:T(8,128)(2,1)} %param.13) | copy-start | bytes 1769476
  0.0 1.6 %copy-start.5 = (bf16[4,8,576]{2,1,0:T(8,128)(2,1)S(1)}, bf16[4,8,576]{2,1,0:T(8,128)(2,1)}, u32[]{:S(2)}) copy-start(bf16[4,8,576]{2,1,0:T(8,128)(2,1)} %param.12) | copy-start | bytes 110596
  0.0 9.4 %copy-start.10 = (s32[4]{0:T(128)S(1)}, s32[4]{0:T(128)}, u32[]{:S(2)}) copy-start(s32[4]{0:T(128)} %lengths.1) | copy-start | bytes 52
  0.0 9.4 %copy-start.9 = (s32[4]{0:T(128)S(1)}, s32[4]{0:T(128)}, u32[]{:S(2)}) copy-start(s32[4]{0:T(128)} %page_index.1) | copy-start | bytes 52
  0.0 9.4 %copy-start.8 = (s32[4]{0:T(128)S(1)}, s32[4]{0:T(128)}, u32[]{:S(2)}) copy-start(s32[4]{0:T(128)} %page_row.1) | copy-start | bytes 52
  1.1 13.8 %collective-permute-start.8 = (bf16[576,512]{1,0:T(8,128)(2,1)S(1)}, bf16[576,512]{1,0:T(8,128)(2,1)S(1)}, u32[]{:S(2)}, u32[]{:S(2)}) collective-permute-start(bf16[576,512]{1,0:T(8,128)(2,1)S(1)} %bitcast.12), channel_id=1, source_target_pairs={{0,1},{1,0},{2,3},{3,2},{4,5},{5,4},{6,7},{7,6},{8,9},{9,8},{10,11... | collective-permute-start | bytes 1769480 | tf_op jit(solution)/shard_map/ppermute | solution.py:31
  1.6 5.8 %collective-permute-start.2 = (bf16[32,576]{1,0:T(8,128)(2,1)S(1)}, bf16[32,576]{1,0:T(8,128)(2,1)S(1)}, u32[]{:S(2)}, u32[]{:S(2)}) collective-permute-start(bf16[32,576]{1,0:T(8,128)(2,1)S(1)} %bitcast.15), channel_id=1, source_target_pairs={{0,8},{1,9},{2,10},{3,11},{4,12},{5,13},{6,14},{7,15},{8,0},{9,1},... | collective-permute-start | bytes 110600 | tf_op jit(solution)/shard_map/ppermute | solution.py:44
  5.1 7.7 %collective-permute-start.4 = (bf16[32,576]{1,0:T(8,128)(2,1)S(1)}, bf16[32,576]{1,0:T(8,128)(2,1)S(1)}, u32[]{:S(2)}, u32[]{:S(2)}) collective-permute-start(bf16[32,576]{1,0:T(8,128)(2,1)S(1)} %bitcast.16), channel_id=1, source_target_pairs={{0,4},{1,5},{2,6},{3,7},{4,0},{5,1},{6,2},{7,3},{8,12},{9,13},{10,... | collective-permute-start | bytes 110600 | tf_op jit(solution)/shard_map/ppermute | solution.py:44
  7.4 6.4 %collective-permute-start.6 = (bf16[32,576]{1,0:T(8,128)(2,1)S(1)}, bf16[32,576]{1,0:T(8,128)(2,1)S(1)}, u32[]{:S(2)}, u32[]{:S(2)}) collective-permute-start(bf16[32,576]{1,0:T(8,128)(2,1)S(1)} %collective-permute-done.2.refs_3_), channel_id=1, source_target_pairs={{0,4},{1,5},{2,6},{3,7},{4,0},{5,1},{6,2},{7,3},{8,12},{9,13},{10,... | collective-permute-start | bytes 110600 | tf_op jit(solution)/shard_map/ppermute | solution.py:44
  10.0 1.7 %collective-permute-start = (s32[8,128]{1,0:T(8,128)S(1)}, s32[8,128]{1,0:T(8,128)S(1)}, u32[]{:S(2)}, u32[]{:S(2)}) collective-permute-start(s32[8,128]{1,0:T(8,128)S(1)} %shard_map.119.refs_0_), channel_id=1, source_target_pairs={{0,1},{1,0},{2,3},{3,2},{4,5},{5,4},{6,7},{7,6},{8,9},{9,8},{10,11... | collective-permute-start | bytes 12296 | tf_op jit(solution)/shard_map/ppermute | solution.py:31
  10.1 5.6 %collective-permute-start.1 = (bf16[32,576]{1,0:T(8,128)(2,1)S(1)}, bf16[32,576]{1,0:T(8,128)(2,1)S(1)}, u32[]{:S(2)}, u32[]{:S(2)}) collective-permute-start(bf16[32,576]{1,0:T(8,128)(2,1)S(1)} %bitcast.17), channel_id=1, source_target_pairs={{0,2},{1,3},{2,0},{3,1},{4,6},{5,7},{6,4},{7,5},{8,10},{9,11},{10,... | collective-permute-start | bytes 110600 | tf_op jit(solution)/shard_map/ppermute | solution.py:44
  11.7 5.3 %collective-permute-start.3 = (bf16[32,576]{1,0:T(8,128)(2,1)S(1)}, bf16[32,576]{1,0:T(8,128)(2,1)S(1)}, u32[]{:S(2)}, u32[]{:S(2)}) collective-permute-start(bf16[32,576]{1,0:T(8,128)(2,1)S(1)} %collective-permute-done.2.refs_3_), channel_id=1, source_target_pairs={{0,2},{1,3},{2,0},{3,1},{4,6},{5,7},{6,4},{7,5},{8,10},{9,11},{10,... | collective-permute-start | bytes 110600 | tf_op jit(solution)/shard_map/ppermute | solution.py:44
  12.8 4.2 %collective-permute-start.5 = (bf16[32,576]{1,0:T(8,128)(2,1)S(1)}, bf16[32,576]{1,0:T(8,128)(2,1)S(1)}, u32[]{:S(2)}, u32[]{:S(2)}) collective-permute-start(bf16[32,576]{1,0:T(8,128)(2,1)S(1)} %collective-permute-done.4.refs_4_), channel_id=1, source_target_pairs={{0,2},{1,3},{2,0},{3,1},{4,6},{5,7},{6,4},{7,5},{8,10},{9,11},{10,... | collective-permute-start | bytes 110600 | tf_op jit(solution)/shard_map/ppermute | solution.py:44
  13.8 4.0 %collective-permute-start.7 = (bf16[32,576]{1,0:T(8,128)(2,1)S(1)}, bf16[32,576]{1,0:T(8,128)(2,1)S(1)}, u32[]{:S(2)}, u32[]{:S(2)}) collective-permute-start(bf16[32,576]{1,0:T(8,128)(2,1)S(1)} %collective-permute-done.6.refs_5_), channel_id=1, source_target_pairs={{0,2},{1,3},{2,0},{3,1},{4,6},{5,7},{6,4},{7,5},{8,10},{9,11},{10,... | collective-permute-start | bytes 110600 | tf_op jit(solution)/shard_map/ppermute | solution.py:44
  17.8 15.8 %copy-start = (bf16[1024,7168]{1,0:T(8,128)(2,1)S(1)}, bf16[1024,7168]{1,0:T(8,128)(2,1)}, u32[]{:S(2)}) copy-start(bf16[1024,7168]{1,0:T(8,128)(2,1)} %out_proj.3) | copy-start | bytes 44040196
  17.8 15.8 %copy-start.3 = (bf16[8,512,128]{2,1,0:T(8,128)(2,1)S(1)}, bf16[8,512,128]{2,1,0:T(8,128)(2,1)}, u32[]{:S(2)}) copy-start(bf16[8,512,128]{2,1,0:T(8,128)(2,1)} %absorb.1) | copy-start | bytes 3145732
  17.8 15.8 %copy-start.7 = (bf16[4,448]{1,0:T(4,128)(2,1)S(1)}, bf16[4,448]{1,0:T(4,128)(2,1)}, u32[]{:S(2)}) copy-start(bf16[4,448]{1,0:T(4,128)(2,1)} %hidden.3) | copy-start | bytes 10756
  35.0 1.2 %collective-permute-start.9 = (f32[4,3584]{1,0:T(4,128)S(1)}, f32[4,3584]{1,0:T(4,128)S(1)}, u32[]{:S(2)}, u32[]{:S(2)}) collective-permute-start(f32[4,3584]{1,0:T(4,128)S(1)} %get-tuple-element.16), channel_id=1, source_target_pairs={{0,1},{1,0},{2,3},{3,2},{4,5},{5,4},{6,7},{7,6},{8,9},{9,8},{10,11... | collective-permute-start | bytes 172040 | tf_op jit(solution)/shard_map/ppermute | solution.py:31
  35.0 13.8 %copy-start.1 = (bf16[7168,576]{0,1:T(8,128)(2,1)S(1)}, bf16[7168,576]{0,1:T(8,128)(2,1)}, u32[]{:S(2)}) copy-start(bf16[7168,576]{0,1:T(8,128)(2,1)} %param.21) | copy-start | bytes 24772612
  35.0 13.8 %copy-start.2 = (bf16[7168,576]{0,1:T(8,128)(2,1)S(1)}, bf16[7168,576]{0,1:T(8,128)(2,1)}, u32[]{:S(2)}) copy-start(bf16[7168,576]{0,1:T(8,128)(2,1)} %param.22) | copy-start | bytes 24772612
  35.0 13.8 %copy-start.6 = (f32[7168]{0:T(1024)S(1)}, f32[7168]{0:T(1024)}, u32[]{:S(2)}) copy-start(f32[7168]{0:T(1024)} %param.18) | copy-start | bytes 86020
  35.1 16.1 %slice-start = ((s8[8257536]{0:T(1024)(128)(4,1)}), s8[4194304]{0:T(1024)(128)(4,1)S(1)}, s32[]{:S(2)}) async-start(s8[8257536]{0:T(1024)(128)(4,1)} %bitcast.10), calls=%async_computation.3 | async-start | bytes 8388608
  36.4 14.8 %slice-start.1 = ((s8[8257536]{0:T(1024)(128)(4,1)}), s8[4063232]{0:T(1024)(128)(4,1)S(1)}, s32[]{:S(2)}) async-start(s8[8257536]{0:T(1024)(128)(4,1)} %bitcast.10), calls=%async_computation.4 | async-start | bytes 8126464
  48.7 2.4 %collective-permute-start.10 = (f32[4,3584]{1,0:T(4,128)S(1)}, f32[4,3584]{1,0:T(4,128)S(1)}, u32[]{:S(2)}, u32[]{:S(2)}) collective-permute-start(f32[4,3584]{1,0:T(4,128)S(1)} %convert_reduce_fusion.mine), channel_id=1, source_target_pairs={{0,1},{1,0},{2,3},{3,2},{4,5},{5,4},{6,7},{7,6},{8,9},{9,8},{10,11... | collective-permute-start | bytes 172040 | tf_op jit(solution)/shard_map/ppermute | solution.py:31

commit v4 on v3

--- a/solution.py
+++ b/solution.py
@@ -36,14 +36,19 @@
     return [list(range(core, count, 2)) for core in range(2)]
 
 
-def gather_blocks(block):
+def gather_blocks(block, mark):
     count = lax.axis_size("ctx")
     blocks, mask = {0: block}, count // 4
     while mask:
         pairs = [(i, i ^ (2 * mask)) for i in range(count)]
-        blocks |= {mask | at: lax.ppermute(held, "ctx", pairs) for at, held in blocks.items()}
+        arrived = {}
+        for at, held in blocks.items():
+            arrived[mask | at] = lax.ppermute(held, "ctx", pairs)
+        blocks |= arrived
+        if len(blocks) == 2:
+            blocks[mask], mark = lax.optimization_barrier((blocks[mask], mark))
         mask //= 2
-    return blocks
+    return blocks, mark
 
 
 def exchange(value):
@@ -55,9 +60,9 @@
     return exchange(jnp.broadcast_to(value[None], (chips,) + value.shape))
 
 
-def call(kernel, out_shape, specs, operands, scratch=(), ahead=()):
+def call(kernel, out_shape, specs, operands, scratch=(), ahead=(), scale=1.0):
     bytes_of = [x.size * x.dtype.itemsize for x in operands]
-    flops = HINT_FLOPS * sum(x.size * x.dtype.itemsize for x in ahead)
+    flops = HINT_FLOPS * scale * sum(x.size * x.dtype.itemsize for x in ahead)
     return pl.pallas_call(
         kernel,
         out_shape=out_shape,
@@ -65,7 +70,7 @@
         out_specs=jax.tree.map(lambda _: VMEM, out_shape),
         scratch_shapes=list(scratch),
         cost_estimate=pl.CostEstimate(
-            flops=flops, bytes_accessed=sum(bytes_of), transcendentals=HINT_TRANSCENDENTALS
+            flops=int(flops), bytes_accessed=sum(bytes_of), transcendentals=int(HINT_TRANSCENDENTALS * scale)
         ),
         compiler_params=pltpu.CompilerParams(vmem_limit_bytes=KERNEL_VMEM),
     )(*operands)
@@ -260,7 +265,7 @@
 
 
 def ffn_kernel(mine, other, both, gain, gate, up, down, blocks, stream_own):
-    rows, half = mine.shape
+    _, half = mine.shape
     width, units = 2 * half, gate.shape[0]
     core = lax.rem(lax.axis_index("ctx"), 2)
     square = jnp.sum(mine[...] * mine[...], axis=1, keepdims=True)
@@ -269,7 +274,7 @@
     acts = (both[...] + expand(other, (1 - core) * half, gain, gate, up)) * norm_scale
     gate_act, up_act = acts[:, :units], acts[:, units:]
     activated = (gate_act / (1.0 + jnp.exp(-gate_act)) * up_act).astype(jnp.bfloat16)
-    count, _, width_dev = blocks.shape
+    _, _, width_dev = blocks.shape
     step = math.lcm(width_dev, LANES)
     for at in range(0, width, step):
         terms = jnp.dot(activated, down[:, at : at + step], preferred_element_type=jnp.float32)
@@ -306,12 +311,12 @@
     width = out_proj.shape[1]
     half = width // 2
     lines = rows * heads
-    group = chips * lines
     bf16, f32 = jnp.bfloat16, jnp.float32
     shaped = jax.ShapeDtypeStruct
 
-    mark = call(first_kernel, shaped((8, LANES), f32), [], (), ahead=(cache, cache))
-    queries, cache_sent, mark = lax.optimization_barrier((queries, cache, mark))
+    mark = call(first_kernel, shaped((8, LANES), f32), [], (), ahead=(cache, cache), scale=0.1)
+    blocks, mark = gather_blocks(queries.reshape(lines, entry), mark)
+    cache_sent, mark = lax.optimization_barrier((cache, mark))
     cache_t = cache.T
     cache_other = swap(cache_sent.T)
     pages = page_row.shape[0]
@@ -328,7 +333,6 @@
         ],
     )
     tables = (table, swap(table))
-    blocks = gather_blocks(queries.reshape(lines, entry))
     near_masks = [mask for mask in blocks if mask % 2 == 0]
     far_masks = [mask for mask in blocks if mask % 2 == 1]
     near = call(

time: 65.8 us -> 65.8 us (level)
  waiting for transfers between devices: 2.84 us -> 4.67 us
  starting transfers between devices: 12.6 us -> 11.4 us
  local copies, waits for them, and re-layouts: 1.18 us -> 0.14 us
    ppermute x7, waiting for transfers between devices: 2.69 us -> 4.53 us  [gather_blocks(): arrived[mask | at] = lax.ppermute(held, 'ctx', pairs)]
    unnamed x26, local copies, waits for them, and re-layouts: 1.11 us -> 0.08 us
where the time goes in v4:
time: 65.8 us; the launch traced here: 65.5 us
  blocking collectives  37.6 us (57%)
  starting transfers between devices  11.4 us (17%)
  Pallas kernels  10.7 us (16%)
  waiting for transfers between devices  4.67 us (7%)
  other arithmetic  0.85 us (1%)
    all_to_all x2, blocking collectives, exchange(): lax.all_to_all(value, 'ctx', 0, 0, tiled=True, axis_index_groups=core_gro...  27.3 us
    ppermute x7, starting transfers between devices, gather_blocks(): arrived[mask | at] = lax.ppermute(held, 'ctx', pairs)  11.3 us
    pallas_call x8, Pallas kernels, call(): pl.pallas_call(kernel, out_shape=out_shape, in_specs=list(specs), out_spe...  10.7 us
    all_to_all x1, blocking collectives, shards(): received = lax.all_to_all(blocks, 'ctx', 0, 0, tiled=True)  10.2 us
    ppermute x7, waiting for transfers between devices, gather_blocks(): arrived[mask | at] = lax.ppermute(held, 'ctx', pairs)  4.53 us
  transfers between devices with their start and end apart: 11, of which 4 were waited for; matrix products, arithmetic and copies ran while one was open for 0% of the time, Pallas kernels for 7%

profile of v4, /device:TPU:0, one launch (start us, length us, event | category | flops | bytes accessed | tf_op | source)
XLA Modules:
  0.0 65.5 jit_solution(6563124243699137488)
XLA Ops:
  0.0 4.1 %collective-permute-start = (bf16[32,576]{1,0:T(8,128)(2,1)}, bf16[32,576]{1,0:T(8,128)(2,1)S(1)}, u32[]{:S(2)}, u32[]{:S(2)}) collective-permute-start(bf16[32,576]{1,0:T(8,128)(2,1)} %bitcast.15), channel_id=1, source_target_pairs={{0,8},{1,9},{2,10},{3,11},{4,12},{5,13},{6,14},{7,15},{8,0},{9,1},... | collective-permute-start | bytes 110600 | tf_op jit(solution)/shard_map/ppermute | solution.py:46
  4.2 2.6 %collective-permute-done.refs_3_ = bf16[32,576]{1,0:T(8,128)(2,1)S(1)} collective-permute-done((bf16[32,576]{1,0:T(8,128)(2,1)}, bf16[32,576]{1,0:T(8,128)(2,1)S(1)}, u32[]{:S(2)}, u32[]{:S(2)}) %collective-permute-start) | collective-permute-done | bytes 36896 | tf_op jit(solution)/shard_map/ppermute | solution.py:46
  6.8 0.0 copy-done.4
  6.8 0.0 collective-permute-start.8
  6.8 0.0 copy-done.5
  6.8 1.5 %collective-permute-start.4 = (bf16[32,576]{1,0:T(8,128)(2,1)S(1)}, bf16[32,576]{1,0:T(8,128)(2,1)S(1)}, u32[]{:S(2)}, u32[]{:S(2)}) collective-permute-start(bf16[32,576]{1,0:T(8,128)(2,1)S(1)} %bitcast.16), channel_id=1, source_target_pairs={{0,4},{1,5},{2,6},{3,7},{4,0},{5,1},{6,2},{7,3},{8,12},{9,13},{10,... | collective-permute-start | bytes 110600 | tf_op jit(solution)/shard_map/ppermute | solution.py:46
  8.3 0.6 collective-permute-start.6
  8.9 0.0 copy-done.8
  8.9 0.0 copy-done.9
  8.9 0.0 copy-done.10
  8.9 0.6 shard_map.119.refs_0_
  9.5 0.1 collective-permute-start.1
  9.6 1.8 %collective-permute-start.2 = (bf16[32,576]{1,0:T(8,128)(2,1)S(1)}, bf16[32,576]{1,0:T(8,128)(2,1)S(1)}, u32[]{:S(2)}, u32[]{:S(2)}) collective-permute-start(bf16[32,576]{1,0:T(8,128)(2,1)S(1)} %bitcast.17), channel_id=1, source_target_pairs={{0,2},{1,3},{2,0},{3,1},{4,6},{5,7},{6,4},{7,5},{8,10},{9,11},{10,... | collective-permute-start | bytes 110600 | tf_op jit(solution)/shard_map/ppermute | solution.py:46
  11.4 0.0 collective-permute-done.4.refs_4_
  11.4 1.2 %collective-permute-start.3 = (bf16[32,576]{1,0:T(8,128)(2,1)S(1)}, bf16[32,576]{1,0:T(8,128)(2,1)S(1)}, u32[]{:S(2)}, u32[]{:S(2)}) collective-permute-start(bf16[32,576]{1,0:T(8,128)(2,1)S(1)} %collective-permute-done.refs_3_), channel_id=1, source_target_pairs={{0,2},{1,3},{2,0},{3,1},{4,6},{5,7},{6,4},{7,5},{8,10},{9,11},{10,... | collective-permute-start | bytes 110600 | tf_op jit(solution)/shard_map/ppermute | solution.py:46
  12.6 0.0 collective-permute-done.1.refs_1_
  12.6 0.8 %collective-permute-start.5 = (bf16[32,576]{1,0:T(8,128)(2,1)S(1)}, bf16[32,576]{1,0:T(8,128)(2,1)S(1)}, u32[]{:S(2)}, u32[]{:S(2)}) collective-permute-start(bf16[32,576]{1,0:T(8,128)(2,1)S(1)} %collective-permute-done.4.refs_4_), channel_id=1, source_target_pairs={{0,2},{1,3},{2,0},{3,1},{4,6},{5,7},{6,4},{7,5},{8,10},{9,11},{10,... | collective-permute-start | bytes 110600 | tf_op jit(solution)/shard_map/ppermute | solution.py:46
  13.4 0.0 collective-permute-done.6.refs_5_
  13.4 1.2 %collective-permute-start.7 = (bf16[32,576]{1,0:T(8,128)(2,1)S(1)}, bf16[32,576]{1,0:T(8,128)(2,1)S(1)}, u32[]{:S(2)}, u32[]{:S(2)}) collective-permute-start(bf16[32,576]{1,0:T(8,128)(2,1)S(1)} %collective-permute-done.6.refs_5_), channel_id=1, source_target_pairs={{0,2},{1,3},{2,0},{3,1},{4,6},{5,7},{6,4},{7,5},{8,10},{9,11},{10,... | collective-permute-start | bytes 110600 | tf_op jit(solution)/shard_map/ppermute | solution.py:46
  14.6 0.0 collective-permute-done.8.refs_7_
  14.6 0.9 %shard_map.120.refs_8_ = bf16[4,32,640]{2,1,0:T(8,128)(2,1)S(1)} custom-call(s32[8,128]{1,0:T(8,128)S(1)} %shard_map.119.refs_0_, s32[8,128]{1,0:T(8,128)S(1)} %collective-permute-done.1.refs_1_, bf16[32,576]{1,0:T(8,128)(2,1)S(1)} %bitcast.18, bf16[32,576]{1,0:T(8,128)(2,1)S(1)} %collective-permute-done.refs_3_, ...), custom_call_target="tpu_custom_call" | custom-call | bytes 1335296 | tf_op jit(solution)/shard_map/pallas_call | solution.py:66
  15.5 0.0 collective-permute-done.2.refs_2_
  15.5 1.1 %collective-permute-done.5.refs_4_ = bf16[32,576]{1,0:T(8,128)(2,1)S(1)} collective-permute-done((bf16[32,576]{1,0:T(8,128)(2,1)S(1)}, bf16[32,576]{1,0:T(8,128)(2,1)S(1)}, u32[]{:S(2)}, u32[]{:S(2)}) %collective-permute-start.5) | collective-permute-done | bytes 36896 | tf_op jit(solution)/shard_map/ppermute | solution.py:46
  16.6 0.0 collective-permute-done.3.refs_3_
  16.6 0.8 %collective-permute-done.7.refs_5_ = bf16[32,576]{1,0:T(8,128)(2,1)S(1)} collective-permute-done((bf16[32,576]{1,0:T(8,128)(2,1)S(1)}, bf16[32,576]{1,0:T(8,128)(2,1)S(1)}, u32[]{:S(2)}, u32[]{:S(2)}) %collective-permute-start.7) | collective-permute-done | bytes 36896 | tf_op jit(solution)/shard_map/ppermute | solution.py:46
  17.4 0.9 %shard_map.121 = bf16[8,32,640]{2,1,0:T(8,128)(2,1)S(1)} custom-call(s32[8,128]{1,0:T(8,128)S(1)} %shard_map.119.refs_0_, s32[8,128]{1,0:T(8,128)S(1)} %collective-permute-done.1.refs_1_, bf16[32,576]{1,0:T(8,128)(2,1)S(1)} %collective-permute-done.2.refs_2_, bf16[32,576]{1,0:T(8,128)(2,1)S(1)} %collective-permute-done.3.refs_3_, ...), custom_call_target="tpu_custom_call" | custom-call | flops 1572864000000 | bytes 1499136 | tf_op jit(solution)/shard_map/pallas_call | solution.py:66
  18.3 15.1 %all_to_all.15.parts = bf16[8,32,640]{2,1,0:T(8,128)(2,1)S(1)} all-to-all(bf16[8,32,640]{2,1,0:T(8,128)(2,1)S(1)} %shard_map.121), channel_id=1, replica_groups={{0,2,4,6,8,10,12,14},{1,3,5,7,9,11,13,15},{16,18,20,22,24,26,28,30},{17..., dimensions={0} | all-to-all | bytes 655360 | tf_op jit(solution)/shard_map/all_to_all | solution.py:55
  33.5 0.0 copy-done
  33.5 0.0 copy-done.3
  33.5 0.0 copy-done.7
  33.5 1.5 %shard_map.122 = (f32[4,3584]{1,0:T(4,128)S(1)}, bf16[4,1024]{1,0:T(4,128)(2,1)S(1)}) custom-call(bf16[8,32,640]{2,1,0:T(8,128)(2,1)S(1)} %all_to_all.15.parts, bf16[8,512,128]{2,1,0:T(8,128)(2,1)S(1)} %copy-done.3, bf16[1024,7168]{1,0:T(8,128)(2,1)S(1)} %copy-done, bf16[4,448]{1,0:T(4,128)(2,1)S(1)} %copy-done.7), custom_call_target="tpu_custom_call" | custom-call | flops 2477260800000 | bytes 16059904 | tf_op jit(solution)/shard_map/pallas_call | solution.py:66
  35.0 0.0 collective-permute-start.9
  35.0 0.0 copy-start.6
  35.0 0.0 slice-start
  35.0 1.1 %shard_map.123 = f32[4,3584]{1,0:T(4,128)S(1)} custom-call(bf16[4,1024]{1,0:T(4,128)(2,1)S(1)} %get-tuple-element.17.flat, bf16[1024,7168]{1,0:T(8,128)(2,1)S(1)} %copy-done, bf16[4,448]{1,0:T(4,128)(2,1)S(1)} %copy-done.7), custom_call_target="tpu_custom_call" | custom-call | bytes 14691840 | tf_op jit(solution)/shard_map/pallas_call | solution.py:66
  36.1 0.1 collective-permute-done.9
  36.2 0.1 broadcast_in_dim.4
  36.3 0.0 slice-start.1
  36.3 12.2 %all_to_all.16 = bf16[8,4,3584]{2,1,0:T(4,128)(2,1)S(1)} all-to-all(bf16[8,4,3584]{2,1,0:T(4,128)(2,1)S(1)} %broadcast_in_dim.4), channel_id=1, replica_groups={{0,2,4,6,8,10,12,14},{1,3,5,7,9,11,13,15},{16,18,20,22,24,26,28,30},{17..., dimensions={0} | all-to-all | bytes 458752 | tf_op jit(solution)/shard_map/all_to_all | solution.py:55
  48.5 0.2 convert_reduce_fusion.mine
  48.7 0.1 collective-permute-start.10
  48.8 0.0 copy-done.1
  48.8 2.2 %shard_map.124.both = f32[4,1152]{1,0:T(4,128)S(1)} custom-call(f32[4,3584]{1,0:T(4,128)S(1)} %convert_reduce_fusion.mine, f32[1,7168]{1,0:T(1,128)S(1)} %bitcast.19, bf16[576,7168]{1,0:T(8,128)(2,1)S(1)} %bitcast.6, bf16[576,7168]{1,0:T(8,128)(2,1)S(1)} %bitcast.8), custom_call_target="tpu_custom_call" | custom-call | bytes 16601088 | tf_op jit(solution)/shard_map/pallas_call | solution.py:66
  51.0 0.0 collective-permute-done.10.other
  51.0 0.0 slice-done.1
  51.1 3.6 %shard_map.125 = (bf16[16,4,448]{2,1,0:T(4,128)(2,1)S(1)}, f32[4,448]{1,0:T(4,128)S(1)}) custom-call(f32[4,3584]{1,0:T(4,128)S(1)} %convert_reduce_fusion.mine, f32[4,3584]{1,0:T(4,128)S(1)} %collective-permute-done.10.other, f32[4,1152]{1,0:T(4,128)S(1)} %shard_map.124.both, f32[1,7168]{1,0:T(1,128)S(1)} %bitcast.20, bf16[576,7168]{1,0:T(8,128)(2,1)S(1)} %bitcast.7, ...), custom_call_target="tpu_custom_call" | custom-call | bytes 24934400 | tf_op jit(solution)/shard_map/pallas_call | solution.py:66
  54.6 10.2 %all_to_all.17 = bf16[16,4,448]{2,1,0:T(4,128)(2,1)S(1)} all-to-all(bf16[16,4,448]{2,1,0:T(4,128)(2,1)S(1)} %get-tuple-element.20), channel_id=1, replica_groups=mesh['groups'=2,'ctx'=16] {'ctx'}, dimensions={0} | all-to-all | bytes 114688 | tf_op jit(solution)/shard_map/all_to_all | solution.py:379
  64.9 0.6 add_convert_fusion.1
  (17 shorter events, 0.1 us)
Async XLA Ops:
  0.0 6.8 %copy-start.4 = (bf16[512,576]{0,1:T(8,128)(2,1)S(1)}, bf16[512,576]{0,1:T(8,128)(2,1)}, u32[]{:S(2)}) copy-start(bf16[512,576]{0,1:T(8,128)(2,1)} %param.13) | copy-start | bytes 1769476
  0.0 6.8 %copy-start.5 = (bf16[4,8,576]{2,1,0:T(8,128)(2,1)S(1)}, bf16[4,8,576]{2,1,0:T(8,128)(2,1)}, u32[]{:S(2)}) copy-start(bf16[4,8,576]{2,1,0:T(8,128)(2,1)} %param.12) | copy-start | bytes 110596
  0.0 8.9 %copy-start.8 = (s32[4]{0:T(128)S(1)}, s32[4]{0:T(128)}, u32[]{:S(2)}) copy-start(s32[4]{0:T(128)} %page_row.1) | copy-start | bytes 52
  0.0 8.9 %copy-start.9 = (s32[4]{0:T(128)S(1)}, s32[4]{0:T(128)}, u32[]{:S(2)}) copy-start(s32[4]{0:T(128)} %page_index.1) | copy-start | bytes 52
  0.0 8.9 %copy-start.10 = (s32[4]{0:T(128)S(1)}, s32[4]{0:T(128)}, u32[]{:S(2)}) copy-start(s32[4]{0:T(128)} %lengths.1) | copy-start | bytes 52
  0.0 6.8 %collective-permute-start = (bf16[32,576]{1,0:T(8,128)(2,1)}, bf16[32,576]{1,0:T(8,128)(2,1)S(1)}, u32[]{:S(2)}, u32[]{:S(2)}) collective-permute-start(bf16[32,576]{1,0:T(8,128)(2,1)} %bitcast.15), channel_id=1, source_target_pairs={{0,8},{1,9},{2,10},{3,11},{4,12},{5,13},{6,14},{7,15},{8,0},{9,1},... | collective-permute-start | bytes 110600 | tf_op jit(solution)/shard_map/ppermute | solution.py:46
  6.8 7.8 %collective-permute-start.8 = (bf16[576,512]{1,0:T(8,128)(2,1)S(1)}, bf16[576,512]{1,0:T(8,128)(2,1)S(1)}, u32[]{:S(2)}, u32[]{:S(2)}) collective-permute-start(bf16[576,512]{1,0:T(8,128)(2,1)S(1)} %bitcast.12), channel_id=1, source_target_pairs={{0,1},{1,0},{2,3},{3,2},{4,5},{5,4},{6,7},{7,6},{8,9},{9,8},{10,11... | collective-permute-start | bytes 1769480 | tf_op jit(solution)/shard_map/ppermute | solution.py:31
  6.8 4.6 %collective-permute-start.4 = (bf16[32,576]{1,0:T(8,128)(2,1)S(1)}, bf16[32,576]{1,0:T(8,128)(2,1)S(1)}, u32[]{:S(2)}, u32[]{:S(2)}) collective-permute-start(bf16[32,576]{1,0:T(8,128)(2,1)S(1)} %bitcast.16), channel_id=1, source_target_pairs={{0,4},{1,5},{2,6},{3,7},{4,0},{5,1},{6,2},{7,3},{8,12},{9,13},{10,... | collective-permute-start | bytes 110600 | tf_op jit(solution)/shard_map/ppermute | solution.py:46
  8.3 5.1 %collective-permute-start.6 = (bf16[32,576]{1,0:T(8,128)(2,1)S(1)}, bf16[32,576]{1,0:T(8,128)(2,1)S(1)}, u32[]{:S(2)}, u32[]{:S(2)}) collective-permute-start(bf16[32,576]{1,0:T(8,128)(2,1)S(1)} %collective-permute-done.refs_3_), channel_id=1, source_target_pairs={{0,4},{1,5},{2,6},{3,7},{4,0},{5,1},{6,2},{7,3},{8,12},{9,13},{10,... | collective-permute-start | bytes 110600 | tf_op jit(solution)/shard_map/ppermute | solution.py:46
  9.5 3.1 %collective-permute-start.1 = (s32[8,128]{1,0:T(8,128)S(1)}, s32[8,128]{1,0:T(8,128)S(1)}, u32[]{:S(2)}, u32[]{:S(2)}) collective-permute-start(s32[8,128]{1,0:T(8,128)S(1)} %shard_map.119.refs_0_), channel_id=1, source_target_pairs={{0,1},{1,0},{2,3},{3,2},{4,5},{5,4},{6,7},{7,6},{8,9},{9,8},{10,11... | collective-permute-start | bytes 12296 | tf_op jit(solution)/shard_map/ppermute | solution.py:31
  9.6 5.9 %collective-permute-start.2 = (bf16[32,576]{1,0:T(8,128)(2,1)S(1)}, bf16[32,576]{1,0:T(8,128)(2,1)S(1)}, u32[]{:S(2)}, u32[]{:S(2)}) collective-permute-start(bf16[32,576]{1,0:T(8,128)(2,1)S(1)} %bitcast.17), channel_id=1, source_target_pairs={{0,2},{1,3},{2,0},{3,1},{4,6},{5,7},{6,4},{7,5},{8,10},{9,11},{10,... | collective-permute-start | bytes 110600 | tf_op jit(solution)/shard_map/ppermute | solution.py:46
  11.4 5.2 %collective-permute-start.3 = (bf16[32,576]{1,0:T(8,128)(2,1)S(1)}, bf16[32,576]{1,0:T(8,128)(2,1)S(1)}, u32[]{:S(2)}, u32[]{:S(2)}) collective-permute-start(bf16[32,576]{1,0:T(8,128)(2,1)S(1)} %collective-permute-done.refs_3_), channel_id=1, source_target_pairs={{0,2},{1,3},{2,0},{3,1},{4,6},{5,7},{6,4},{7,5},{8,10},{9,11},{10,... | collective-permute-start | bytes 110600 | tf_op jit(solution)/shard_map/ppermute | solution.py:46
  12.6 4.0 %collective-permute-start.5 = (bf16[32,576]{1,0:T(8,128)(2,1)S(1)}, bf16[32,576]{1,0:T(8,128)(2,1)S(1)}, u32[]{:S(2)}, u32[]{:S(2)}) collective-permute-start(bf16[32,576]{1,0:T(8,128)(2,1)S(1)} %collective-permute-done.4.refs_4_), channel_id=1, source_target_pairs={{0,2},{1,3},{2,0},{3,1},{4,6},{5,7},{6,4},{7,5},{8,10},{9,11},{10,... | collective-permute-start | bytes 110600 | tf_op jit(solution)/shard_map/ppermute | solution.py:46
  13.4 4.0 %collective-permute-start.7 = (bf16[32,576]{1,0:T(8,128)(2,1)S(1)}, bf16[32,576]{1,0:T(8,128)(2,1)S(1)}, u32[]{:S(2)}, u32[]{:S(2)}) collective-permute-start(bf16[32,576]{1,0:T(8,128)(2,1)S(1)} %collective-permute-done.6.refs_5_), channel_id=1, source_target_pairs={{0,2},{1,3},{2,0},{3,1},{4,6},{5,7},{6,4},{7,5},{8,10},{9,11},{10,... | collective-permute-start | bytes 110600 | tf_op jit(solution)/shard_map/ppermute | solution.py:46
  17.4 16.1 %copy-start = (bf16[1024,7168]{1,0:T(8,128)(2,1)S(1)}, bf16[1024,7168]{1,0:T(8,128)(2,1)}, u32[]{:S(2)}) copy-start(bf16[1024,7168]{1,0:T(8,128)(2,1)} %out_proj.3) | copy-start | bytes 44040196
  17.4 16.1 %copy-start.3 = (bf16[8,512,128]{2,1,0:T(8,128)(2,1)S(1)}, bf16[8,512,128]{2,1,0:T(8,128)(2,1)}, u32[]{:S(2)}) copy-start(bf16[8,512,128]{2,1,0:T(8,128)(2,1)} %absorb.1) | copy-start | bytes 3145732
  17.4 16.1 %copy-start.7 = (bf16[4,448]{1,0:T(4,128)(2,1)S(1)}, bf16[4,448]{1,0:T(4,128)(2,1)}, u32[]{:S(2)}) copy-start(bf16[4,448]{1,0:T(4,128)(2,1)} %hidden.3) | copy-start | bytes 10756
  35.0 1.2 %collective-permute-start.9 = (f32[4,3584]{1,0:T(4,128)S(1)}, f32[4,3584]{1,0:T(4,128)S(1)}, u32[]{:S(2)}, u32[]{:S(2)}) collective-permute-start(f32[4,3584]{1,0:T(4,128)S(1)} %get-tuple-element.18), channel_id=1, source_target_pairs={{0,1},{1,0},{2,3},{3,2},{4,5},{5,4},{6,7},{7,6},{8,9},{9,8},{10,11... | collective-permute-start | bytes 172040 | tf_op jit(solution)/shard_map/ppermute | solution.py:31
  35.0 13.8 %copy-start.1 = (bf16[7168,576]{0,1:T(8,128)(2,1)S(1)}, bf16[7168,576]{0,1:T(8,128)(2,1)}, u32[]{:S(2)}) copy-start(bf16[7168,576]{0,1:T(8,128)(2,1)} %param.21) | copy-start | bytes 24772612
  35.0 13.8 %copy-start.2 = (bf16[7168,576]{0,1:T(8,128)(2,1)S(1)}, bf16[7168,576]{0,1:T(8,128)(2,1)}, u32[]{:S(2)}) copy-start(bf16[7168,576]{0,1:T(8,128)(2,1)} %param.22) | copy-start | bytes 24772612
  35.0 13.8 %copy-start.6 = (f32[7168]{0:T(1024)S(1)}, f32[7168]{0:T(1024)}, u32[]{:S(2)}) copy-start(f32[7168]{0:T(1024)} %param.18) | copy-start | bytes 86020
  35.0 16.1 %slice-start = ((s8[8257536]{0:T(1024)(128)(4,1)}), s8[4194304]{0:T(1024)(128)(4,1)S(1)}, s32[]{:S(2)}) async-start(s8[8257536]{0:T(1024)(128)(4,1)} %bitcast.10), calls=%async_computation.3 | async-start | bytes 8388608
  36.3 14.8 %slice-start.1 = ((s8[8257536]{0:T(1024)(128)(4,1)}), s8[4063232]{0:T(1024)(128)(4,1)S(1)}, s32[]{:S(2)}) async-start(s8[8257536]{0:T(1024)(128)(4,1)} %bitcast.10), calls=%async_computation.4 | async-start | bytes 8126464
  48.7 2.4 %collective-permute-start.10 = (f32[4,3584]{1,0:T(4,128)S(1)}, f32[4,3584]{1,0:T(4,128)S(1)}, u32[]{:S(2)}, u32[]{:S(2)}) collective-permute-start(f32[4,3584]{1,0:T(4,128)S(1)} %convert_reduce_fusion.mine), channel_id=1, source_target_pairs={{0,1},{1,0},{2,3},{3,2},{4,5},{5,4},{6,7},{7,6},{8,9},{9,8},{10,11... | collective-permute-start | bytes 172040 | tf_op jit(solution)/shard_map/ppermute | solution.py:31

commit v5 on v4

--- a/solution.py
+++ b/solution.py
@@ -14,6 +14,7 @@
 PAGE = 128
 LANES = 128
 COLUMN_BLOCK = 1792
+STATS = 16
 KERNEL_VMEM = 12 << 20
 HINT_FLOPS = 100_000
 HINT_TRANSCENDENTALS = 100_000_000
@@ -23,7 +24,6 @@
 EPS = 1e-06
 
 VMEM = pl.BlockSpec(memory_space=pltpu.VMEM)
-HBM = pl.BlockSpec(memory_space=pltpu.HBM)
 
 
 def swap(value):
@@ -88,7 +88,7 @@
     tile = jnp.zeros(lane.shape, jnp.float32)
     for at, piece in enumerate(as_pieces(shard_max) + as_pieces(total)):
         tile = jnp.where(lane == at, piece, tile)
-    return tile.astype(jnp.bfloat16)
+    return tile
 
 
 def from_stats(tile):
@@ -102,22 +102,14 @@
     mark[...] = jnp.zeros_like(mark)
 
 
-def table_kernel(page_row, page_index, lengths, mark, table, *scratch):
-    held, arrived = scratch[:3], scratch[3]
-    copies = [
-        pltpu.make_async_copy(source, target, arrived.at[at])
-        for at, (source, target) in enumerate(zip((page_row, page_index, lengths), held))
-    ]
-    for copy in copies:
-        copy.start()
-    for copy in copies:
-        copy.wait()
-    rows_held, index_held, lengths_held = held
-    for page in range(page_row.shape[0]):
-        owner = rows_held[page]
-        filled = lengths_held[owner] - index_held[page] * PAGE
-        table[2 * page : 2 * page + 1] = jnp.full((1, LANES), owner, jnp.int32)
-        table[2 * page + 1 : 2 * page + 2] = jnp.full((1, LANES), filled, jnp.int32)
+def table_kernel(page_row, page_index, lengths, mark, table):
+    for page in range(page_row.shape[1]):
+        owner = page_row[:, page : page + 1]
+        filled = page_index[:, page : page + 1] * -PAGE
+        for row in range(lengths.shape[1]):
+            filled += jnp.where(owner == row, lengths[:, row : row + 1], 0)
+        table[2 * page : 2 * page + 1] = jnp.broadcast_to(owner, (1, LANES))
+        table[2 * page + 1 : 2 * page + 2] = jnp.broadcast_to(filled, (1, LANES))
 
 
 def attend_kernel(rows, heads, masks, tables, queries, own, other, before, message):
@@ -153,13 +145,16 @@
             preferred_element_type=jnp.float32,
         )
     lines = rows * heads
-    stats = stats_tile(chip_max, total)
+    stats = stats_tile(chip_max, total).T[:STATS].astype(jnp.bfloat16)
     latent = latent.astype(jnp.bfloat16)
     chip = lax.div(lax.axis_index("ctx"), 2)
     for at, mask in enumerate(masks):
         target = at if before is None else chip ^ mask
-        message[target, :, :LAT] = latent[at * lines : (at + 1) * lines]
-        message[target, :, LAT:] = stats[at * lines : (at + 1) * lines]
+        for tile in range(LAT // LANES):
+            columns = slice(tile * LANES, (tile + 1) * LANES)
+            block = latent[at * lines : (at + 1) * lines, columns]
+            message[target, tile * lines : (tile + 1) * lines] = block
+        message[target, LAT // LANES * lines :] = stats
     if before is not None:
         finished, finished_masks = before
         for at, mask in enumerate(finished_masks):
@@ -209,24 +204,37 @@
         target[:, pl.ds(pl.multiple_of(lax.rem(start, half), LANES), span)] += residual
 
 
-def heads_kernel(rows, heads, parts, absorb, out_proj, hidden, send, flat_out, latent_buf):
-    chips = parts.shape[0]
-    stats = [from_stats(parts[chip, :, LAT:]) for chip in range(chips)]
+def heads_kernel(
+    rows, heads, orders, parts, absorb, out_proj, hidden, send, flat_out, latent_buf, stats_buf
+):
+    chips, lines = parts.shape[0], rows * heads
+    tiles = range(LAT // LANES)
+    last = LAT // LANES * lines
+    gathered = [parts[chip, last:].astype(jnp.float32) for chip in range(chips)]
+    stats_buf[...] = jnp.concatenate(gathered, axis=0).T
+    own_chip = lax.div(lax.axis_index("ctx"), 2)
+    stats = []
+    for chip in range(chips):
+        mask = chip ^ own_chip
+        place = jnp.int32(0)
+        for order in orders:
+            for at, held in enumerate(order):
+                place = jnp.where(mask == held, at, place)
+        block = stats_buf[pl.ds(pl.multiple_of(place * lines, 8), lines), :]
+        stats.append(from_stats(block[:, chip * STATS : (chip + 1) * STATS]))
     joint = functools.reduce(jnp.maximum, [shard_max for shard_max, _ in stats])
-    total = jnp.zeros_like(joint)
-    latent = jnp.zeros((rows * heads, LAT), jnp.float32)
-    for chip, (shard_max, part_total) in enumerate(stats):
-        factor = jnp.exp(shard_max - joint)
-        total += part_total * factor
-        latent += parts[chip, :, :LAT].astype(jnp.float32) * factor
-    latent = latent / total
-    tiles = range(LAT // LANES)
+    factors = [jnp.exp(shard_max - joint) for shard_max, _ in stats]
+    total = sum(part_total * factor for (_, part_total), factor in zip(stats, factors))
     for tile in tiles:
-        latent_buf[tile] = latent[:, tile * LANES : (tile + 1) * LANES]
+        latent = jnp.zeros((lines, LANES), jnp.float32)
+        for chip, factor in enumerate(factors):
+            part = parts[chip, tile * lines : (tile + 1) * lines]
+            latent += part.astype(jnp.float32) * factor
+        latent_buf[tile] = latent / total
     value_heads = []
     for head in range(heads):
-        lines = pl.ds(head, rows, stride=heads)
-        own = jnp.concatenate([latent_buf[tile, lines, :] for tile in tiles], axis=1)
+        picked = pl.ds(head, rows, stride=heads)
+        own = jnp.concatenate([latent_buf[tile, picked, :] for tile in tiles], axis=1)
         own = own.astype(jnp.bfloat16)
         value_heads.append(jnp.dot(own, absorb[head], preferred_element_type=jnp.float32))
     flat = jnp.concatenate(value_heads, axis=1).astype(jnp.bfloat16)
@@ -323,38 +331,36 @@
     table = call(
         table_kernel,
         shaped((2 * pages, LANES), jnp.int32),
-        [HBM] * 3 + [VMEM],
-        (page_row, page_index, lengths, mark),
-        scratch=[
-            pltpu.SMEM((pages,), jnp.int32),
-            pltpu.SMEM((pages,), jnp.int32),
-            pltpu.SMEM((rows,), jnp.int32),
-            pltpu.SemaphoreType.DMA((3,)),
-        ],
+        [VMEM] * 4,
+        (page_row[None], page_index[None], lengths[None], mark),
     )
     tables = (table, swap(table))
     near_masks = [mask for mask in blocks if mask % 2 == 0]
     far_masks = [mask for mask in blocks if mask % 2 == 1]
+    block_shape = (LAT // LANES * lines + STATS, LANES)
     near = call(
         functools.partial(near_kernel, rows, heads, near_masks),
-        shaped((len(near_masks), lines, LAT + LANES), bf16),
+        shaped((len(near_masks),) + block_shape, bf16),
         [VMEM] * (len(near_masks) + 4),
         tables + tuple(blocks[mask] for mask in near_masks) + (cache_t, cache_other),
     )
     message = call(
         functools.partial(far_kernel, rows, heads, far_masks, near_masks),
-        shaped((chips, lines, LAT + LANES), bf16),
+        shaped((chips,) + block_shape, bf16),
         [VMEM] * (len(far_masks) + 5),
         tables + tuple(blocks[mask] for mask in far_masks) + (cache_t, cache_other, near),
         ahead=(absorb_value, out_proj),
     )
     parts = exchange(message)
     send, flat = call(
-        functools.partial(heads_kernel, rows, heads),
+        functools.partial(heads_kernel, rows, heads, (near_masks, far_masks)),
         (shaped((rows, half), f32), shaped((rows, absorb_value.shape[0] * VHEAD), bf16)),
         [VMEM] * 4,
         (parts, absorb_value, out_proj, hidden_in),
-        scratch=[pltpu.VMEM((LAT // LANES, lines, LANES), f32)],
+        scratch=[
+            pltpu.VMEM((LAT // LANES, lines, LANES), f32),
+            pltpu.VMEM((LANES, chips * STATS), f32),
+        ],
         ahead=(gate_proj, up_proj, down_proj),
     )
     keep = call(

time: 65.8 us -> 65.7 us (level)
  no operation moved by 1% of the time
where the time goes in v5:
time: 65.7 us; the launch traced here: 65.4 us
  blocking collectives  37.5 us (57%)
  starting transfers between devices  11.9 us (18%)
  Pallas kernels  10.6 us (16%)
  waiting for transfers between devices  4.3 us (7%)
  other arithmetic  0.85 us (1%)
    all_to_all x2, blocking collectives, exchange(): lax.all_to_all(value, 'ctx', 0, 0, tiled=True, axis_index_groups=core_gro...  27.3 us
    ppermute x7, starting transfers between devices, gather_blocks(): arrived[mask | at] = lax.ppermute(held, 'ctx', pairs)  11.8 us
    pallas_call x8, Pallas kernels, call(): pl.pallas_call(kernel, out_shape=out_shape, in_specs=list(specs), out_spe...  10.6 us
    all_to_all x1, blocking collectives, shards(): received = lax.all_to_all(blocks, 'ctx', 0, 0, tiled=True)  10.2 us
    ppermute x7, waiting for transfers between devices, gather_blocks(): arrived[mask | at] = lax.ppermute(held, 'ctx', pairs)  4.16 us
  transfers between devices with their start and end apart: 11, of which 4 were waited for; matrix products, arithmetic and copies ran while one was open for 0% of the time, Pallas kernels for 7%

profile of v5, /device:TPU:0, one launch (start us, length us, event | category | flops | bytes accessed | tf_op | source)
XLA Modules:
  0.0 65.4 jit_solution(1844193960547902347)
XLA Ops:
  0.0 4.1 %collective-permute-start = (bf16[32,576]{1,0:T(8,128)(2,1)}, bf16[32,576]{1,0:T(8,128)(2,1)S(1)}, u32[]{:S(2)}, u32[]{:S(2)}) collective-permute-start(bf16[32,576]{1,0:T(8,128)(2,1)} %bitcast.18), channel_id=1, source_target_pairs={{0,8},{1,9},{2,10},{3,11},{4,12},{5,13},{6,14},{7,15},{8,0},{9,1},... | collective-permute-start | bytes 110600 | tf_op jit(solution)/shard_map/ppermute | solution.py:46
  4.2 2.6 %collective-permute-done.refs_3_ = bf16[32,576]{1,0:T(8,128)(2,1)S(1)} collective-permute-done((bf16[32,576]{1,0:T(8,128)(2,1)}, bf16[32,576]{1,0:T(8,128)(2,1)S(1)}, u32[]{:S(2)}, u32[]{:S(2)}) %collective-permute-start) | collective-permute-done | bytes 36896 | tf_op jit(solution)/shard_map/ppermute | solution.py:46
  6.8 0.0 copy-done.4
  6.8 0.0 collective-permute-start.8
  6.8 0.0 copy-done.5
  6.8 1.5 %collective-permute-start.4 = (bf16[32,576]{1,0:T(8,128)(2,1)S(1)}, bf16[32,576]{1,0:T(8,128)(2,1)S(1)}, u32[]{:S(2)}, u32[]{:S(2)}) collective-permute-start(bf16[32,576]{1,0:T(8,128)(2,1)S(1)} %bitcast.19), channel_id=1, source_target_pairs={{0,4},{1,5},{2,6},{3,7},{4,0},{5,1},{6,2},{7,3},{8,12},{9,13},{10,... | collective-permute-start | bytes 110600 | tf_op jit(solution)/shard_map/ppermute | solution.py:46
  8.3 0.6 collective-permute-start.6
  8.9 0.0 copy-done.8
  8.9 0.0 copy-done.9
  8.9 0.0 copy-done.10
  8.9 0.1 shard_map.119.refs_0_
  9.0 0.0 collective-permute-start.1
  9.1 1.8 %collective-permute-start.2 = (bf16[32,576]{1,0:T(8,128)(2,1)S(1)}, bf16[32,576]{1,0:T(8,128)(2,1)S(1)}, u32[]{:S(2)}, u32[]{:S(2)}) collective-permute-start(bf16[32,576]{1,0:T(8,128)(2,1)S(1)} %bitcast.20), channel_id=1, source_target_pairs={{0,2},{1,3},{2,0},{3,1},{4,6},{5,7},{6,4},{7,5},{8,10},{9,11},{10,... | collective-permute-start | bytes 110600 | tf_op jit(solution)/shard_map/ppermute | solution.py:46
  10.9 0.0 collective-permute-done.4.refs_4_
  10.9 1.7 %collective-permute-start.3 = (bf16[32,576]{1,0:T(8,128)(2,1)S(1)}, bf16[32,576]{1,0:T(8,128)(2,1)S(1)}, u32[]{:S(2)}, u32[]{:S(2)}) collective-permute-start(bf16[32,576]{1,0:T(8,128)(2,1)S(1)} %collective-permute-done.refs_3_), channel_id=1, source_target_pairs={{0,2},{1,3},{2,0},{3,1},{4,6},{5,7},{6,4},{7,5},{8,10},{9,11},{10,... | collective-permute-start | bytes 110600 | tf_op jit(solution)/shard_map/ppermute | solution.py:46
  12.6 0.0 collective-permute-done.1.refs_1_
  12.6 0.3 collective-permute-start.5
  12.9 0.0 collective-permute-done.6.refs_5_
  12.9 1.7 %collective-permute-start.7 = (bf16[32,576]{1,0:T(8,128)(2,1)S(1)}, bf16[32,576]{1,0:T(8,128)(2,1)S(1)}, u32[]{:S(2)}, u32[]{:S(2)}) collective-permute-start(bf16[32,576]{1,0:T(8,128)(2,1)S(1)} %collective-permute-done.6.refs_5_), channel_id=1, source_target_pairs={{0,2},{1,3},{2,0},{3,1},{4,6},{5,7},{6,4},{7,5},{8,10},{9,11},{10,... | collective-permute-start | bytes 110600 | tf_op jit(solution)/shard_map/ppermute | solution.py:46
  14.6 0.0 collective-permute-done.8.refs_7_
  14.6 0.9 %shard_map.120.refs_8_ = bf16[4,144,128]{2,1,0:T(8,128)(2,1)S(1)} custom-call(s32[8,128]{1,0:T(8,128)S(1)} %shard_map.119.refs_0_, s32[8,128]{1,0:T(8,128)S(1)} %collective-permute-done.1.refs_1_, bf16[32,576]{1,0:T(8,128)(2,1)S(1)} %bitcast.21, bf16[32,576]{1,0:T(8,128)(2,1)S(1)} %collective-permute-done.refs_3_, ...), custom_call_target="tpu_custom_call" | custom-call | bytes 1335296 | tf_op jit(solution)/shard_map/pallas_call | solution.py:66
  15.5 0.0 collective-permute-done.2.refs_2_
  15.5 1.1 %collective-permute-done.5.refs_4_ = bf16[32,576]{1,0:T(8,128)(2,1)S(1)} collective-permute-done((bf16[32,576]{1,0:T(8,128)(2,1)S(1)}, bf16[32,576]{1,0:T(8,128)(2,1)S(1)}, u32[]{:S(2)}, u32[]{:S(2)}) %collective-permute-start.5) | collective-permute-done | bytes 36896 | tf_op jit(solution)/shard_map/ppermute | solution.py:46
  16.6 0.0 collective-permute-done.3.refs_3_
  16.6 0.4 collective-permute-done.7.refs_5_
  17.0 0.9 %shard_map.121 = bf16[8,144,128]{2,1,0:T(8,128)(2,1)S(1)} custom-call(s32[8,128]{1,0:T(8,128)S(1)} %shard_map.119.refs_0_, s32[8,128]{1,0:T(8,128)S(1)} %collective-permute-done.1.refs_1_, bf16[32,576]{1,0:T(8,128)(2,1)S(1)} %collective-permute-done.2.refs_2_, bf16[32,576]{1,0:T(8,128)(2,1)S(1)} %collective-permute-done.3.refs_3_, ...), custom_call_target="tpu_custom_call" | custom-call | flops 1572864000000 | bytes 1482752 | tf_op jit(solution)/shard_map/pallas_call | solution.py:66
  17.9 15.1 %all_to_all.15.parts = bf16[8,144,128]{2,1,0:T(8,128)(2,1)S(1)} all-to-all(bf16[8,144,128]{2,1,0:T(8,128)(2,1)S(1)} %shard_map.121), channel_id=1, replica_groups={{0,2,4,6,8,10,12,14},{1,3,5,7,9,11,13,15},{16,18,20,22,24,26,28,30},{17..., dimensions={0} | all-to-all | bytes 589824 | tf_op jit(solution)/shard_map/all_to_all | solution.py:55
  33.0 0.0 copy-done
  33.1 0.0 copy-done.3
  33.1 0.0 copy-done.7
  33.1 1.8 %shard_map.122 = (f32[4,3584]{1,0:T(4,128)S(1)}, bf16[4,1024]{1,0:T(4,128)(2,1)S(1)}) custom-call(bf16[8,144,128]{2,1,0:T(8,128)(2,1)S(1)} %all_to_all.15.parts, bf16[8,512,128]{2,1,0:T(8,128)(2,1)S(1)} %copy-done.3, bf16[1024,7168]{1,0:T(8,128)(2,1)S(1)} %copy-done, bf16[4,448]{1,0:T(4,128)(2,1)S(1)} %copy-done.7), custom_call_target="tpu_custom_call" | custom-call | flops 2477260800000 | bytes 16027136 | tf_op jit(solution)/shard_map/pallas_call | solution.py:66
  34.9 0.0 collective-permute-start.9
  34.9 0.0 copy-start.6
  34.9 0.0 slice-start
  34.9 1.1 %shard_map.123 = f32[4,3584]{1,0:T(4,128)S(1)} custom-call(bf16[4,1024]{1,0:T(4,128)(2,1)S(1)} %get-tuple-element.17.flat, bf16[1024,7168]{1,0:T(8,128)(2,1)S(1)} %copy-done, bf16[4,448]{1,0:T(4,128)(2,1)S(1)} %copy-done.7), custom_call_target="tpu_custom_call" | custom-call | bytes 14691840 | tf_op jit(solution)/shard_map/pallas_call | solution.py:66
  36.0 0.1 collective-permute-done.9
  36.2 0.1 broadcast_in_dim.21
  36.2 0.0 slice-start.1
  36.2 12.2 %all_to_all.16 = bf16[8,4,3584]{2,1,0:T(4,128)(2,1)S(1)} all-to-all(bf16[8,4,3584]{2,1,0:T(4,128)(2,1)S(1)} %broadcast_in_dim.21), channel_id=1, replica_groups={{0,2,4,6,8,10,12,14},{1,3,5,7,9,11,13,15},{16,18,20,22,24,26,28,30},{17..., dimensions={0} | all-to-all | bytes 458752 | tf_op jit(solution)/shard_map/all_to_all | solution.py:55
  48.4 0.2 convert_reduce_fusion.mine
  48.6 0.1 collective-permute-start.10
  48.7 0.0 copy-done.1
  48.7 2.2 %shard_map.124.both = f32[4,1152]{1,0:T(4,128)S(1)} custom-call(f32[4,3584]{1,0:T(4,128)S(1)} %convert_reduce_fusion.mine, f32[1,7168]{1,0:T(1,128)S(1)} %bitcast.22, bf16[576,7168]{1,0:T(8,128)(2,1)S(1)} %bitcast.9, bf16[576,7168]{1,0:T(8,128)(2,1)S(1)} %bitcast.11), custom_call_target="tpu_custom_call" | custom-call | bytes 16601088 | tf_op jit(solution)/shard_map/pallas_call | solution.py:66
  51.0 0.0 collective-permute-done.10.other
  51.0 0.0 slice-done.1
  51.0 3.6 %shard_map.125 = (bf16[16,4,448]{2,1,0:T(4,128)(2,1)S(1)}, f32[4,448]{1,0:T(4,128)S(1)}) custom-call(f32[4,3584]{1,0:T(4,128)S(1)} %convert_reduce_fusion.mine, f32[4,3584]{1,0:T(4,128)S(1)} %collective-permute-done.10.other, f32[4,1152]{1,0:T(4,128)S(1)} %shard_map.124.both, f32[1,7168]{1,0:T(1,128)S(1)} %bitcast.23, bf16[576,7168]{1,0:T(8,128)(2,1)S(1)} %bitcast.10, ...), custom_call_target="tpu_custom_call" | custom-call | bytes 24934400 | tf_op jit(solution)/shard_map/pallas_call | solution.py:66
  54.6 10.2 %all_to_all.17 = bf16[16,4,448]{2,1,0:T(4,128)(2,1)S(1)} all-to-all(bf16[16,4,448]{2,1,0:T(4,128)(2,1)S(1)} %get-tuple-element.20), channel_id=1, replica_groups=mesh['groups'=2,'ctx'=16] {'ctx'}, dimensions={0} | all-to-all | bytes 114688 | tf_op jit(solution)/shard_map/all_to_all | solution.py:385
  64.8 0.6 add_convert_fusion.1
  (17 shorter events, 0.1 us)
Async XLA Ops:
  0.0 6.8 %copy-start.4 = (bf16[512,576]{0,1:T(8,128)(2,1)S(1)}, bf16[512,576]{0,1:T(8,128)(2,1)}, u32[]{:S(2)}) copy-start(bf16[512,576]{0,1:T(8,128)(2,1)} %param.13) | copy-start | bytes 1769476
  0.0 6.8 %copy-start.5 = (bf16[4,8,576]{2,1,0:T(8,128)(2,1)S(1)}, bf16[4,8,576]{2,1,0:T(8,128)(2,1)}, u32[]{:S(2)}) copy-start(bf16[4,8,576]{2,1,0:T(8,128)(2,1)} %param.12) | copy-start | bytes 110596
  0.0 8.9 %copy-start.8 = (s32[4]{0:T(128)S(1)}, s32[4]{0:T(128)}, u32[]{:S(2)}) copy-start(s32[4]{0:T(128)} %param.14) | copy-start | bytes 52
  0.0 8.9 %copy-start.9 = (s32[4]{0:T(128)S(1)}, s32[4]{0:T(128)}, u32[]{:S(2)}) copy-start(s32[4]{0:T(128)} %param.15) | copy-start | bytes 52
  0.0 8.9 %copy-start.10 = (s32[4]{0:T(128)S(1)}, s32[4]{0:T(128)}, u32[]{:S(2)}) copy-start(s32[4]{0:T(128)} %param.16) | copy-start | bytes 52
  0.0 6.8 %collective-permute-start = (bf16[32,576]{1,0:T(8,128)(2,1)}, bf16[32,576]{1,0:T(8,128)(2,1)S(1)}, u32[]{:S(2)}, u32[]{:S(2)}) collective-permute-start(bf16[32,576]{1,0:T(8,128)(2,1)} %bitcast.18), channel_id=1, source_target_pairs={{0,8},{1,9},{2,10},{3,11},{4,12},{5,13},{6,14},{7,15},{8,0},{9,1},... | collective-permute-start | bytes 110600 | tf_op jit(solution)/shard_map/ppermute | solution.py:46
  6.8 7.8 %collective-permute-start.8 = (bf16[576,512]{1,0:T(8,128)(2,1)S(1)}, bf16[576,512]{1,0:T(8,128)(2,1)S(1)}, u32[]{:S(2)}, u32[]{:S(2)}) collective-permute-start(bf16[576,512]{1,0:T(8,128)(2,1)S(1)} %bitcast.15), channel_id=1, source_target_pairs={{0,1},{1,0},{2,3},{3,2},{4,5},{5,4},{6,7},{7,6},{8,9},{9,8},{10,11... | collective-permute-start | bytes 1769480 | tf_op jit(solution)/shard_map/ppermute | solution.py:31
  6.8 4.1 %collective-permute-start.4 = (bf16[32,576]{1,0:T(8,128)(2,1)S(1)}, bf16[32,576]{1,0:T(8,128)(2,1)S(1)}, u32[]{:S(2)}, u32[]{:S(2)}) collective-permute-start(bf16[32,576]{1,0:T(8,128)(2,1)S(1)} %bitcast.19), channel_id=1, source_target_pairs={{0,4},{1,5},{2,6},{3,7},{4,0},{5,1},{6,2},{7,3},{8,12},{9,13},{10,... | collective-permute-start | bytes 110600 | tf_op jit(solution)/shard_map/ppermute | solution.py:46
  8.3 4.6 %collective-permute-start.6 = (bf16[32,576]{1,0:T(8,128)(2,1)S(1)}, bf16[32,576]{1,0:T(8,128)(2,1)S(1)}, u32[]{:S(2)}, u32[]{:S(2)}) collective-permute-start(bf16[32,576]{1,0:T(8,128)(2,1)S(1)} %collective-permute-done.refs_3_), channel_id=1, source_target_pairs={{0,4},{1,5},{2,6},{3,7},{4,0},{5,1},{6,2},{7,3},{8,12},{9,13},{10,... | collective-permute-start | bytes 110600 | tf_op jit(solution)/shard_map/ppermute | solution.py:46
  9.0 3.6 %collective-permute-start.1 = (s32[8,128]{1,0:T(8,128)S(1)}, s32[8,128]{1,0:T(8,128)S(1)}, u32[]{:S(2)}, u32[]{:S(2)}) collective-permute-start(s32[8,128]{1,0:T(8,128)S(1)} %shard_map.119.refs_0_), channel_id=1, source_target_pairs={{0,1},{1,0},{2,3},{3,2},{4,5},{5,4},{6,7},{7,6},{8,9},{9,8},{10,11... | collective-permute-start | bytes 12296 | tf_op jit(solution)/shard_map/ppermute | solution.py:31
  9.1 6.4 %collective-permute-start.2 = (bf16[32,576]{1,0:T(8,128)(2,1)S(1)}, bf16[32,576]{1,0:T(8,128)(2,1)S(1)}, u32[]{:S(2)}, u32[]{:S(2)}) collective-permute-start(bf16[32,576]{1,0:T(8,128)(2,1)S(1)} %bitcast.20), channel_id=1, source_target_pairs={{0,2},{1,3},{2,0},{3,1},{4,6},{5,7},{6,4},{7,5},{8,10},{9,11},{10,... | collective-permute-start | bytes 110600 | tf_op jit(solution)/shard_map/ppermute | solution.py:46
  10.9 5.7 %collective-permute-start.3 = (bf16[32,576]{1,0:T(8,128)(2,1)S(1)}, bf16[32,576]{1,0:T(8,128)(2,1)S(1)}, u32[]{:S(2)}, u32[]{:S(2)}) collective-permute-start(bf16[32,576]{1,0:T(8,128)(2,1)S(1)} %collective-permute-done.refs_3_), channel_id=1, source_target_pairs={{0,2},{1,3},{2,0},{3,1},{4,6},{5,7},{6,4},{7,5},{8,10},{9,11},{10,... | collective-permute-start | bytes 110600 | tf_op jit(solution)/shard_map/ppermute | solution.py:46
  12.6 4.0 %collective-permute-start.5 = (bf16[32,576]{1,0:T(8,128)(2,1)S(1)}, bf16[32,576]{1,0:T(8,128)(2,1)S(1)}, u32[]{:S(2)}, u32[]{:S(2)}) collective-permute-start(bf16[32,576]{1,0:T(8,128)(2,1)S(1)} %collective-permute-done.4.refs_4_), channel_id=1, source_target_pairs={{0,2},{1,3},{2,0},{3,1},{4,6},{5,7},{6,4},{7,5},{8,10},{9,11},{10,... | collective-permute-start | bytes 110600 | tf_op jit(solution)/shard_map/ppermute | solution.py:46
  12.9 4.1 %collective-permute-start.7 = (bf16[32,576]{1,0:T(8,128)(2,1)S(1)}, bf16[32,576]{1,0:T(8,128)(2,1)S(1)}, u32[]{:S(2)}, u32[]{:S(2)}) collective-permute-start(bf16[32,576]{1,0:T(8,128)(2,1)S(1)} %collective-permute-done.6.refs_5_), channel_id=1, source_target_pairs={{0,2},{1,3},{2,0},{3,1},{4,6},{5,7},{6,4},{7,5},{8,10},{9,11},{10,... | collective-permute-start | bytes 110600 | tf_op jit(solution)/shard_map/ppermute | solution.py:46
  17.0 16.0 %copy-start = (bf16[1024,7168]{1,0:T(8,128)(2,1)S(1)}, bf16[1024,7168]{1,0:T(8,128)(2,1)}, u32[]{:S(2)}) copy-start(bf16[1024,7168]{1,0:T(8,128)(2,1)} %out_proj.3) | copy-start | bytes 44040196
  17.0 16.0 %copy-start.3 = (bf16[8,512,128]{2,1,0:T(8,128)(2,1)S(1)}, bf16[8,512,128]{2,1,0:T(8,128)(2,1)}, u32[]{:S(2)}) copy-start(bf16[8,512,128]{2,1,0:T(8,128)(2,1)} %absorb.1) | copy-start | bytes 3145732
  17.0 16.0 %copy-start.7 = (bf16[4,448]{1,0:T(4,128)(2,1)S(1)}, bf16[4,448]{1,0:T(4,128)(2,1)}, u32[]{:S(2)}) copy-start(bf16[4,448]{1,0:T(4,128)(2,1)} %hidden.3) | copy-start | bytes 10756
  34.9 1.2 %collective-permute-start.9 = (f32[4,3584]{1,0:T(4,128)S(1)}, f32[4,3584]{1,0:T(4,128)S(1)}, u32[]{:S(2)}, u32[]{:S(2)}) collective-permute-start(f32[4,3584]{1,0:T(4,128)S(1)} %get-tuple-element.18), channel_id=1, source_target_pairs={{0,1},{1,0},{2,3},{3,2},{4,5},{5,4},{6,7},{7,6},{8,9},{9,8},{10,11... | collective-permute-start | bytes 172040 | tf_op jit(solution)/shard_map/ppermute | solution.py:31
  34.9 13.8 %copy-start.1 = (bf16[7168,576]{0,1:T(8,128)(2,1)S(1)}, bf16[7168,576]{0,1:T(8,128)(2,1)}, u32[]{:S(2)}) copy-start(bf16[7168,576]{0,1:T(8,128)(2,1)} %param.21) | copy-start | bytes 24772612
  34.9 13.8 %copy-start.2 = (bf16[7168,576]{0,1:T(8,128)(2,1)S(1)}, bf16[7168,576]{0,1:T(8,128)(2,1)}, u32[]{:S(2)}) copy-start(bf16[7168,576]{0,1:T(8,128)(2,1)} %param.22) | copy-start | bytes 24772612
  34.9 13.8 %copy-start.6 = (f32[7168]{0:T(1024)S(1)}, f32[7168]{0:T(1024)}, u32[]{:S(2)}) copy-start(f32[7168]{0:T(1024)} %param.18) | copy-start | bytes 86020
  34.9 16.1 %slice-start = ((s8[8257536]{0:T(1024)(128)(4,1)}), s8[4194304]{0:T(1024)(128)(4,1)S(1)}, s32[]{:S(2)}) async-start(s8[8257536]{0:T(1024)(128)(4,1)} %bitcast.13), calls=%async_computation.3 | async-start | bytes 8388608
  36.2 14.8 %slice-start.1 = ((s8[8257536]{0:T(1024)(128)(4,1)}), s8[4063232]{0:T(1024)(128)(4,1)S(1)}, s32[]{:S(2)}) async-start(s8[8257536]{0:T(1024)(128)(4,1)} %bitcast.13), calls=%async_computation.4 | async-start | bytes 8126464
  48.6 2.4 %collective-permute-start.10 = (f32[4,3584]{1,0:T(4,128)S(1)}, f32[4,3584]{1,0:T(4,128)S(1)}, u32[]{:S(2)}, u32[]{:S(2)}) collective-permute-start(f32[4,3584]{1,0:T(4,128)S(1)} %convert_reduce_fusion.mine), channel_id=1, source_target_pairs={{0,1},{1,0},{2,3},{3,2},{4,5},{5,4},{6,7},{7,6},{8,9},{9,8},{10,11... | collective-permute-start | bytes 172040 | tf_op jit(solution)/shard_map/ppermute | solution.py:31

commit v6 on v5

--- a/solution.py
+++ b/solution.py
@@ -207,28 +207,25 @@
 def heads_kernel(
     rows, heads, orders, parts, absorb, out_proj, hidden, send, flat_out, latent_buf, stats_buf
 ):
-    chips, lines = parts.shape[0], rows * heads
+    lines = rows * heads
     tiles = range(LAT // LANES)
     last = LAT // LANES * lines
-    gathered = [parts[chip, last:].astype(jnp.float32) for chip in range(chips)]
+    own_chip = lax.div(lax.axis_index("ctx"), 2)
+    masks = [mask for order in orders for mask in order]
+    places = [place for order in orders for place in range(len(order))]
+    gathered = [parts[own_chip ^ mask, last:].astype(jnp.float32) for mask in masks]
     stats_buf[...] = jnp.concatenate(gathered, axis=0).T
-    own_chip = lax.div(lax.axis_index("ctx"), 2)
     stats = []
-    for chip in range(chips):
-        mask = chip ^ own_chip
-        place = jnp.int32(0)
-        for order in orders:
-            for at, held in enumerate(order):
-                place = jnp.where(mask == held, at, place)
-        block = stats_buf[pl.ds(pl.multiple_of(place * lines, 8), lines), :]
-        stats.append(from_stats(block[:, chip * STATS : (chip + 1) * STATS]))
+    for at, place in enumerate(places):
+        block = stats_buf[place * lines : (place + 1) * lines, :]
+        stats.append(from_stats(block[:, at * STATS : (at + 1) * STATS]))
     joint = functools.reduce(jnp.maximum, [shard_max for shard_max, _ in stats])
     factors = [jnp.exp(shard_max - joint) for shard_max, _ in stats]
     total = sum(part_total * factor for (_, part_total), factor in zip(stats, factors))
     for tile in tiles:
         latent = jnp.zeros((lines, LANES), jnp.float32)
-        for chip, factor in enumerate(factors):
-            part = parts[chip, tile * lines : (tile + 1) * lines]
+        for mask, factor in zip(masks, factors):
+            part = parts[own_chip ^ mask, tile * lines : (tile + 1) * lines]
             latent += part.astype(jnp.float32) * factor
         latent_buf[tile] = latent / total
     value_heads = []

time: 65.7 us -> 65.6 us (level)
  no operation moved by 1% of the time
where the time goes in v6:
time: 65.6 us; the launch traced here: 65.4 us
  blocking collectives  37.5 us (57%)
  starting transfers between devices  11.9 us (18%)
  Pallas kernels  10.5 us (16%)
  waiting for transfers between devices  4.3 us (7%)
  other arithmetic  0.85 us (1%)
    all_to_all x2, blocking collectives, exchange(): lax.all_to_all(value, 'ctx', 0, 0, tiled=True, axis_index_groups=core_gro...  27.3 us
    ppermute x7, starting transfers between devices, gather_blocks(): arrived[mask | at] = lax.ppermute(held, 'ctx', pairs)  11.8 us
    pallas_call x8, Pallas kernels, call(): pl.pallas_call(kernel, out_shape=out_shape, in_specs=list(specs), out_spe...  10.5 us
    all_to_all x1, blocking collectives, shards(): received = lax.all_to_all(blocks, 'ctx', 0, 0, tiled=True)  10.2 us
    ppermute x7, waiting for transfers between devices, gather_blocks(): arrived[mask | at] = lax.ppermute(held, 'ctx', pairs)  4.16 us
  transfers between devices with their start and end apart: 11, of which 4 were waited for; matrix products, arithmetic and copies ran while one was open for 0% of the time, Pallas kernels for 7%

profile of v6, /device:TPU:0, one launch (start us, length us, event | category | flops | bytes accessed | tf_op | source)
XLA Modules:
  0.0 65.4 jit_solution(6377826333848669153)
XLA Ops:
  0.0 4.1 %collective-permute-start = (bf16[32,576]{1,0:T(8,128)(2,1)}, bf16[32,576]{1,0:T(8,128)(2,1)S(1)}, u32[]{:S(2)}, u32[]{:S(2)}) collective-permute-start(bf16[32,576]{1,0:T(8,128)(2,1)} %bitcast.18), channel_id=1, source_target_pairs={{0,8},{1,9},{2,10},{3,11},{4,12},{5,13},{6,14},{7,15},{8,0},{9,1},... | collective-permute-start | bytes 110600 | tf_op jit(solution)/shard_map/ppermute | solution.py:46
  4.2 2.6 %collective-permute-done.refs_3_ = bf16[32,576]{1,0:T(8,128)(2,1)S(1)} collective-permute-done((bf16[32,576]{1,0:T(8,128)(2,1)}, bf16[32,576]{1,0:T(8,128)(2,1)S(1)}, u32[]{:S(2)}, u32[]{:S(2)}) %collective-permute-start) | collective-permute-done | bytes 36896 | tf_op jit(solution)/shard_map/ppermute | solution.py:46
  6.8 0.0 copy-done.4
  6.8 0.0 collective-permute-start.8
  6.8 0.0 copy-done.5
  6.8 1.5 %collective-permute-start.4 = (bf16[32,576]{1,0:T(8,128)(2,1)S(1)}, bf16[32,576]{1,0:T(8,128)(2,1)S(1)}, u32[]{:S(2)}, u32[]{:S(2)}) collective-permute-start(bf16[32,576]{1,0:T(8,128)(2,1)S(1)} %bitcast.19), channel_id=1, source_target_pairs={{0,4},{1,5},{2,6},{3,7},{4,0},{5,1},{6,2},{7,3},{8,12},{9,13},{10,... | collective-permute-start | bytes 110600 | tf_op jit(solution)/shard_map/ppermute | solution.py:46
  8.3 0.6 collective-permute-start.6
  8.9 0.0 copy-done.8
  8.9 0.0 copy-done.9
  8.9 0.0 copy-done.10
  8.9 0.1 shard_map.119.refs_0_
  9.0 0.0 collective-permute-start.1
  9.1 1.8 %collective-permute-start.2 = (bf16[32,576]{1,0:T(8,128)(2,1)S(1)}, bf16[32,576]{1,0:T(8,128)(2,1)S(1)}, u32[]{:S(2)}, u32[]{:S(2)}) collective-permute-start(bf16[32,576]{1,0:T(8,128)(2,1)S(1)} %bitcast.20), channel_id=1, source_target_pairs={{0,2},{1,3},{2,0},{3,1},{4,6},{5,7},{6,4},{7,5},{8,10},{9,11},{10,... | collective-permute-start | bytes 110600 | tf_op jit(solution)/shard_map/ppermute | solution.py:46
  10.9 0.0 collective-permute-done.4.refs_4_
  10.9 1.7 %collective-permute-start.3 = (bf16[32,576]{1,0:T(8,128)(2,1)S(1)}, bf16[32,576]{1,0:T(8,128)(2,1)S(1)}, u32[]{:S(2)}, u32[]{:S(2)}) collective-permute-start(bf16[32,576]{1,0:T(8,128)(2,1)S(1)} %collective-permute-done.refs_3_), channel_id=1, source_target_pairs={{0,2},{1,3},{2,0},{3,1},{4,6},{5,7},{6,4},{7,5},{8,10},{9,11},{10,... | collective-permute-start | bytes 110600 | tf_op jit(solution)/shard_map/ppermute | solution.py:46
  12.6 0.0 collective-permute-done.1.refs_1_
  12.6 0.3 collective-permute-start.5
  12.9 0.0 collective-permute-done.6.refs_5_
  12.9 1.7 %collective-permute-start.7 = (bf16[32,576]{1,0:T(8,128)(2,1)S(1)}, bf16[32,576]{1,0:T(8,128)(2,1)S(1)}, u32[]{:S(2)}, u32[]{:S(2)}) collective-permute-start(bf16[32,576]{1,0:T(8,128)(2,1)S(1)} %collective-permute-done.6.refs_5_), channel_id=1, source_target_pairs={{0,2},{1,3},{2,0},{3,1},{4,6},{5,7},{6,4},{7,5},{8,10},{9,11},{10,... | collective-permute-start | bytes 110600 | tf_op jit(solution)/shard_map/ppermute | solution.py:46
  14.6 0.0 collective-permute-done.8.refs_7_
  14.6 0.9 %shard_map.120.refs_8_ = bf16[4,144,128]{2,1,0:T(8,128)(2,1)S(1)} custom-call(s32[8,128]{1,0:T(8,128)S(1)} %shard_map.119.refs_0_, s32[8,128]{1,0:T(8,128)S(1)} %collective-permute-done.1.refs_1_, bf16[32,576]{1,0:T(8,128)(2,1)S(1)} %bitcast.21, bf16[32,576]{1,0:T(8,128)(2,1)S(1)} %collective-permute-done.refs_3_, ...), custom_call_target="tpu_custom_call" | custom-call | bytes 1335296 | tf_op jit(solution)/shard_map/pallas_call | solution.py:66
  15.5 0.0 collective-permute-done.2.refs_2_
  15.5 1.1 %collective-permute-done.5.refs_4_ = bf16[32,576]{1,0:T(8,128)(2,1)S(1)} collective-permute-done((bf16[32,576]{1,0:T(8,128)(2,1)S(1)}, bf16[32,576]{1,0:T(8,128)(2,1)S(1)}, u32[]{:S(2)}, u32[]{:S(2)}) %collective-permute-start.5) | collective-permute-done | bytes 36896 | tf_op jit(solution)/shard_map/ppermute | solution.py:46
  16.6 0.0 collective-permute-done.3.refs_3_
  16.6 0.4 collective-permute-done.7.refs_5_
  17.0 0.9 %shard_map.121 = bf16[8,144,128]{2,1,0:T(8,128)(2,1)S(1)} custom-call(s32[8,128]{1,0:T(8,128)S(1)} %shard_map.119.refs_0_, s32[8,128]{1,0:T(8,128)S(1)} %collective-permute-done.1.refs_1_, bf16[32,576]{1,0:T(8,128)(2,1)S(1)} %collective-permute-done.2.refs_2_, bf16[32,576]{1,0:T(8,128)(2,1)S(1)} %collective-permute-done.3.refs_3_, ...), custom_call_target="tpu_custom_call" | custom-call | flops 1572864000000 | bytes 1482752 | tf_op jit(solution)/shard_map/pallas_call | solution.py:66
  17.9 15.1 %all_to_all.15.parts = bf16[8,144,128]{2,1,0:T(8,128)(2,1)S(1)} all-to-all(bf16[8,144,128]{2,1,0:T(8,128)(2,1)S(1)} %shard_map.121), channel_id=1, replica_groups={{0,2,4,6,8,10,12,14},{1,3,5,7,9,11,13,15},{16,18,20,22,24,26,28,30},{17..., dimensions={0} | all-to-all | bytes 589824 | tf_op jit(solution)/shard_map/all_to_all | solution.py:55
  33.0 0.0 copy-done
  33.1 0.0 copy-done.3
  33.1 0.0 copy-done.7
  33.1 1.8 %shard_map.122 = (f32[4,3584]{1,0:T(4,128)S(1)}, bf16[4,1024]{1,0:T(4,128)(2,1)S(1)}) custom-call(bf16[8,144,128]{2,1,0:T(8,128)(2,1)S(1)} %all_to_all.15.parts, bf16[8,512,128]{2,1,0:T(8,128)(2,1)S(1)} %copy-done.3, bf16[1024,7168]{1,0:T(8,128)(2,1)S(1)} %copy-done, bf16[4,448]{1,0:T(4,128)(2,1)S(1)} %copy-done.7), custom_call_target="tpu_custom_call" | custom-call | flops 2477260800000 | bytes 16027136 | tf_op jit(solution)/shard_map/pallas_call | solution.py:66
  34.8 0.0 collective-permute-start.9
  34.9 0.0 copy-start.6
  34.9 0.0 slice-start
  34.9 1.1 %shard_map.123 = f32[4,3584]{1,0:T(4,128)S(1)} custom-call(bf16[4,1024]{1,0:T(4,128)(2,1)S(1)} %get-tuple-element.17.flat, bf16[1024,7168]{1,0:T(8,128)(2,1)S(1)} %copy-done, bf16[4,448]{1,0:T(4,128)(2,1)S(1)} %copy-done.7), custom_call_target="tpu_custom_call" | custom-call | bytes 14691840 | tf_op jit(solution)/shard_map/pallas_call | solution.py:66
  35.9 0.1 collective-permute-done.9
  36.1 0.1 broadcast_in_dim.21
  36.2 0.0 slice-start.1
  36.2 12.2 %all_to_all.16 = bf16[8,4,3584]{2,1,0:T(4,128)(2,1)S(1)} all-to-all(bf16[8,4,3584]{2,1,0:T(4,128)(2,1)S(1)} %broadcast_in_dim.21), channel_id=1, replica_groups={{0,2,4,6,8,10,12,14},{1,3,5,7,9,11,13,15},{16,18,20,22,24,26,28,30},{17..., dimensions={0} | all-to-all | bytes 458752 | tf_op jit(solution)/shard_map/all_to_all | solution.py:55
  48.4 0.2 convert_reduce_fusion.mine
  48.6 0.1 collective-permute-start.10
  48.7 2.2 %shard_map.124.both = f32[4,1152]{1,0:T(4,128)S(1)} custom-call(f32[4,3584]{1,0:T(4,128)S(1)} %convert_reduce_fusion.mine, f32[1,7168]{1,0:T(1,128)S(1)} %bitcast.22, bf16[576,7168]{1,0:T(8,128)(2,1)S(1)} %bitcast.9, bf16[576,7168]{1,0:T(8,128)(2,1)S(1)} %bitcast.11), custom_call_target="tpu_custom_call" | custom-call | bytes 16601088 | tf_op jit(solution)/shard_map/pallas_call | solution.py:66
  50.9 0.0 collective-permute-done.10.other
  50.9 0.0 slice-done
  50.9 0.0 slice-done.1
  51.0 3.6 %shard_map.125 = (bf16[16,4,448]{2,1,0:T(4,128)(2,1)S(1)}, f32[4,448]{1,0:T(4,128)S(1)}) custom-call(f32[4,3584]{1,0:T(4,128)S(1)} %convert_reduce_fusion.mine, f32[4,3584]{1,0:T(4,128)S(1)} %collective-permute-done.10.other, f32[4,1152]{1,0:T(4,128)S(1)} %shard_map.124.both, f32[1,7168]{1,0:T(1,128)S(1)} %bitcast.23, bf16[576,7168]{1,0:T(8,128)(2,1)S(1)} %bitcast.10, ...), custom_call_target="tpu_custom_call" | custom-call | bytes 24934400 | tf_op jit(solution)/shard_map/pallas_call | solution.py:66
  54.5 10.2 %all_to_all.17 = bf16[16,4,448]{2,1,0:T(4,128)(2,1)S(1)} all-to-all(bf16[16,4,448]{2,1,0:T(4,128)(2,1)S(1)} %get-tuple-element.20), channel_id=1, replica_groups=mesh['groups'=2,'ctx'=16] {'ctx'}, dimensions={0} | all-to-all | bytes 114688 | tf_op jit(solution)/shard_map/all_to_all | solution.py:382
  64.8 0.6 add_convert_fusion.1
  (17 shorter events, 0.1 us)
Async XLA Ops:
  0.0 6.8 %copy-start.4 = (bf16[512,576]{0,1:T(8,128)(2,1)S(1)}, bf16[512,576]{0,1:T(8,128)(2,1)}, u32[]{:S(2)}) copy-start(bf16[512,576]{0,1:T(8,128)(2,1)} %param.13) | copy-start | bytes 1769476
  0.0 6.8 %copy-start.5 = (bf16[4,8,576]{2,1,0:T(8,128)(2,1)S(1)}, bf16[4,8,576]{2,1,0:T(8,128)(2,1)}, u32[]{:S(2)}) copy-start(bf16[4,8,576]{2,1,0:T(8,128)(2,1)} %param.12) | copy-start | bytes 110596
  0.0 8.9 %copy-start.8 = (s32[4]{0:T(128)S(1)}, s32[4]{0:T(128)}, u32[]{:S(2)}) copy-start(s32[4]{0:T(128)} %param.14) | copy-start | bytes 52
  0.0 8.9 %copy-start.9 = (s32[4]{0:T(128)S(1)}, s32[4]{0:T(128)}, u32[]{:S(2)}) copy-start(s32[4]{0:T(128)} %param.15) | copy-start | bytes 52
  0.0 8.9 %copy-start.10 = (s32[4]{0:T(128)S(1)}, s32[4]{0:T(128)}, u32[]{:S(2)}) copy-start(s32[4]{0:T(128)} %param.16) | copy-start | bytes 52
  0.0 6.8 %collective-permute-start = (bf16[32,576]{1,0:T(8,128)(2,1)}, bf16[32,576]{1,0:T(8,128)(2,1)S(1)}, u32[]{:S(2)}, u32[]{:S(2)}) collective-permute-start(bf16[32,576]{1,0:T(8,128)(2,1)} %bitcast.18), channel_id=1, source_target_pairs={{0,8},{1,9},{2,10},{3,11},{4,12},{5,13},{6,14},{7,15},{8,0},{9,1},... | collective-permute-start | bytes 110600 | tf_op jit(solution)/shard_map/ppermute | solution.py:46
  6.8 7.8 %collective-permute-start.8 = (bf16[576,512]{1,0:T(8,128)(2,1)S(1)}, bf16[576,512]{1,0:T(8,128)(2,1)S(1)}, u32[]{:S(2)}, u32[]{:S(2)}) collective-permute-start(bf16[576,512]{1,0:T(8,128)(2,1)S(1)} %bitcast.15), channel_id=1, source_target_pairs={{0,1},{1,0},{2,3},{3,2},{4,5},{5,4},{6,7},{7,6},{8,9},{9,8},{10,11... | collective-permute-start | bytes 1769480 | tf_op jit(solution)/shard_map/ppermute | solution.py:31
  6.8 4.1 %collective-permute-start.4 = (bf16[32,576]{1,0:T(8,128)(2,1)S(1)}, bf16[32,576]{1,0:T(8,128)(2,1)S(1)}, u32[]{:S(2)}, u32[]{:S(2)}) collective-permute-start(bf16[32,576]{1,0:T(8,128)(2,1)S(1)} %bitcast.19), channel_id=1, source_target_pairs={{0,4},{1,5},{2,6},{3,7},{4,0},{5,1},{6,2},{7,3},{8,12},{9,13},{10,... | collective-permute-start | bytes 110600 | tf_op jit(solution)/shard_map/ppermute | solution.py:46
  8.3 4.6 %collective-permute-start.6 = (bf16[32,576]{1,0:T(8,128)(2,1)S(1)}, bf16[32,576]{1,0:T(8,128)(2,1)S(1)}, u32[]{:S(2)}, u32[]{:S(2)}) collective-permute-start(bf16[32,576]{1,0:T(8,128)(2,1)S(1)} %collective-permute-done.refs_3_), channel_id=1, source_target_pairs={{0,4},{1,5},{2,6},{3,7},{4,0},{5,1},{6,2},{7,3},{8,12},{9,13},{10,... | collective-permute-start | bytes 110600 | tf_op jit(solution)/shard_map/ppermute | solution.py:46
  9.0 3.6 %collective-permute-start.1 = (s32[8,128]{1,0:T(8,128)S(1)}, s32[8,128]{1,0:T(8,128)S(1)}, u32[]{:S(2)}, u32[]{:S(2)}) collective-permute-start(s32[8,128]{1,0:T(8,128)S(1)} %shard_map.119.refs_0_), channel_id=1, source_target_pairs={{0,1},{1,0},{2,3},{3,2},{4,5},{5,4},{6,7},{7,6},{8,9},{9,8},{10,11... | collective-permute-start | bytes 12296 | tf_op jit(solution)/shard_map/ppermute | solution.py:31
  9.1 6.4 %collective-permute-start.2 = (bf16[32,576]{1,0:T(8,128)(2,1)S(1)}, bf16[32,576]{1,0:T(8,128)(2,1)S(1)}, u32[]{:S(2)}, u32[]{:S(2)}) collective-permute-start(bf16[32,576]{1,0:T(8,128)(2,1)S(1)} %bitcast.20), channel_id=1, source_target_pairs={{0,2},{1,3},{2,0},{3,1},{4,6},{5,7},{6,4},{7,5},{8,10},{9,11},{10,... | collective-permute-start | bytes 110600 | tf_op jit(solution)/shard_map/ppermute | solution.py:46
  10.9 5.7 %collective-permute-start.3 = (bf16[32,576]{1,0:T(8,128)(2,1)S(1)}, bf16[32,576]{1,0:T(8,128)(2,1)S(1)}, u32[]{:S(2)}, u32[]{:S(2)}) collective-permute-start(bf16[32,576]{1,0:T(8,128)(2,1)S(1)} %collective-permute-done.refs_3_), channel_id=1, source_target_pairs={{0,2},{1,3},{2,0},{3,1},{4,6},{5,7},{6,4},{7,5},{8,10},{9,11},{10,... | collective-permute-start | bytes 110600 | tf_op jit(solution)/shard_map/ppermute | solution.py:46
  12.6 4.0 %collective-permute-start.5 = (bf16[32,576]{1,0:T(8,128)(2,1)S(1)}, bf16[32,576]{1,0:T(8,128)(2,1)S(1)}, u32[]{:S(2)}, u32[]{:S(2)}) collective-permute-start(bf16[32,576]{1,0:T(8,128)(2,1)S(1)} %collective-permute-done.4.refs_4_), channel_id=1, source_target_pairs={{0,2},{1,3},{2,0},{3,1},{4,6},{5,7},{6,4},{7,5},{8,10},{9,11},{10,... | collective-permute-start | bytes 110600 | tf_op jit(solution)/shard_map/ppermute | solution.py:46
  12.9 4.1 %collective-permute-start.7 = (bf16[32,576]{1,0:T(8,128)(2,1)S(1)}, bf16[32,576]{1,0:T(8,128)(2,1)S(1)}, u32[]{:S(2)}, u32[]{:S(2)}) collective-permute-start(bf16[32,576]{1,0:T(8,128)(2,1)S(1)} %collective-permute-done.6.refs_5_), channel_id=1, source_target_pairs={{0,2},{1,3},{2,0},{3,1},{4,6},{5,7},{6,4},{7,5},{8,10},{9,11},{10,... | collective-permute-start | bytes 110600 | tf_op jit(solution)/shard_map/ppermute | solution.py:46
  17.0 16.0 %copy-start = (bf16[1024,7168]{1,0:T(8,128)(2,1)S(1)}, bf16[1024,7168]{1,0:T(8,128)(2,1)}, u32[]{:S(2)}) copy-start(bf16[1024,7168]{1,0:T(8,128)(2,1)} %out_proj.3) | copy-start | bytes 44040196
  17.0 16.0 %copy-start.3 = (bf16[8,512,128]{2,1,0:T(8,128)(2,1)S(1)}, bf16[8,512,128]{2,1,0:T(8,128)(2,1)}, u32[]{:S(2)}) copy-start(bf16[8,512,128]{2,1,0:T(8,128)(2,1)} %absorb.1) | copy-start | bytes 3145732
  17.0 16.0 %copy-start.7 = (bf16[4,448]{1,0:T(4,128)(2,1)S(1)}, bf16[4,448]{1,0:T(4,128)(2,1)}, u32[]{:S(2)}) copy-start(bf16[4,448]{1,0:T(4,128)(2,1)} %hidden.3) | copy-start | bytes 10756
  34.8 1.2 %collective-permute-start.9 = (f32[4,3584]{1,0:T(4,128)S(1)}, f32[4,3584]{1,0:T(4,128)S(1)}, u32[]{:S(2)}, u32[]{:S(2)}) collective-permute-start(f32[4,3584]{1,0:T(4,128)S(1)} %get-tuple-element.18), channel_id=1, source_target_pairs={{0,1},{1,0},{2,3},{3,2},{4,5},{5,4},{6,7},{7,6},{8,9},{9,8},{10,11... | collective-permute-start | bytes 172040 | tf_op jit(solution)/shard_map/ppermute | solution.py:31
  34.8 13.8 %copy-start.1 = (bf16[7168,576]{0,1:T(8,128)(2,1)S(1)}, bf16[7168,576]{0,1:T(8,128)(2,1)}, u32[]{:S(2)}) copy-start(bf16[7168,576]{0,1:T(8,128)(2,1)} %param.21) | copy-start | bytes 24772612
  34.8 13.8 %copy-start.2 = (bf16[7168,576]{0,1:T(8,128)(2,1)S(1)}, bf16[7168,576]{0,1:T(8,128)(2,1)}, u32[]{:S(2)}) copy-start(bf16[7168,576]{0,1:T(8,128)(2,1)} %param.22) | copy-start | bytes 24772612
  34.9 13.8 %copy-start.6 = (f32[7168]{0:T(1024)S(1)}, f32[7168]{0:T(1024)}, u32[]{:S(2)}) copy-start(f32[7168]{0:T(1024)} %param.18) | copy-start | bytes 86020
  34.9 16.1 %slice-start = ((s8[8257536]{0:T(1024)(128)(4,1)}), s8[4194304]{0:T(1024)(128)(4,1)S(1)}, s32[]{:S(2)}) async-start(s8[8257536]{0:T(1024)(128)(4,1)} %bitcast.13), calls=%async_computation.3 | async-start | bytes 8388608
  36.2 14.8 %slice-start.1 = ((s8[8257536]{0:T(1024)(128)(4,1)}), s8[4063232]{0:T(1024)(128)(4,1)S(1)}, s32[]{:S(2)}) async-start(s8[8257536]{0:T(1024)(128)(4,1)} %bitcast.13), calls=%async_computation.4 | async-start | bytes 8126464
  48.6 2.4 %collective-permute-start.10 = (f32[4,3584]{1,0:T(4,128)S(1)}, f32[4,3584]{1,0:T(4,128)S(1)}, u32[]{:S(2)}, u32[]{:S(2)}) collective-permute-start(f32[4,3584]{1,0:T(4,128)S(1)} %convert_reduce_fusion.mine), channel_id=1, source_target_pairs={{0,1},{1,0},{2,3},{3,2},{4,5},{5,4},{6,7},{7,6},{8,9},{9,8},{10,11... | collective-permute-start | bytes 172040 | tf_op jit(solution)/shard_map/ppermute | solution.py:31
